TPU v7x, 512 devices: a whole 4x8x8 slice. The times are simulated.
512 devices in a mesh: lat: 32 (over z, x_hi, core), lon: 16 (over y, x_lo).
Axes of the slice: x: 4 (x_hi: 2, x_lo: 2; x = x_hi * 2 + x_lo), y: 8, z: 8, core: 2. Of those that a mesh axis runs over, the one named last changes fastest.
Arguments:
- latent: float32 [256, 448, 640], P('lat', 'lon'), may hold values from -6 to 6
- conv_first: float32 [25, 640], replicated, may hold values from -1.2 to 1.2
- conv_second: float32 [25, 640], replicated, may hold values from -1.2 to 1.2
- filter_gains: float32 [192, 640], P(None, 'lon'), may hold values from -4 to 4
- norm_gain: float32 [640], replicated, may hold values from 0.5 to 1.5
- up_weight: bfloat16 [640, 1280], replicated, may hold values from -0.25 to 0.25
- down_weight: bfloat16 [1280, 640], replicated, may hold values from -0.15625 to 0.15625
Outputs:
- block_out: float32 [256, 448, 640], P('lat', 'lon')
All inputs are finite; a program needn't handle non-finite values.
Results may differ from a plain program's by a relative error of at most 0.0012.
Values sent between devices are 32-bit elements; how exact they have to be, the bound alone decides.
No kernel may reach another device: no remote copies, remote signals or barrier semaphores. Data moves between devices by JAX's collectives and lax.ppermute only.
A program may use at most 64 MiB of HBM per device.

v0:
```python
import math

import jax
import jax.numpy as jnp
import numpy as np
from jax import lax
from jax.experimental import pallas as pl
from jax.experimental.pallas import tpu as pltpu
from jax.sharding import PartitionSpec as P

ROWS, COLS, CHANNELS, HIDDEN = 8, 28, 640, 1280
LAT, LON, SLICE = 32, 16, 40
NLAT, NLON, MODES = 256, 448, 192
OWN = MODES // LAT
KEPT = OWN + 1
LON_CHUNK = 72
LAT_CHUNK = 35
f32, bf16 = jnp.float32, jnp.bfloat16


def split_np(table):
    high = table.astype(np.float32).astype(jnp.bfloat16)
    low = (table - high.astype(np.float64)).astype(np.float32).astype(jnp.bfloat16)
    return high, low


def order_of(owner, slot):
    return owner * OWN + slot if slot < OWN else MODES + owner


def fourier_np():
    half, sector, step = np.meshgrid(np.arange(2), np.arange(LON), np.arange(16), indexing="ij")
    place = (sector * COLS + half * 14 + step).reshape(-1)
    valid = (step < 14).reshape(-1)
    forward = np.zeros((2, KEPT, LAT, 512))
    inverse = np.zeros((2, 512, 8, LAT))
    for slot in range(KEPT):
        for owner in range(LAT):
            order = order_of(owner, slot)
            angle = 2.0 * np.pi * ((order * place) % NLON) / NLON
            double = 1.0 if order == 0 else 2.0
            real, imag = np.cos(angle), -np.sin(angle)
            if order == 0:
                imag = np.cos(np.pi * (place % 2))
            forward[0, slot, owner] = real / NLON * valid
            forward[1, slot, owner] = imag / NLON * valid
            inverse[0, :, slot, owner] = real * double * valid
            inverse[1, :, slot, owner] = imag * double * valid
    return forward.reshape(2 * KEPT * LAT, 512), inverse.reshape(2, 512, 8 * LAT)


def phase_np():
    table = np.zeros((LAT, 5, 2, 3, 4))
    for owner in range(LAT):
        for slot in range(KEPT):
            order = order_of(owner, slot)
            for b in range(-2, 3):
                angle = 2.0 * np.pi * ((order * b) % NLON) / NLON
                where = (owner, b + 2, slot // 4)
                table[where + (0, slot % 4)] = np.cos(angle)
                table[where + (1, slot % 4)] = np.cos(np.pi * b) if order == 0 else np.cos(angle)
                table[where + (2, slot % 4)] = np.sin(angle)
    return table.reshape(LAT, 5, 24).astype(np.float32)


def latitude_np():
    e, q = np.meshgrid(np.arange(ROWS), np.arange(LAT), indexing="ij")
    theta = np.pi * ((q * ROWS + e).reshape(-1) + 0.5) / NLAT
    weight = 2.0 * np.pi * np.pi * np.sin(theta) / NLAT
    rows = np.stack([np.cos(theta), np.log(np.sin(theta)), weight])
    return np.concatenate([rows, np.zeros((5, NLAT))]).astype(np.float32)


def seed_np():
    seeds = np.zeros((LAT, 8, 128), np.float32)
    for m in range(MODES):
        value = 0.5 * (
            math.log((2 * m + 1) / (4 * math.pi))
            + math.lgamma(2 * m + 1)
            - 2 * m * math.log(2)
            - 2 * math.lgamma(m + 1)
        )
        seeds[m // OWN, m % OWN] = value
    return seeds


def lane_slot(width):
    return lax.broadcasted_iota(jnp.int32, (1, 128), 1) // width


def swap_blocks(values, width):
    values = list(values)
    step = len(values) // 2
    while step:
        shift = step * width
        first = lane_slot(shift) % 2 == 0
        for a in range(len(values)):
            if not a & step:
                low, high = values[a], values[a | step]
                values[a] = jnp.where(first, low, pltpu.roll(high, shift, 1))
                values[a | step] = jnp.where(first, pltpu.roll(low, 128 - shift, 1), high)
        step //= 2
    return values


def split(value):
    high = value.astype(bf16)
    return high, (value - high.astype(f32)).astype(bf16)


def dot(a, b, dims=((1,), (0,))):
    return lax.dot_general(a, b, (dims, ((), ())), preferred_element_type=f32)


def dot3(a, b, dims=((1,), (0,))):
    return dot(a[0], b[0], dims) + (dot(a[1], b[0], dims) + dot(a[0], b[1], dims))


def pack_kernel(x_ref, out_ref):
    first = lane_slot(8) % 2 == 0
    for j in range(5):
        blocks = swap_blocks([x_ref[i, :, 128 * j : 128 * j + 128] for i in range(ROWS)], 16)
        for b in range(8):
            pair, place = divmod(8 * j + b, 5)
            even, odd = 2 * pair * LON_CHUNK, (2 * pair + 1) * LON_CHUNK
            block = blocks[b]
            if place == 2:
                top, bottom = block[:14], block[14:]
                out_ref[even + 56 : even + 70] = jnp.where(first, top, pltpu.roll(bottom, 8, 1))
                out_ref[odd + 56 : odd + 70] = jnp.where(first, pltpu.roll(top, 120, 1), bottom)
                out_ref[even + 70 : even + 72] = jnp.zeros((2, 128), f32)
                out_ref[odd + 70 : odd + 72] = jnp.zeros((2, 128), f32)
            else:
                base = (even, even + 28, None, odd, odd + 28)[place]
                out_ref[base : base + 28] = block


def forward_kernel(in_ref, high_ref, low_ref, out_ref):
    totals = []
    for half in range(2):
        pieces = []
        for start in (14 * half, 28 + 14 * half, 56):
            pieces.append(
                jnp.concatenate(
                    [in_ref[LON_CHUNK * q + start : LON_CHUNK * q + start + 16] for q in range(LON)],
                    axis=0,
                )
            )
        x = split(jnp.concatenate(pieces, axis=1))
        lanes = slice(256 * half, 256 * half + 256)
        totals.append(dot3((high_ref[:, lanes], low_ref[:, lanes]), x))
    both = totals[0][:, :256] + totals[1][:, :256]
    g0, g1 = totals[0][:, 256:], totals[1][:, 256:]
    half_rows = KEPT * LAT
    first = lane_slot(8) % 2 == 0
    last = jnp.where(
        first,
        g0[:half_rows] + pltpu.roll(g1[:half_rows], 120, 1),
        pltpu.roll(g0[half_rows:], 8, 1) + g1[half_rows:],
    )
    for row in range(2 * KEPT):
        part = both[LAT * row : LAT * row + LAT]
        out_ref[pl.ds(row, LAT, stride=LAT_CHUNK), :] = part[:, :128]
        out_ref[pl.ds(14 + row, LAT, stride=LAT_CHUNK), :] = part[:, 128:]
    for row in range(KEPT):
        out_ref[pl.ds(28 + row, LAT, stride=LAT_CHUNK), :] = last[LAT * row : LAT * row + LAT]


def legendre_kernel(owner_ref, angle_ref, seed_ref, high_ref, low_ref, left_ref, right_ref):
    slot = lax.broadcasted_iota(jnp.int32, (8, 256), 0)
    order_at = jnp.where(slot < OWN, owner_ref[0] * OWN + slot, 2 * MODES)
    order = order_at.astype(f32)
    degree = lax.broadcasted_iota(jnp.int32, (8, 256), 1).astype(f32)
    square, below = degree * degree, (degree - 1.0) * (degree - 1.0)
    upper = jnp.sqrt(
        jnp.maximum(4.0 * square - 1.0, 1.0) / jnp.maximum(square - order * order, 1.0)
    )
    lower = jnp.sqrt(
        jnp.maximum(below - order * order, 0.0) / jnp.maximum(4.0 * below - 1.0, 1.0)
    )
    product = upper * lower
    cosine = jnp.broadcast_to(angle_ref[0:1, :], (8, 256))
    diagonal = jnp.exp(seed_ref[:, 0:1] + order * angle_ref[1:2, :])
    previous = jnp.zeros((8, 256), f32)
    earlier = previous
    for l in range(MODES):
        current = jnp.where(
            order_at == l,
            diagonal,
            (upper[:, l : l + 1] * cosine) * previous - product[:, l : l + 1] * earlier,
        )
        left_ref[8 * l : 8 * l + 8] = current[:, :128]
        right_ref[8 * l : 8 * l + 8] = current[:, 128:]
        previous, earlier = current, previous
    for k in range(OWN):
        for part, source in enumerate((left_ref, right_ref)):
            high, low = split(source[pl.ds(k, MODES, stride=8), :])
            high_ref[k, :, 128 * part : 128 * part + 128] = high
            low_ref[k, :, 128 * part : 128 * part + 128] = low


def spectral_kernel(in_ref, high_ref, low_ref, taps_ref, gain_ref, angle_ref, out_ref, u_ref, v_ref, f_ref):
    lane = lax.broadcasted_iota(jnp.int32, (1, 128), 1) % LAT

    def fill_edges(ref):
        for part in range(2):
            for group in range(2):
                for e in (0, 1):
                    block = pltpu.roll(ref[part, group, 2 + e], 127, 1)
                    ref[part, group, 10 + e] = jnp.where(lane == LAT - 1, 0.0, block)
                    block = pltpu.roll(ref[part, group, 8 + e], 1, 1)
                    ref[part, group, e] = jnp.where(lane == 0, 0.0, block)

    def stencil(ref, which, store):
        for group in range(2):
            for tile in range(5):
                rows = slice(8 * tile, 8 * tile + 8)
                taps = []
                for a in range(5):
                    base = (which * 5 + a) * SLICE + 8 * tile
                    taps.append(
                        [
                            taps_ref[base : base + 8, (group * 3 + kind) * 128 : (group * 3 + kind) * 128 + 128]
                            for kind in range(3)
                        ]
                    )
                real = [ref[0, group, e, rows] for e in range(12)]
                imag = [ref[1, group, e, rows] for e in range(12)]
                for e in range(ROWS):
                    total_r, total_i = real[e + 2], imag[e + 2]
                    for a in range(5):
                        r_tap, s_tap, i_tap = taps[a]
                        total_r = total_r + (r_tap * real[e + a] - i_tap * imag[e + a])
                        total_i = total_i + (s_tap * imag[e + a] + i_tap * real[e + a])
                    store(group, rows, e, total_r, total_i)

    def rows_of(start, count):
        pieces = [in_ref[pl.ds(start + n, LAT, stride=LAT_CHUNK), :] for n in range(count)]
        if count < 4:
            pieces.append(jnp.zeros((LAT * (4 - count), 128), f32))
        return jnp.concatenate(pieces, axis=0).T

    for group in range(2):
        count = min(4, KEPT - 4 * group)
        for tile in range(2):
            for part in range(2):
                block = rows_of(14 * tile + KEPT * part + 4 * group, count)
                for e in range(ROWS):
                    u_ref[part, group, 2 + e, 16 * tile : 16 * tile + 16] = block[16 * e : 16 * e + 16]
        block = rows_of(28 + 4 * group, count)
        for e in range(ROWS):
            for part in range(2):
                start = 16 * e + 8 * part
                u_ref[part, group, 2 + e, 32:40] = block[start : start + 8]
    fill_edges(u_ref)

    def keep_first(group, rows, e, total_r, total_i):
        v_ref[0, group, 2 + e, rows] = total_r
        v_ref[1, group, 2 + e, rows] = total_i

    stencil(u_ref, 0, keep_first)

    weight = angle_ref[2:3, :]
    for part in range(2):
        for group in range(2):
            halves = [
                swap_blocks([v_ref[part, group, 2 + 4 * j + e] for e in range(4)], 32) for j in range(2)
            ]
            for n in range(4):
                if 4 * group + n < OWN:
                    f_ref[4 * group + n, SLICE * part : SLICE * part + SLICE] = (
                        jnp.concatenate([halves[0][n], halves[1][n]], axis=1) * weight
                    )
    for k in range(OWN):
        table = (high_ref[k], low_ref[k])
        spectrum = dot3(split(f_ref[k]), table, ((1,), (1,)))
        gain = gain_ref[80:160] if k == 0 else gain_ref[0:80]
        f_ref[k] = dot3(split(spectrum * gain), table)
    for part in range(2):
        for group in range(2):
            rows = slice(SLICE * part, SLICE * part + SLICE)
            for j in range(2):
                values = [
                    f_ref[4 * group + n, rows, 128 * j : 128 * j + 128]
                    if 4 * group + n < OWN
                    else jnp.zeros((SLICE, 128), f32)
                    for n in range(4)
                ]
                for e, value in enumerate(swap_blocks(values, 32)):
                    v_ref[part, group, 2 + 4 * j + e] = v_ref[part, group, 2 + 4 * j + e] + value
    fill_edges(v_ref)

    def keep_second(group, rows, e, total_r, total_i):
        u_ref[0, group, 2 + e, rows] = total_r
        u_ref[1, group, 2 + e, rows] = total_i

    stencil(v_ref, 1, keep_second)

    def give(start, count, pieces):
        block = jnp.concatenate(pieces, axis=0).T
        for n in range(count):
            out_ref[pl.ds(start + n, LAT, stride=LAT_CHUNK), :] = block[LAT * n : LAT * n + LAT]

    for group in range(2):
        count = min(4, KEPT - 4 * group)
        for tile in range(2):
            for part in range(2):
                give(
                    14 * tile + KEPT * part + 4 * group,
                    count,
                    [u_ref[part, group, 2 + e, 16 * tile : 16 * tile + 16] for e in range(ROWS)],
                )
        give(
            28 + 4 * group,
            count,
            [u_ref[part, group, 2 + e, 32:40] for e in range(ROWS) for part in range(2)],
        )


def inverse_kernel(in_ref, high_ref, low_ref, out_ref):
    totals = []
    for part in range(2):
        columns = []
        for start in (KEPT * part, 14 + KEPT * part, 28):
            pieces = [in_ref[pl.ds(start + k, LAT, stride=LAT_CHUNK), :] for k in range(KEPT)]
            columns.append(jnp.concatenate(pieces + [jnp.zeros((LAT, 128), f32)], axis=0))
        x = split(jnp.concatenate(columns, axis=1))
        totals.append(dot3((high_ref[part], low_ref[part]), x))
    both = totals[0][:, :256] + totals[1][:, :256]
    g0, g1 = totals[0][:, 256:], totals[1][:, 256:]
    first = lane_slot(8) % 2 == 0
    last = jnp.where(
        first,
        g0[:256] + pltpu.roll(g1[:256], 120, 1),
        pltpu.roll(g0[256:], 8, 1) + g1[256:],
    )
    for q in range(LON):
        base = LON_CHUNK * q
        for tile in range(2):
            for half in range(2):
                row = 256 * half + 16 * q
                start = base + 28 * tile + 14 * half
                out_ref[start : start + 14] = both[row : row + 14, 128 * tile : 128 * tile + 128]
        out_ref[base + 56 : base + 72] = last[16 * q : 16 * q + 16]


def mlp_kernel(in_ref, gain_ref, up_ref, down_ref, out_ref, x_ref):
    first = lane_slot(8) % 2 == 0
    for j in range(5):
        blocks = []
        for b in range(8):
            pair, place = divmod(8 * j + b, 5)
            even, odd = 2 * pair * LON_CHUNK, (2 * pair + 1) * LON_CHUNK
            if place == 2:
                e, o = in_ref[even + 56 : even + 70], in_ref[odd + 56 : odd + 70]
                top = jnp.where(first, e, pltpu.roll(o, 8, 1))
                bottom = jnp.where(first, pltpu.roll(e, 120, 1), o)
                blocks.append(jnp.concatenate([top, bottom], axis=0))
            else:
                base = (even, even + 28, None, odd, odd + 28)[place]
                blocks.append(in_ref[base : base + 28])
        for i, value in enumerate(swap_blocks(blocks, 16)):
            x_ref[i, 0:28, 128 * j : 128 * j + 128] = value
    x_ref[:, 28:32, :] = jnp.zeros((ROWS, 4, CHANNELS), f32)
    x = x_ref[...].reshape(ROWS * 32, CHANNELS)
    average = jnp.mean(x, axis=-1, keepdims=True)
    centred = x - average
    spread = jnp.mean(centred * centred, axis=-1, keepdims=True)
    normed = (centred * lax.rsqrt(spread + 1e-05) * gain_ref[...]).astype(bf16)
    total = x
    for n in range(5):
        cut = slice(256 * n, 256 * n + 256)
        hidden = dot(normed, up_ref[:, cut])
        active = jax.nn.gelu(hidden, approximate=True).astype(bf16)
        total = total + dot(active, down_ref[cut, :])
    for i in range(ROWS):
        out_ref[i] = total[32 * i : 32 * i + 28]


def vmem(count):
    return [pl.BlockSpec(memory_space=pltpu.VMEM)] * count


def run(kernel, shape, *operands, scratch=(), cost=(0, 0)):
    return pl.pallas_call(
        kernel,
        out_shape=jax.ShapeDtypeStruct(shape, f32),
        in_specs=vmem(len(operands)),
        out_specs=pl.BlockSpec(memory_space=pltpu.VMEM),
        scratch_shapes=list(scratch),
        cost_estimate=pl.CostEstimate(flops=cost[0], bytes_accessed=cost[1], transcendentals=0),
    )(*operands)


def legendre(owner, angles, seeds):
    table = jax.ShapeDtypeStruct((OWN, MODES, NLAT), bf16)
    return pl.pallas_call(
        legendre_kernel,
        out_shape=(table, table),
        in_specs=[pl.BlockSpec(memory_space=pltpu.SMEM)] + vmem(2),
        out_specs=vmem(2),
        scratch_shapes=[pltpu.VMEM((8 * MODES, 128), f32)] * 2,
        cost_estimate=pl.CostEstimate(flops=10**7, bytes_accessed=10**7, transcendentals=0),
    )(owner, angles, seeds)


def own_channels(array, axis, start, odd):
    part = lax.dynamic_slice_in_dim(array, start, SLICE, axis)
    return jnp.where(odd, jnp.roll(part, -8, axis), part)


def exchange(array, axis, count):
    rows = array.shape[0] // count
    shape = (count, rows, 128) if rows % 8 == 0 else (count, 1, rows * 128)
    moved = lax.all_to_all(array.reshape(shape), axis, split_axis=0, concat_axis=0, tiled=True)
    return moved.reshape(array.shape)


def per_device(latent, conv_first, conv_second, filter_gains, norm_gain, up_weight, down_weight):
    band = lax.axis_index("lat")
    sector = lax.axis_index("lon")
    odd = sector % 2 == 1
    forward, inverse = fourier_np()
    forward, inverse = split_np(forward), split_np(inverse)
    angles = jnp.asarray(latitude_np())

    packed = run(pack_kernel, (LON * LON_CHUNK, 128), latent)
    circles = exchange(packed, "lon", LON)

    seeds = lax.dynamic_index_in_dim(jnp.asarray(seed_np()), band, 0, False)
    high, low = legendre(band.astype(jnp.int32).reshape(1), angles, seeds)
    phases = lax.dynamic_index_in_dim(jnp.asarray(phase_np()), band, 0, False)
    spread_np = np.kron(np.eye(24, dtype=np.float32), np.ones((1, LAT), np.float32))
    taps = jnp.stack([conv_first, conv_second]).reshape(2, 5, 5, CHANNELS)
    taps = own_channels(taps, 3, sector * SLICE, odd).transpose(0, 1, 3, 2).reshape(10 * SLICE, 5)
    taps = jnp.dot(taps, phases, precision=lax.Precision.HIGHEST)
    taps = jnp.dot(taps, jnp.asarray(spread_np), precision=lax.Precision.HIGHEST)
    gains = own_channels(filter_gains, 1, 0, odd).T
    gains = jnp.concatenate([gains, gains, gains, jnp.where(band == 0, 0.0, gains)], axis=0)

    coeffs = run(forward_kernel, (LAT * LAT_CHUNK, 128), circles, *map(jnp.asarray, forward))
    orders = exchange(coeffs, "lat", LAT)
    state = pltpu.VMEM((2, 2, 12, SLICE, 128), f32)
    third = run(
        spectral_kernel,
        (LAT * LAT_CHUNK, 128),
        orders,
        high,
        low,
        taps,
        gains,
        angles,
        scratch=[state, state, pltpu.VMEM((OWN, 2 * SLICE, NLAT), f32)],
    )
    returned = exchange(third, "lat", LAT)
    restored = run(inverse_kernel, (LON * LON_CHUNK, 128), returned, *map(jnp.asarray, inverse))
    arrived = exchange(restored, "lon", LON)
    return run(
        mlp_kernel,
        (ROWS, COLS, CHANNELS),
        arrived,
        norm_gain.reshape(1, CHANNELS),
        up_weight,
        down_weight,
        scratch=[pltpu.VMEM((ROWS, 32, CHANNELS), f32)],
    )


def solution(mesh):
    return jax.shard_map(
        per_device,
        mesh=mesh,
        in_specs=(P("lat", "lon", None), P(), P(), P(None, "lon"), P(), P(), P()),
        out_specs=P("lat", "lon", None),
        check_vma=False,
    )
```

profile of v0, /device:TPU:4, one launch (start us, length us, event | category | flops | bytes accessed | tf_op | source)
XLA Modules:
  0.0 132.4 jit_solution(1950119418455030273)
XLA Ops:
  0.0 2.1 %copy.21.x_ref = f32[8,28,640]{2,1,0:T(8,128)} copy(f32[8,28,640]{2,0,1:T(8,128)} %param.15) | data formatting | bytes 1146880 | tf_op args[0]
  2.1 3.1 %shard_map.145 = f32[1152,128]{1,0:T(8,128)} custom-call(f32[8,28,640]{2,1,0:T(8,128)} %copy.21.x_ref), custom_call_target="tpu_custom_call" | custom-call | tf_op jit(solution)/shard_map/pallas_call | solution.py:385
  5.2 7.8 %all-to-all-start = ((f32[16,72,128]{2,1,0:T(8,128)}), f32[16,72,128]{2,1,0:T(8,128)S(1)}, u32[]{:S(2)}, u32[]{:S(2)}) async-start(f32[16,72,128]{2,1,0:T(8,128)} %bitcast.26), calls=%async_computation | async-start | bytes 1179648 | tf_op jit(solution)/shard_map/all_to_all | solution.py:415
  13.1 18.9 %all-to-all-done = f32[16,72,128]{2,1,0:T(8,128)S(1)} async-done(((f32[16,72,128]{2,1,0:T(8,128)}), f32[16,72,128]{2,1,0:T(8,128)S(1)}, u32[]{:S(2)}, u32[]{:S(2)}) %all-to-all-start) | async-done | bytes 589856 | tf_op jit(solution)/shard_map/all_to_all | solution.py:415
  32.0 0.8 copy-done.1
  32.8 3.1 %shard_map.146 = f32[1120,128]{1,0:T(8,128)} custom-call(f32[1152,128]{1,0:T(8,128)} %bitcast.27, bf16[448,512]{1,0:T(8,128)(2,1)} %constant.59.clone.high_ref, bf16[448,512]{1,0:T(8,128)(2,1)} %constant.60.clone.low_ref), custom_call_target="tpu_custom_call" | custom-call | tf_op jit(solution)/shard_map/pallas_call | solution.py:385
  35.8 13.6 %all-to-all-start.1 = ((f32[32,1,4480]{2,1,0:T(1,128)}), f32[32,1,4480]{2,1,0:T(1,128)S(1)}, u32[]{:S(2)}, u32[]{:S(2)}) async-start(f32[32,1,4480]{2,1,0:T(1,128)} %bitcast.32), calls=%async_computation.1 | async-start | bytes 1146880 | tf_op jit(solution)/shard_map/all_to_all | solution.py:415
  49.6 0.1 fusion.1
  49.8 1.3 dynamic-slice_bitcast_fusion.seed_ref
  51.1 2.6 %shard_map.147 = (bf16[6,192,256]{2,1,0:T(8,128)(2,1)}, bf16[6,192,256]{2,1,0:T(8,128)(2,1)}) custom-call(s32[1]{0:T(128)} %bitcast.4.owner_ref, f32[8,256]{1,0:T(8,128)} %constant.55.clone.angle_ref, f32[8,128]{1,0:T(8,128)} %dynamic-slice_bitcast_fusion.seed_ref), custom_call_target="tpu_custom_call" | custom-call | flops 10000000 | bytes 10000000 | tf_op jit(solution)/shard_map/pallas_call | solution.py:397
  53.7 0.7 pad_maximum_fusion.gain_ref
  54.4 0.9 fusion.3
  55.3 2.2 %fusion.8.taps_ref = f32[400,768]{1,0:T(8,128)} fusion(f32[400,24]{0,1:T(8,128)S(1)} %fusion.3, f32[24,768]{1,0:T(8,128)S(1)} %copy-done.6), kind=kOutput, calls=%fused_computation.14 | convolution fusion | flops 88473600 | bytes 1340928 | tf_op jit(solution)/shard_map/dot_general | solution.py:437
  57.5 10.6 %all-to-all-done.1 = f32[32,1,4480]{2,1,0:T(1,128)S(1)} async-done(((f32[32,1,4480]{2,1,0:T(1,128)}), f32[32,1,4480]{2,1,0:T(1,128)S(1)}, u32[]{:S(2)}, u32[]{:S(2)}) %all-to-all-start.1) | async-done | bytes 573472 | tf_op jit(solution)/shard_map/all_to_all | solution.py:415
  68.1 0.8 copy-done.2
  69.0 5.6 %shard_map.148 = f32[1120,128]{1,0:T(8,128)} custom-call(f32[1120,128]{1,0:T(8,128)} %bitcast.29, bf16[6,192,256]{2,1,0:T(8,128)(2,1)} %get-tuple-element.7.high_ref, bf16[6,192,256]{2,1,0:T(8,128)(2,1)} %get-tuple-element.8.low_ref, f32[400,768]{1,0:T(8,128)} %fusion.8.taps_ref, f32[160,192]{1,0:T(8,128)} %pad_maximum_fusion.gain_ref, ...), custom_call_target="tpu_custom_call" | custom-call | tf_op jit(solution)/shard_map/pallas_call | solution.py:385
  74.5 23.8 %all_to_all.20 = f32[32,1,4480]{2,1,0:T(1,128)} all-to-all(f32[32,1,4480]{2,1,0:T(1,128)} %bitcast.30), channel_id=1, replica_groups=mesh['lat'=32,'lon'=16] {'lat'}, dimensions={0} | all-to-all | bytes 1146880 | tf_op jit(solution)/shard_map/all_to_all | solution.py:415
  98.4 3.2 %shard_map.149 = f32[1152,128]{1,0:T(8,128)} custom-call(f32[1120,128]{1,0:T(8,128)} %bitcast.31, bf16[2,512,256]{2,1,0:T(8,128)(2,1)} %constant.61.clone.high_ref, bf16[2,512,256]{2,1,0:T(8,128)(2,1)} %constant.62.clone.low_ref), custom_call_target="tpu_custom_call" | custom-call | tf_op jit(solution)/shard_map/pallas_call | solution.py:385
  101.6 3.6 %all-to-all-start.3 = ((f32[16,72,128]{2,1,0:T(8,128)}), f32[16,72,128]{2,1,0:T(8,128)S(1)}, u32[]{:S(2)}, u32[]{:S(2)}) async-start(f32[16,72,128]{2,1,0:T(8,128)} %bitcast.28), calls=%async_computation.3 | async-start | bytes 1179648 | tf_op jit(solution)/shard_map/all_to_all | solution.py:415
  105.2 0.6 reshape.48.gain_ref
  105.7 18.3 %all-to-all-done.3 = f32[16,72,128]{2,1,0:T(8,128)S(1)} async-done(((f32[16,72,128]{2,1,0:T(8,128)}), f32[16,72,128]{2,1,0:T(8,128)S(1)}, u32[]{:S(2)}, u32[]{:S(2)}) %all-to-all-start.3) | async-done | bytes 589856 | tf_op jit(solution)/shard_map/all_to_all | solution.py:415
  124.1 0.8 copy-done
  124.9 5.3 %shard_map.150 = f32[8,28,640]{2,1,0:T(8,128)} custom-call(f32[1152,128]{1,0:T(8,128)} %bitcast.25, f32[1,640]{1,0:T(1,128)} %reshape.48.gain_ref, bf16[640,1280]{1,0:T(8,128)(2,1)} %up_ref.1, bf16[1280,640]{1,0:T(8,128)(2,1)} %down_ref.1), custom_call_target="tpu_custom_call" | custom-call | tf_op jit(solution)/shard_map/pallas_call | solution.py:385
  130.2 2.2 %copy.25 = f32[8,28,640]{2,0,1:T(8,128)} copy(f32[8,28,640]{2,1,0:T(8,128)} %shard_map.150) | data formatting | bytes 1146880 | tf_op jit(solution)/shard_map/pallas_call | solution.py:385
  (24 shorter events, 0.3 us)
Async XLA Ops:
  0.0 13.0 %copy-start.4 = (f32[25,640]{1,0:T(8,128)S(1)}, f32[25,640]{1,0:T(8,128)}, u32[]{:S(2)}) copy-start(f32[25,640]{1,0:T(8,128)} %param.16) | copy-start | bytes 192004
  2.1 11.0 %copy-start.5 = (f32[25,640]{1,0:T(8,128)S(1)}, f32[25,640]{1,0:T(8,128)}, u32[]{:S(2)}) copy-start(f32[25,640]{1,0:T(8,128)} %param.17) | copy-start | bytes 192004
  5.2 26.8 %all-to-all-start = ((f32[16,72,128]{2,1,0:T(8,128)}), f32[16,72,128]{2,1,0:T(8,128)S(1)}, u32[]{:S(2)}, u32[]{:S(2)}) async-start(f32[16,72,128]{2,1,0:T(8,128)} %bitcast.26), calls=%async_computation | async-start | bytes 1179648 | tf_op jit(solution)/shard_map/all_to_all | solution.py:415
  32.0 0.8 copy-start.1
  32.8 20.9 %copy-start.3 = (f32[192,40]{0,1:T(8,128)S(1)}, f32[192,40]{0,1:T(8,128)}, u32[]{:S(2)}) copy-start(f32[192,40]{0,1:T(8,128)} %param.18) | copy-start | bytes 92164
  32.8 20.9 %slice-start = ((f32[192,40]{0,1:T(8,128)}), f32[192,8]{0,1:T(8,128)S(1)}, s32[]{:S(2)}) async-start(f32[192,40]{0,1:T(8,128)} %param.18), calls=%async_computation.4 | async-start | bytes 16384 | tf_op jit(solution)/shard_map/jit(_roll_static)/slice | solution.py:409
  32.8 20.9 %slice-start.1 = ((f32[192,40]{0,1:T(8,128)}), f32[192,32]{0,1:T(8,128)S(1)}, s32[]{:S(2)}) async-start(f32[192,40]{0,1:T(8,128)} %param.18), calls=%async_computation.5 | async-start | bytes 65536 | tf_op jit(solution)/shard_map/jit(_roll_static)/slice | solution.py:409
  35.8 19.5 %copy-start.6 = (f32[24,768]{1,0:T(8,128)S(1)}, f32[24,768]{1,0:T(8,128)}, u32[]{:S(2)}) copy-start(f32[24,768]{1,0:T(8,128)} %constant.58.clone) | copy-start | bytes 221188
  35.8 32.3 %all-to-all-start.1 = ((f32[32,1,4480]{2,1,0:T(1,128)}), f32[32,1,4480]{2,1,0:T(1,128)S(1)}, u32[]{:S(2)}, u32[]{:S(2)}) async-start(f32[32,1,4480]{2,1,0:T(1,128)} %bitcast.32), calls=%async_computation.1 | async-start | bytes 1146880 | tf_op jit(solution)/shard_map/all_to_all | solution.py:415
  68.1 0.8 copy-start.2
  98.4 6.8 %copy-start.7 = (f32[640]{0:T(1024)S(1)}, f32[640]{0:T(1024)}, u32[]{:S(2)}) copy-start(f32[640]{0:T(1024)} %param.19) | copy-start | bytes 7684
  101.6 22.5 %all-to-all-start.3 = ((f32[16,72,128]{2,1,0:T(8,128)}), f32[16,72,128]{2,1,0:T(8,128)S(1)}, u32[]{:S(2)}, u32[]{:S(2)}) async-start(f32[16,72,128]{2,1,0:T(8,128)} %bitcast.28), calls=%async_computation.3 | async-start | bytes 1179648 | tf_op jit(solution)/shard_map/all_to_all | solution.py:415
  124.1 0.8 copy-start
where the time goes:
time: 133 us; the launch traced here: 132 us
  waiting for transfers between devices  47.8 us (36%)
  starting transfers between devices  25 us (19%)
  blocking collectives  23.8 us (18%)
  Pallas kernels  22.9 us (17%)
  local copies, waits for them, and re-layouts  8.84 us (7%)
  matrix products  3.15 us (2%)
    all_to_all x3, waiting for transfers between devices, exchange(): lax.all_to_all(array.reshape(shape), axis, split_axis=0, concat_axis=0, t...  47.8 us
    all_to_all x3, starting transfers between devices, exchange(): lax.all_to_all(array.reshape(shape), axis, split_axis=0, concat_axis=0, t...  25 us
    all_to_all x1, blocking collectives, exchange(): lax.all_to_all(array.reshape(shape), axis, split_axis=0, concat_axis=0, t...  23.8 us
    pallas_call x5, Pallas kernels, run(): pl.pallas_call(kernel, out_shape=jax.ShapeDtypeStruct(shape, f32), in_spe...  20.2 us
    unnamed x17, local copies, waits for them, and re-layouts  4.55 us
  transfers between devices with their start and end apart: 3, of which 3 were waited for; matrix products, arithmetic and copies ran while one was open for 5% of the time, Pallas kernels for 2%

commit v1 on v0

--- a/solution.py
+++ b/solution.py
@@ -119,7 +119,7 @@
 def pack_kernel(x_ref, out_ref):
     first = lane_slot(8) % 2 == 0
     for j in range(5):
-        blocks = swap_blocks([x_ref[i, :, 128 * j : 128 * j + 128] for i in range(ROWS)], 16)
+        blocks = swap_blocks([x_ref[:, i, 128 * j : 128 * j + 128] for i in range(ROWS)], 16)
         for b in range(8):
             pair, place = divmod(8 * j + b, 5)
             even, odd = 2 * pair * LON_CHUNK, (2 * pair + 1) * LON_CHUNK
@@ -344,7 +344,9 @@
         out_ref[base + 56 : base + 72] = last[16 * q : 16 * q + 16]
 
 
-def mlp_kernel(in_ref, gain_ref, up_ref, down_ref, out_ref, x_ref):
+def mlp_kernel(in_ref, gain_ref, up_ref, down_hbm, out_ref, x_ref, down_ref, arrival):
+    fetch = pltpu.make_async_copy(down_hbm, down_ref, arrival)
+    fetch.start()
     first = lane_slot(8) % 2 == 0
     for j in range(5):
         blocks = []
@@ -360,34 +362,34 @@
                 base = (even, even + 28, None, odd, odd + 28)[place]
                 blocks.append(in_ref[base : base + 28])
         for i, value in enumerate(swap_blocks(blocks, 16)):
-            x_ref[i, 0:28, 128 * j : 128 * j + 128] = value
-    x_ref[:, 28:32, :] = jnp.zeros((ROWS, 4, CHANNELS), f32)
-    x = x_ref[...].reshape(ROWS * 32, CHANNELS)
+            x_ref[:, i, 128 * j : 128 * j + 128] = value
+    x = x_ref[...].reshape(COLS * ROWS, CHANNELS)
     average = jnp.mean(x, axis=-1, keepdims=True)
     centred = x - average
     spread = jnp.mean(centred * centred, axis=-1, keepdims=True)
     normed = (centred * lax.rsqrt(spread + 1e-05) * gain_ref[...]).astype(bf16)
     total = x
+    fetch.wait()
     for n in range(5):
         cut = slice(256 * n, 256 * n + 256)
         hidden = dot(normed, up_ref[:, cut])
         active = jax.nn.gelu(hidden, approximate=True).astype(bf16)
         total = total + dot(active, down_ref[cut, :])
-    for i in range(ROWS):
-        out_ref[i] = total[32 * i : 32 * i + 28]
+    out_ref[...] = total.reshape(COLS, ROWS, CHANNELS)
 
 
 def vmem(count):
     return [pl.BlockSpec(memory_space=pltpu.VMEM)] * count
 
 
-def run(kernel, shape, *operands, scratch=(), cost=(0, 0)):
+def run(kernel, shape, *operands, scratch=(), cost=(0, 0), grant=24, far=0):
     return pl.pallas_call(
         kernel,
         out_shape=jax.ShapeDtypeStruct(shape, f32),
-        in_specs=vmem(len(operands)),
+        in_specs=vmem(len(operands) - far) + [pl.BlockSpec(memory_space=pl.ANY)] * far,
         out_specs=pl.BlockSpec(memory_space=pltpu.VMEM),
         scratch_shapes=list(scratch),
+        compiler_params=pltpu.CompilerParams(vmem_limit_bytes=grant << 20),
         cost_estimate=pl.CostEstimate(flops=cost[0], bytes_accessed=cost[1], transcendentals=0),
     )(*operands)
 
@@ -400,6 +402,7 @@
         in_specs=[pl.BlockSpec(memory_space=pltpu.SMEM)] + vmem(2),
         out_specs=vmem(2),
         scratch_shapes=[pltpu.VMEM((8 * MODES, 128), f32)] * 2,
+        compiler_params=pltpu.CompilerParams(vmem_limit_bytes=16 << 20),
         cost_estimate=pl.CostEstimate(flops=10**7, bytes_accessed=10**7, transcendentals=0),
     )(owner, angles, seeds)
 
@@ -424,7 +427,7 @@
     forward, inverse = split_np(forward), split_np(inverse)
     angles = jnp.asarray(latitude_np())
 
-    packed = run(pack_kernel, (LON * LON_CHUNK, 128), latent)
+    packed = run(pack_kernel, (LON * LON_CHUNK, 128), latent.transpose(1, 0, 2))
     circles = exchange(packed, "lon", LON)
 
     seeds = lax.dynamic_index_in_dim(jnp.asarray(seed_np()), band, 0, False)
@@ -455,15 +458,21 @@
     returned = exchange(third, "lat", LAT)
     restored = run(inverse_kernel, (LON * LON_CHUNK, 128), returned, *map(jnp.asarray, inverse))
     arrived = exchange(restored, "lon", LON)
-    return run(
+    result = run(
         mlp_kernel,
-        (ROWS, COLS, CHANNELS),
+        (COLS, ROWS, CHANNELS),
         arrived,
         norm_gain.reshape(1, CHANNELS),
         up_weight,
         down_weight,
-        scratch=[pltpu.VMEM((ROWS, 32, CHANNELS), f32)],
-    )
+        scratch=[
+            pltpu.VMEM((COLS, ROWS, CHANNELS), f32),
+            pltpu.VMEM((HIDDEN, CHANNELS), bf16),
+            pltpu.SemaphoreType.DMA,
+        ],
+        far=1,
+    )
+    return result.transpose(1, 0, 2)
 
 
 def solution(mesh):

time: 133 us -> 120 us (0.902)
  Pallas kernels: 22.9 us -> 13 us
  local copies, waits for them, and re-layouts: 8.84 us -> 3.42 us
  waiting for transfers between devices: 47.8 us -> 52.3 us
    pallas_call x5, Pallas kernels: 20.2 us -> 12.1 us  [run(): pl.pallas_call(kernel, out_shape=jax.ShapeDtypeStruct(shape, f32), in_spe...]
    all_to_all x3, waiting for transfers between devices: 47.8 us -> 52.3 us  [exchange(): lax.all_to_all(array.reshape(shape), axis, split_axis=0, concat_axis=0, t...]
    pallas_call x1 -> x0, local copies, waits for them, and re-layouts: 2.23 us -> none  [run(): pl.pallas_call(kernel, out_shape=jax.ShapeDtypeStruct(shape, f32), in_spe...]
    unnamed x17 -> x26, local copies, waits for them, and re-layouts: 4.55 us -> 2.53 us
    pallas_call x1, Pallas kernels: 2.61 us -> 0.89 us  [legendre(): pl.pallas_call(legendre_kernel, out_shape=(table, table), in_specs=[pl.Bl...]
  transfers between devices with their start and end apart: 3 -> 3, of which waited for: 3 -> 3; matrix products, arithmetic and copies ran while one was open for 5% -> 3% of each run, Pallas kernels for 2% -> 1%
where the time goes in v1:
time: 120 us
  waiting for transfers between devices  52.3 us (44%)
  starting transfers between devices  25 us (21%)
  blocking collectives  23.5 us (20%)
  Pallas kernels  13 us (11%)
  local copies, waits for them, and re-layouts  3.42 us (3%)
  matrix products  2.1 us (2%)
    all_to_all x3, waiting for transfers between devices, exchange(): lax.all_to_all(array.reshape(shape), axis, split_axis=0, concat_axis=0, t...  52.3 us
    all_to_all x3, starting transfers between devices, exchange(): lax.all_to_all(array.reshape(shape), axis, split_axis=0, concat_axis=0, t...  25 us
    all_to_all x1, blocking collectives, exchange(): lax.all_to_all(array.reshape(shape), axis, split_axis=0, concat_axis=0, t...  23.5 us
    pallas_call x5, Pallas kernels, run(): pl.pallas_call(kernel, out_shape=jax.ShapeDtypeStruct(shape, f32), in_spe...  12.1 us
    unnamed x26, local copies, waits for them, and re-layouts  2.53 us
  transfers between devices with their start and end apart: 3, of which 3 were waited for; matrix products, arithmetic and copies ran while one was open for 3% of the time, Pallas kernels for 1%

profile of v1, /device:TPU:4, one launch (start us, length us, event | category | flops | bytes accessed | tf_op | source)
XLA Modules:
  0.0 119.8 jit_solution(13276680751715764710)
XLA Ops:
  0.0 1.1 copy-done.2
  1.1 2.0 %shard_map.145 = f32[1152,128]{1,0:T(8,128)} custom-call(f32[28,8,640]{2,1,0:T(8,128)S(1)} %bitcast.32), custom_call_target="tpu_custom_call" | custom-call | tf_op jit(solution)/shard_map/pallas_call | solution.py:386
  3.1 7.8 %all-to-all-start = ((f32[16,72,128]{2,1,0:T(8,128)}), f32[16,72,128]{2,1,0:T(8,128)S(1)}, u32[]{:S(2)}, u32[]{:S(2)}) async-start(f32[16,72,128]{2,1,0:T(8,128)} %bitcast.1), calls=%async_computation | async-start | bytes 1179648 | tf_op jit(solution)/shard_map/all_to_all | solution.py:418
  11.0 18.9 %all-to-all-done = f32[16,72,128]{2,1,0:T(8,128)S(1)} async-done(((f32[16,72,128]{2,1,0:T(8,128)}), f32[16,72,128]{2,1,0:T(8,128)S(1)}, u32[]{:S(2)}, u32[]{:S(2)}) %all-to-all-start) | async-done | bytes 589856 | tf_op jit(solution)/shard_map/all_to_all | solution.py:418
  29.9 0.0 slice-start
  29.9 0.0 slice-start.1
  29.9 1.7 %shard_map.146 = f32[1120,128]{1,0:T(8,128)} custom-call(f32[1152,128]{1,0:T(8,128)S(1)} %bitcast.27, bf16[448,512]{1,0:T(8,128)(2,1)S(1)} %copy-done.5, bf16[448,512]{1,0:T(8,128)(2,1)S(1)} %copy-done.6), custom_call_target="tpu_custom_call" | custom-call | tf_op jit(solution)/shard_map/pallas_call | solution.py:386
  31.6 13.6 %all-to-all-start.1 = ((f32[32,1,4480]{2,1,0:T(1,128)}), f32[32,1,4480]{2,1,0:T(1,128)S(1)}, u32[]{:S(2)}, u32[]{:S(2)}) async-start(f32[32,1,4480]{2,1,0:T(1,128)} %bitcast.3), calls=%async_computation.1 | async-start | bytes 1146880 | tf_op jit(solution)/shard_map/all_to_all | solution.py:418
  45.2 0.1 fusion
  45.3 0.1 slice.20
  45.3 0.1 fusion.1
  45.5 0.1 reshape.43
  45.5 0.7 dynamic-slice_bitcast_fusion.seed_ref
  46.2 0.9 shard_map.147
  47.2 0.9 fusion.3
  48.1 1.2 fusion.8.taps_ref
  49.3 14.6 %all-to-all-done.1 = f32[32,1,4480]{2,1,0:T(1,128)S(1)} async-done(((f32[32,1,4480]{2,1,0:T(1,128)}), f32[32,1,4480]{2,1,0:T(1,128)S(1)}, u32[]{:S(2)}, u32[]{:S(2)}) %all-to-all-start.1) | async-done | bytes 573472 | tf_op jit(solution)/shard_map/all_to_all | solution.py:418
  63.9 2.9 %shard_map.148 = f32[1120,128]{1,0:T(8,128)S(1)} custom-call(f32[1120,128]{1,0:T(8,128)S(1)} %bitcast.29, bf16[6,192,256]{2,1,0:T(8,128)(2,1)S(1)} %get-tuple-element.7.high_ref, bf16[6,192,256]{2,1,0:T(8,128)(2,1)S(1)} %get-tuple-element.8.low_ref, f32[400,768]{1,0:T(8,128)S(1)} %fusion.8.taps_ref, f32[160,192]{1,0:T(8,128)S(1)} %pad_maximum_fusion.gain_ref, ...), custom_call_target="tpu_custom_call" | custom-call | tf_op jit(solution)/shard_map/pallas_call | solution.py:386
  66.8 23.5 %all_to_all.20 = f32[32,1,4480]{2,1,0:T(1,128)S(1)} all-to-all(f32[32,1,4480]{2,1,0:T(1,128)S(1)} %bitcast.30), channel_id=1, replica_groups=mesh['lat'=32,'lon'=16] {'lat'}, dimensions={0} | all-to-all | bytes 1146880 | tf_op jit(solution)/shard_map/all_to_all | solution.py:418
  90.4 1.8 %shard_map.149 = f32[1152,128]{1,0:T(8,128)} custom-call(f32[1120,128]{1,0:T(8,128)S(1)} %bitcast.31, bf16[2,512,256]{2,1,0:T(8,128)(2,1)S(1)} %copy-done.3, bf16[2,512,256]{2,1,0:T(8,128)(2,1)S(1)} %copy-done.4), custom_call_target="tpu_custom_call" | custom-call | tf_op jit(solution)/shard_map/pallas_call | solution.py:386
  92.2 3.6 %all-to-all-start.3 = ((f32[16,72,128]{2,1,0:T(8,128)}), f32[16,72,128]{2,1,0:T(8,128)S(1)}, u32[]{:S(2)}, u32[]{:S(2)}) async-start(f32[16,72,128]{2,1,0:T(8,128)} %bitcast.12), calls=%async_computation.3 | async-start | bytes 1179648 | tf_op jit(solution)/shard_map/all_to_all | solution.py:418
  95.8 18.9 %all-to-all-done.3 = f32[16,72,128]{2,1,0:T(8,128)S(1)} async-done(((f32[16,72,128]{2,1,0:T(8,128)}), f32[16,72,128]{2,1,0:T(8,128)S(1)}, u32[]{:S(2)}, u32[]{:S(2)}) %all-to-all-start.3) | async-done | bytes 589856 | tf_op jit(solution)/shard_map/all_to_all | solution.py:418
  114.7 1.4 %copy-done.1 = bf16[1280,640]{1,0:T(8,128)(2,1)S(1)} copy-done((bf16[1280,640]{1,0:T(8,128)(2,1)S(1)}, bf16[1280,640]{1,0:T(8,128)(2,1)}, u32[]{:S(2)}) %copy-start.1) | copy-done | bytes 1638424
  116.1 3.7 %shard_map.150 = f32[28,8,640]{2,1,0:T(8,128)} custom-call(f32[1152,128]{1,0:T(8,128)S(1)} %bitcast.28, f32[1,640]{1,0:T(1,128)S(1)} %reshape.48.gain_ref, bf16[640,1280]{1,0:T(8,128)(2,1)S(1)} %copy-done, bf16[1280,640]{1,0:T(8,128)(2,1)S(1)} %copy-done.1), custom_call_target="tpu_custom_call" | custom-call | tf_op jit(solution)/shard_map/pallas_call | solution.py:386
  (32 shorter events, 0.1 us)
Async XLA Ops:
  0.0 1.1 copy-start.2
  1.1 9.9 %copy-start.9 = (f32[25,640]{1,0:T(8,128)S(1)}, f32[25,640]{1,0:T(8,128)}, u32[]{:S(2)}) copy-start(f32[25,640]{1,0:T(8,128)} %param.16) | copy-start | bytes 192004
  1.1 9.9 %copy-start.10 = (f32[25,640]{1,0:T(8,128)S(1)}, f32[25,640]{1,0:T(8,128)}, u32[]{:S(2)}) copy-start(f32[25,640]{1,0:T(8,128)} %param.17) | copy-start | bytes 192004
  1.1 28.8 %copy-start.5 = (bf16[448,512]{1,0:T(8,128)(2,1)S(1)}, bf16[448,512]{1,0:T(8,128)(2,1)}, u32[]{:S(2)}) copy-start(bf16[448,512]{1,0:T(8,128)(2,1)} %constant.59.clone.high_ref) | copy-start | bytes 1376260
  1.1 28.8 %copy-start.6 = (bf16[448,512]{1,0:T(8,128)(2,1)S(1)}, bf16[448,512]{1,0:T(8,128)(2,1)}, u32[]{:S(2)}) copy-start(bf16[448,512]{1,0:T(8,128)(2,1)} %constant.60.clone.low_ref) | copy-start | bytes 1376260
  3.1 26.8 %all-to-all-start = ((f32[16,72,128]{2,1,0:T(8,128)}), f32[16,72,128]{2,1,0:T(8,128)S(1)}, u32[]{:S(2)}, u32[]{:S(2)}) async-start(f32[16,72,128]{2,1,0:T(8,128)} %bitcast.1), calls=%async_computation | async-start | bytes 1179648 | tf_op jit(solution)/shard_map/all_to_all | solution.py:418
  29.8 16.4 %copy-start.7 = (f32[8,256]{1,0:T(8,128)S(1)}, f32[8,256]{1,0:T(8,128)}, u32[]{:S(2)}) copy-start(f32[8,256]{1,0:T(8,128)} %constant.55.clone.angle_ref) | copy-start | bytes 24580
  29.8 17.3 %copy-start.8 = (f32[192,40]{0,1:T(8,128)S(1)}, f32[192,40]{0,1:T(8,128)}, u32[]{:S(2)}) copy-start(f32[192,40]{0,1:T(8,128)} %param.18) | copy-start | bytes 92164
  29.9 17.3 %slice-start = ((f32[192,40]{0,1:T(8,128)}), f32[192,8]{0,1:T(8,128)S(1)}, s32[]{:S(2)}) async-start(f32[192,40]{0,1:T(8,128)} %param.18), calls=%async_computation.4 | async-start | bytes 16384 | tf_op jit(solution)/shard_map/jit(_roll_static)/slice | solution.py:412
  29.9 17.3 %slice-start.1 = ((f32[192,40]{0,1:T(8,128)}), f32[192,32]{0,1:T(8,128)S(1)}, s32[]{:S(2)}) async-start(f32[192,40]{0,1:T(8,128)} %param.18), calls=%async_computation.5 | async-start | bytes 65536 | tf_op jit(solution)/shard_map/jit(_roll_static)/slice | solution.py:412
  31.6 16.5 %copy-start.11 = (f32[24,768]{1,0:T(8,128)S(1)}, f32[24,768]{1,0:T(8,128)}, u32[]{:S(2)}) copy-start(f32[24,768]{1,0:T(8,128)} %constant.58.clone) | copy-start | bytes 221188
  31.6 32.3 %all-to-all-start.1 = ((f32[32,1,4480]{2,1,0:T(1,128)}), f32[32,1,4480]{2,1,0:T(1,128)S(1)}, u32[]{:S(2)}, u32[]{:S(2)}) async-start(f32[32,1,4480]{2,1,0:T(1,128)} %bitcast.3), calls=%async_computation.1 | async-start | bytes 1146880 | tf_op jit(solution)/shard_map/all_to_all | solution.py:418
  63.9 26.5 %copy-start.3 = (bf16[2,512,256]{2,1,0:T(8,128)(2,1)S(1)}, bf16[2,512,256]{2,1,0:T(8,128)(2,1)}, u32[]{:S(2)}) copy-start(bf16[2,512,256]{2,1,0:T(8,128)(2,1)} %constant.61.clone.high_ref) | copy-start | bytes 1572868
  63.9 26.5 %copy-start.4 = (bf16[2,512,256]{2,1,0:T(8,128)(2,1)S(1)}, bf16[2,512,256]{2,1,0:T(8,128)(2,1)}, u32[]{:S(2)}) copy-start(bf16[2,512,256]{2,1,0:T(8,128)(2,1)} %constant.62.clone.low_ref) | copy-start | bytes 1572868
  90.4 5.4 %copy-start.12 = (f32[640]{0:T(1024)S(1)}, f32[640]{0:T(1024)}, u32[]{:S(2)}) copy-start(f32[640]{0:T(1024)} %param.19) | copy-start | bytes 7684
  90.4 24.3 %copy-start = (bf16[640,1280]{1,0:T(8,128)(2,1)S(1)}, bf16[640,1280]{1,0:T(8,128)(2,1)}, u32[]{:S(2)}) copy-start(bf16[640,1280]{1,0:T(8,128)(2,1)} %up_ref.1) | copy-start | bytes 4915204
  92.2 22.5 %all-to-all-start.3 = ((f32[16,72,128]{2,1,0:T(8,128)}), f32[16,72,128]{2,1,0:T(8,128)S(1)}, u32[]{:S(2)}, u32[]{:S(2)}) async-start(f32[16,72,128]{2,1,0:T(8,128)} %bitcast.12), calls=%async_computation.3 | async-start | bytes 1179648 | tf_op jit(solution)/shard_map/all_to_all | solution.py:418
  114.7 1.4 %copy-start.1 = (bf16[1280,640]{1,0:T(8,128)(2,1)S(1)}, bf16[1280,640]{1,0:T(8,128)(2,1)}, u32[]{:S(2)}) copy-start(bf16[1280,640]{1,0:T(8,128)(2,1)} %down_hbm.1) | copy-start | bytes 4915204

commit v2 on v1

--- a/solution.py
+++ b/solution.py
@@ -116,9 +116,15 @@
     return dot(a[0], b[0], dims) + (dot(a[1], b[0], dims) + dot(a[0], b[1], dims))
 
 
-def pack_kernel(x_ref, out_ref):
+def pack_kernel(x_hbm, out_ref, x_ref, arrivals):
     first = lane_slot(8) % 2 == 0
+    fetches = []
     for j in range(5):
+        lanes = pl.ds(128 * j, 128)
+        fetches.append(pltpu.make_async_copy(x_hbm.at[:, :, lanes], x_ref.at[:, :, lanes], arrivals.at[j]))
+        fetches[j].start()
+    for j in range(5):
+        fetches[j].wait()
         blocks = swap_blocks([x_ref[:, i, 128 * j : 128 * j + 128] for i in range(ROWS)], 16)
         for b in range(8):
             pair, place = divmod(8 * j + b, 5)
@@ -344,9 +350,7 @@
         out_ref[base + 56 : base + 72] = last[16 * q : 16 * q + 16]
 
 
-def mlp_kernel(in_ref, gain_ref, up_ref, down_hbm, out_ref, x_ref, down_ref, arrival):
-    fetch = pltpu.make_async_copy(down_hbm, down_ref, arrival)
-    fetch.start()
+def mlp_kernel(in_ref, gain_ref, up_ref, down_ref, out_hbm, x_ref, y_ref, sent):
     first = lane_slot(8) % 2 == 0
     for j in range(5):
         blocks = []
@@ -367,27 +371,33 @@
     average = jnp.mean(x, axis=-1, keepdims=True)
     centred = x - average
     spread = jnp.mean(centred * centred, axis=-1, keepdims=True)
-    normed = (centred * lax.rsqrt(spread + 1e-05) * gain_ref[...]).astype(bf16)
-    total = x
-    fetch.wait()
+    normed = (centred * lax.rsqrt(spread + 1e-05) * gain_ref[...].reshape(1, CHANNELS)).astype(bf16)
+    active = []
     for n in range(5):
-        cut = slice(256 * n, 256 * n + 256)
-        hidden = dot(normed, up_ref[:, cut])
-        active = jax.nn.gelu(hidden, approximate=True).astype(bf16)
-        total = total + dot(active, down_ref[cut, :])
-    out_ref[...] = total.reshape(COLS, ROWS, CHANNELS)
+        hidden = dot(normed, up_ref[:, 256 * n : 256 * n + 256])
+        active.append(jax.nn.gelu(hidden, approximate=True).astype(bf16))
+    active = jnp.concatenate(active, axis=1)
+    stores = []
+    for n, (start, width) in enumerate(((0, 256), (256, 256), (512, 128))):
+        lanes = pl.ds(start, width)
+        total = x[:, start : start + width] + dot(active, down_ref[:, start : start + width])
+        y_ref[:, :, start : start + width] = total.reshape(COLS, ROWS, width)
+        stores.append(pltpu.make_async_copy(y_ref.at[:, :, lanes], out_hbm.at[:, :, lanes], sent.at[n]))
+        stores[n].start()
+    for store in stores:
+        store.wait()
 
 
 def vmem(count):
     return [pl.BlockSpec(memory_space=pltpu.VMEM)] * count
 
 
-def run(kernel, shape, *operands, scratch=(), cost=(0, 0), grant=24, far=0):
+def run(kernel, shape, *operands, scratch=(), cost=(0, 0), grant=24, far=0, out=pltpu.VMEM):
     return pl.pallas_call(
         kernel,
         out_shape=jax.ShapeDtypeStruct(shape, f32),
-        in_specs=vmem(len(operands) - far) + [pl.BlockSpec(memory_space=pl.ANY)] * far,
-        out_specs=pl.BlockSpec(memory_space=pltpu.VMEM),
+        in_specs=vmem(len(operands) - far) + [pl.BlockSpec(memory_space=pltpu.HBM)] * far,
+        out_specs=pl.BlockSpec(memory_space=out),
         scratch_shapes=list(scratch),
         compiler_params=pltpu.CompilerParams(vmem_limit_bytes=grant << 20),
         cost_estimate=pl.CostEstimate(flops=cost[0], bytes_accessed=cost[1], transcendentals=0),
@@ -427,7 +437,14 @@
     forward, inverse = split_np(forward), split_np(inverse)
     angles = jnp.asarray(latitude_np())
 
-    packed = run(pack_kernel, (LON * LON_CHUNK, 128), latent.transpose(1, 0, 2))
+    packed = run(
+        pack_kernel,
+        (LON * LON_CHUNK, 128),
+        latent.transpose(1, 0, 2),
+        scratch=[pltpu.VMEM((COLS, ROWS, CHANNELS), f32), pltpu.SemaphoreType.DMA((5,))],
+        far=1,
+        grant=60,
+    )
     circles = exchange(packed, "lon", LON)
 
     seeds = lax.dynamic_index_in_dim(jnp.asarray(seed_np()), band, 0, False)
@@ -462,15 +479,15 @@
         mlp_kernel,
         (COLS, ROWS, CHANNELS),
         arrived,
-        norm_gain.reshape(1, CHANNELS),
+        norm_gain,
         up_weight,
         down_weight,
         scratch=[
             pltpu.VMEM((COLS, ROWS, CHANNELS), f32),
-            pltpu.VMEM((HIDDEN, CHANNELS), bf16),
-            pltpu.SemaphoreType.DMA,
+            pltpu.VMEM((COLS, ROWS, CHANNELS), f32),
+            pltpu.SemaphoreType.DMA((3,)),
         ],
-        far=1,
+        out=pltpu.HBM,
     )
     return result.transpose(1, 0, 2)
 

time: 120 us -> 117 us (0.975)
  blocking collectives: 23.5 us -> 45.4 us
  waiting for transfers between devices: 52.3 us -> 33.4 us
  starting transfers between devices: 25 us -> 21.4 us
  local copies, waits for them, and re-layouts: 3.42 us -> 0.94 us
    all_to_all x1 -> x2, blocking collectives: 23.5 us -> 45.4 us  [exchange(): lax.all_to_all(array.reshape(shape), axis, split_axis=0, concat_axis=0, t...]
    all_to_all x3 -> x2, waiting for transfers between devices: 52.3 us -> 33.4 us  [exchange(): lax.all_to_all(array.reshape(shape), axis, split_axis=0, concat_axis=0, t...]
    all_to_all x3 -> x2, starting transfers between devices: 25 us -> 21.4 us  [exchange(): lax.all_to_all(array.reshape(shape), axis, split_axis=0, concat_axis=0, t...]
    unnamed x26 -> x24, local copies, waits for them, and re-layouts: 2.53 us -> 0.05 us
  transfers between devices with their start and end apart: 3 -> 2, of which waited for: 3 -> 2; matrix products, arithmetic and copies ran while one was open for 3% -> 3% of each run, Pallas kernels for 1% -> 1%
where the time goes in v2:
time: 117 us; the launch traced here: 116 us
  blocking collectives  45.4 us (39%)
  waiting for transfers between devices  33.4 us (29%)
  starting transfers between devices  21.4 us (18%)
  Pallas kernels  12.8 us (11%)
  matrix products  2.12 us (2%)
    all_to_all x2, blocking collectives, exchange(): lax.all_to_all(array.reshape(shape), axis, split_axis=0, concat_axis=0, t...  45.4 us
    all_to_all x2, waiting for transfers between devices, exchange(): lax.all_to_all(array.reshape(shape), axis, split_axis=0, concat_axis=0, t...  33.4 us
    all_to_all x2, starting transfers between devices, exchange(): lax.all_to_all(array.reshape(shape), axis, split_axis=0, concat_axis=0, t...  21.4 us
    pallas_call x5, Pallas kernels, run(): pl.pallas_call(kernel, out_shape=jax.ShapeDtypeStruct(shape, f32), in_spe...  11.9 us
  transfers between devices with their start and end apart: 2, of which 2 were waited for; matrix products, arithmetic and copies ran while one was open for 3% of the time, Pallas kernels for 1%

profile of v2, /device:TPU:4, one launch (start us, length us, event | category | flops | bytes accessed | tf_op | source)
XLA Modules:
  0.0 116.5 jit_solution(4414269211004533205)
XLA Ops:
  0.0 0.0 copy-start.10
  0.0 3.4 %shard_map.145 = f32[1152,128]{1,0:T(8,128)} custom-call(f32[28,8,640]{2,1,0:T(8,128)} %bitcast.34), custom_call_target="tpu_custom_call" | custom-call | tf_op jit(solution)/shard_map/pallas_call | solution.py:396
  3.4 7.9 %all-to-all-start = ((f32[16,72,128]{2,1,0:T(8,128)}), f32[16,72,128]{2,1,0:T(8,128)S(1)}, u32[]{:S(2)}, u32[]{:S(2)}) async-start(f32[16,72,128]{2,1,0:T(8,128)} %bitcast.33), calls=%async_computation | async-start | bytes 1179648 | tf_op jit(solution)/shard_map/all_to_all | solution.py:428
  11.3 18.9 %all-to-all-done = f32[16,72,128]{2,1,0:T(8,128)S(1)} async-done(((f32[16,72,128]{2,1,0:T(8,128)}), f32[16,72,128]{2,1,0:T(8,128)S(1)}, u32[]{:S(2)}, u32[]{:S(2)}) %all-to-all-start) | async-done | bytes 589856 | tf_op jit(solution)/shard_map/all_to_all | solution.py:428
  30.2 0.0 slice-start
  30.2 0.0 slice-start.1
  30.2 1.7 %shard_map.146 = f32[1120,128]{1,0:T(8,128)} custom-call(f32[1152,128]{1,0:T(8,128)S(1)} %bitcast.28, bf16[448,512]{1,0:T(8,128)(2,1)S(1)} %copy-done.5, bf16[448,512]{1,0:T(8,128)(2,1)S(1)} %copy-done.4), custom_call_target="tpu_custom_call" | custom-call | tf_op jit(solution)/shard_map/pallas_call | solution.py:396
  32.0 13.6 %all-to-all-start.1 = ((f32[32,1,4480]{2,1,0:T(1,128)}), f32[32,1,4480]{2,1,0:T(1,128)S(1)}, u32[]{:S(2)}, u32[]{:S(2)}) async-start(f32[32,1,4480]{2,1,0:T(1,128)} %bitcast.3), calls=%async_computation.1 | async-start | bytes 1146880 | tf_op jit(solution)/shard_map/all_to_all | solution.py:428
  45.5 0.1 fusion
  45.6 0.1 slice.20
  45.7 0.1 fusion.1
  45.8 0.1 reshape.40
  45.9 0.7 dynamic-slice_bitcast_fusion.seed_ref
  46.6 0.9 shard_map.147
  47.6 0.9 fusion.3
  48.5 1.2 %fusion.8.taps_ref = f32[400,768]{1,0:T(8,128)S(1)} fusion(f32[400,24]{0,1:T(8,128)S(1)} %fusion.3, f32[24,768]{1,0:T(8,128)S(1)} %copy-done.11), kind=kOutput, calls=%fused_computation.14 | convolution fusion | flops 88473600 | bytes 1340928 | tf_op jit(solution)/shard_map/dot_general | solution.py:457
  49.7 14.6 %all-to-all-done.1 = f32[32,1,4480]{2,1,0:T(1,128)S(1)} async-done(((f32[32,1,4480]{2,1,0:T(1,128)}), f32[32,1,4480]{2,1,0:T(1,128)S(1)}, u32[]{:S(2)}, u32[]{:S(2)}) %all-to-all-start.1) | async-done | bytes 573472 | tf_op jit(solution)/shard_map/all_to_all | solution.py:428
  64.3 3.1 %shard_map.148 = f32[1120,128]{1,0:T(8,128)S(1)} custom-call(f32[1120,128]{1,0:T(8,128)S(1)} %bitcast.30, bf16[6,192,256]{2,1,0:T(8,128)(2,1)S(1)} %get-tuple-element.7.high_ref, bf16[6,192,256]{2,1,0:T(8,128)(2,1)S(1)} %get-tuple-element.8.low_ref, f32[400,768]{1,0:T(8,128)S(1)} %fusion.8.taps_ref, f32[160,192]{1,0:T(8,128)S(1)} %pad_maximum_fusion.gain_ref, ...), custom_call_target="tpu_custom_call" | custom-call | tf_op jit(solution)/shard_map/pallas_call | solution.py:396
  67.4 23.5 %all_to_all.20 = f32[32,1,4480]{2,1,0:T(1,128)S(1)} all-to-all(f32[32,1,4480]{2,1,0:T(1,128)S(1)} %bitcast.31), channel_id=1, replica_groups=mesh['lat'=32,'lon'=16] {'lat'}, dimensions={0} | all-to-all | bytes 1146880 | tf_op jit(solution)/shard_map/all_to_all | solution.py:428
  90.9 0.0 copy-done.2
  90.9 0.0 copy-start.7
  90.9 1.0 shard_map.149
  91.9 21.9 %all_to_all.21 = f32[16,72,128]{2,1,0:T(8,128)S(1)} all-to-all(f32[16,72,128]{2,1,0:T(8,128)S(1)} %bitcast.29), channel_id=1, replica_groups=mesh['lat'=32,'lon'=16] {'lon'}, dimensions={0} | all-to-all | bytes 1179648 | tf_op jit(solution)/shard_map/all_to_all | solution.py:428
  113.8 2.7 %shard_map.150 = f32[28,8,640]{2,1,0:T(8,128)} custom-call(f32[1152,128]{1,0:T(8,128)S(1)} %bitcast.27, f32[640]{0:T(1024)S(1)} %copy-done.7, bf16[640,1280]{1,0:T(8,128)(2,1)S(1)} %copy-done, bf16[1280,640]{1,0:T(8,128)(2,1)S(1)} %copy-done.1), custom_call_target="tpu_custom_call" | custom-call | tf_op jit(solution)/shard_map/pallas_call | solution.py:396
  (28 shorter events, 0.1 us)
Async XLA Ops:
  0.0 30.2 %copy-start.4 = (bf16[448,512]{1,0:T(8,128)(2,1)S(1)}, bf16[448,512]{1,0:T(8,128)(2,1)}, u32[]{:S(2)}) copy-start(bf16[448,512]{1,0:T(8,128)(2,1)} %constant.60.clone.low_ref) | copy-start | bytes 1376260
  0.0 30.2 %copy-start.5 = (bf16[448,512]{1,0:T(8,128)(2,1)S(1)}, bf16[448,512]{1,0:T(8,128)(2,1)}, u32[]{:S(2)}) copy-start(bf16[448,512]{1,0:T(8,128)(2,1)} %constant.59.clone.high_ref) | copy-start | bytes 1376260
  0.0 11.3 %copy-start.9 = (f32[25,640]{1,0:T(8,128)S(1)}, f32[25,640]{1,0:T(8,128)}, u32[]{:S(2)}) copy-start(f32[25,640]{1,0:T(8,128)} %param.16) | copy-start | bytes 192004
  0.0 11.3 %copy-start.10 = (f32[25,640]{1,0:T(8,128)S(1)}, f32[25,640]{1,0:T(8,128)}, u32[]{:S(2)}) copy-start(f32[25,640]{1,0:T(8,128)} %param.17) | copy-start | bytes 192004
  3.4 26.8 %all-to-all-start = ((f32[16,72,128]{2,1,0:T(8,128)}), f32[16,72,128]{2,1,0:T(8,128)S(1)}, u32[]{:S(2)}, u32[]{:S(2)}) async-start(f32[16,72,128]{2,1,0:T(8,128)} %bitcast.33), calls=%async_computation | async-start | bytes 1179648 | tf_op jit(solution)/shard_map/all_to_all | solution.py:428
  30.2 16.4 %copy-start.6 = (f32[8,256]{1,0:T(8,128)S(1)}, f32[8,256]{1,0:T(8,128)}, u32[]{:S(2)}) copy-start(f32[8,256]{1,0:T(8,128)} %constant.55.clone.angle_ref) | copy-start | bytes 24580
  30.2 17.3 %copy-start.8 = (f32[192,40]{0,1:T(8,128)S(1)}, f32[192,40]{0,1:T(8,128)}, u32[]{:S(2)}) copy-start(f32[192,40]{0,1:T(8,128)} %param.18) | copy-start | bytes 92164
  30.2 17.3 %slice-start = ((f32[192,40]{0,1:T(8,128)}), f32[192,8]{0,1:T(8,128)S(1)}, s32[]{:S(2)}) async-start(f32[192,40]{0,1:T(8,128)} %param.18), calls=%async_computation.4 | async-start | bytes 16384 | tf_op jit(solution)/shard_map/jit(_roll_static)/slice | solution.py:422
  30.2 17.3 %slice-start.1 = ((f32[192,40]{0,1:T(8,128)}), f32[192,32]{0,1:T(8,128)S(1)}, s32[]{:S(2)}) async-start(f32[192,40]{0,1:T(8,128)} %param.18), calls=%async_computation.5 | async-start | bytes 65536 | tf_op jit(solution)/shard_map/jit(_roll_static)/slice | solution.py:422
  31.9 16.5 %copy-start.11 = (f32[24,768]{1,0:T(8,128)S(1)}, f32[24,768]{1,0:T(8,128)}, u32[]{:S(2)}) copy-start(f32[24,768]{1,0:T(8,128)} %constant.58.clone) | copy-start | bytes 221188
  32.0 32.3 %all-to-all-start.1 = ((f32[32,1,4480]{2,1,0:T(1,128)}), f32[32,1,4480]{2,1,0:T(1,128)S(1)}, u32[]{:S(2)}, u32[]{:S(2)}) async-start(f32[32,1,4480]{2,1,0:T(1,128)} %bitcast.3), calls=%async_computation.1 | async-start | bytes 1146880 | tf_op jit(solution)/shard_map/all_to_all | solution.py:428
  64.3 26.6 %copy-start.2 = (bf16[2,512,256]{2,1,0:T(8,128)(2,1)S(1)}, bf16[2,512,256]{2,1,0:T(8,128)(2,1)}, u32[]{:S(2)}) copy-start(bf16[2,512,256]{2,1,0:T(8,128)(2,1)} %constant.62.clone.low_ref) | copy-start | bytes 1572868
  64.3 26.6 %copy-start.3 = (bf16[2,512,256]{2,1,0:T(8,128)(2,1)S(1)}, bf16[2,512,256]{2,1,0:T(8,128)(2,1)}, u32[]{:S(2)}) copy-start(bf16[2,512,256]{2,1,0:T(8,128)(2,1)} %constant.61.clone.high_ref) | copy-start | bytes 1572868
  90.9 22.9 %copy-start = (bf16[640,1280]{1,0:T(8,128)(2,1)S(1)}, bf16[640,1280]{1,0:T(8,128)(2,1)}, u32[]{:S(2)}) copy-start(bf16[640,1280]{1,0:T(8,128)(2,1)} %up_ref.1) | copy-start | bytes 4915204
  90.9 22.9 %copy-start.1 = (bf16[1280,640]{1,0:T(8,128)(2,1)S(1)}, bf16[1280,640]{1,0:T(8,128)(2,1)}, u32[]{:S(2)}) copy-start(bf16[1280,640]{1,0:T(8,128)(2,1)} %down_ref.1) | copy-start | bytes 4915204
  90.9 22.9 %copy-start.7 = (f32[640]{0:T(1024)S(1)}, f32[640]{0:T(1024)}, u32[]{:S(2)}) copy-start(f32[640]{0:T(1024)} %gain_ref.1) | copy-start | bytes 7684

commit v3 on v2

--- a/solution.py
+++ b/solution.py
@@ -14,7 +14,7 @@
 OWN = MODES // LAT
 KEPT = OWN + 1
 LON_CHUNK = 72
-LAT_CHUNK = 35
+LAT_CHUNK = 30
 f32, bf16 = jnp.float32, jnp.bfloat16
 
 
@@ -50,7 +50,7 @@
 
 
 def phase_np():
-    table = np.zeros((LAT, 5, 2, 3, 4))
+    table = np.zeros((LAT, 8, 2, 3, 4))
     for owner in range(LAT):
         for slot in range(KEPT):
             order = order_of(owner, slot)
@@ -60,7 +60,7 @@
                 table[where + (0, slot % 4)] = np.cos(angle)
                 table[where + (1, slot % 4)] = np.cos(np.pi * b) if order == 0 else np.cos(angle)
                 table[where + (2, slot % 4)] = np.sin(angle)
-    return table.reshape(LAT, 5, 24).astype(np.float32)
+    return table.reshape(LAT, 8, 24).astype(np.float32)
 
 
 def latitude_np():
@@ -116,13 +116,14 @@
     return dot(a[0], b[0], dims) + (dot(a[1], b[0], dims) + dot(a[0], b[1], dims))
 
 
-def pack_kernel(x_hbm, out_ref, x_ref, arrivals):
+def pack_kernel(x_hbm, out_hbm, x_ref, out_ref, arrivals, sent):
     first = lane_slot(8) % 2 == 0
     fetches = []
     for j in range(5):
         lanes = pl.ds(128 * j, 128)
         fetches.append(pltpu.make_async_copy(x_hbm.at[:, :, lanes], x_ref.at[:, :, lanes], arrivals.at[j]))
         fetches[j].start()
+    stores = []
     for j in range(5):
         fetches[j].wait()
         blocks = swap_blocks([x_ref[:, i, 128 * j : 128 * j + 128] for i in range(ROWS)], 16)
@@ -139,9 +140,15 @@
             else:
                 base = (even, even + 28, None, odd, odd + 28)[place]
                 out_ref[base : base + 28] = block
-
-
-def forward_kernel(in_ref, high_ref, low_ref, out_ref):
+            if place == 4:
+                rows = pl.ds(even, 2 * LON_CHUNK)
+                stores.append(pltpu.make_async_copy(out_ref.at[rows], out_hbm.at[rows], sent.at[pair]))
+                stores[pair].start()
+    for store in stores:
+        store.wait()
+
+
+def forward_kernel(in_ref, high_ref, low_ref, out_ref, local_ref, up_ref, down_ref):
     totals = []
     for half in range(2):
         pieces = []
@@ -164,12 +171,111 @@
         g0[:half_rows] + pltpu.roll(g1[:half_rows], 120, 1),
         pltpu.roll(g0[half_rows:], 8, 1) + g1[half_rows:],
     )
-    for row in range(2 * KEPT):
-        part = both[LAT * row : LAT * row + LAT]
-        out_ref[pl.ds(row, LAT, stride=LAT_CHUNK), :] = part[:, :128]
-        out_ref[pl.ds(14 + row, LAT, stride=LAT_CHUNK), :] = part[:, 128:]
-    for row in range(KEPT):
-        out_ref[pl.ds(28 + row, LAT, stride=LAT_CHUNK), :] = last[LAT * row : LAT * row + LAT]
+    for r in range(2):
+        for k in range(OWN):
+            part = both[LAT * (KEPT * r + k) : LAT * (KEPT * r + k) + LAT]
+            row = OWN * r + k
+            out_ref[pl.ds(row, LAT, stride=LAT_CHUNK), :] = part[:, :128]
+            out_ref[pl.ds(2 * OWN + row, LAT, stride=LAT_CHUNK), :] = part[:, 128:]
+    for k in range(OWN):
+        out_ref[pl.ds(4 * OWN + k, LAT, stride=LAT_CHUNK), :] = last[LAT * k : LAT * k + LAT]
+    left = lane_slot(64) == 0
+    for r in range(2):
+        part = both[LAT * (KEPT * r + OWN) : LAT * (KEPT * r + OWN) + LAT]
+        a, b = part[:, :128], part[:, 128:]
+        rows = slice(LAT * r, LAT * r + LAT)
+        local_ref[rows, :128] = a
+        local_ref[rows, 128:256] = b
+        up_ref[rows] = jnp.where(left, pltpu.roll(a, 64, 1), b)
+        down_ref[rows] = jnp.where(left, a, pltpu.roll(b, 64, 1))
+    part = last[LAT * OWN : LAT * OWN + LAT]
+    local_ref[0:LAT, 256:] = part
+    local_ref[LAT:, 256:] = jnp.zeros((LAT, 128), f32)
+    up_ref[2 * LAT :] = part
+    down_ref[2 * LAT :] = part
+
+
+def local_kernel(band_ref, own_ref, below_ref, above_ref, taps_ref, wave_ref, out_ref):
+    lane = lax.broadcasted_iota(jnp.int32, (1, 128), 1)
+    left = lane < 64
+    south = jnp.where(band_ref[0] == 0, 0.0, 1.0)
+    north = jnp.where(band_ref[0] == LAT - 1, 0.0, 1.0)
+    masks = (jnp.where(left, south, 1.0), jnp.where(left, 1.0, north))
+
+    def extend(own, below, above):
+        turned = pltpu.roll(own, 64, 1)
+        return jnp.where(left, below, turned), jnp.where(left, turned, above)
+
+    def turn(value):
+        return pltpu.roll(value, 64, 1)
+
+    def shifted(tiles, a):
+        if a == 0:
+            return tiles
+        amount = (-16 * a) % 128
+        first, second = (pltpu.roll(tile, amount, 1) for tile in tiles)
+        if a > 0:
+            keep = lane < 128 - 16 * a
+            return jnp.where(keep, first, second), jnp.where(keep, second, first)
+        keep = lane >= -16 * a
+        return jnp.where(keep, first, second), jnp.where(keep, second, first)
+
+    def weights(which, a, tile):
+        rows = [taps_ref[(which * 5 + a) * 5 + b : (which * 5 + a) * 5 + b + 1, 128 * tile : 128 * tile + 128] for b in range(5)]
+        cos1, cos2, sin1, sin2 = (wave_ref[:, 128 * n : 128 * n + 128] for n in range(4))
+        real = rows[2] + (rows[3] + rows[1]) * cos1 + (rows[4] + rows[0]) * cos2
+        imag = (rows[3] - rows[1]) * sin1 + (rows[4] - rows[0]) * sin2
+        return real, imag
+
+    for tile in range(2):
+        parts = []
+        for r in range(2):
+            rows = slice(LAT * r, LAT * r + LAT)
+            own = own_ref[rows, 128 * tile : 128 * tile + 128]
+            below, above = below_ref[rows], above_ref[rows]
+            if tile == 0:
+                parts.append(extend(own, below, turn(above)))
+            else:
+                parts.append(extend(own, turn(below), above))
+        for which in range(2):
+            real, imag = [list(value) for value in parts]
+            for a in range(-2, 3):
+                w_r, w_i = weights(which, a + 2, tile)
+                e_r, e_i = shifted(parts[0], a), shifted(parts[1], a)
+                for n in range(2):
+                    real[n] = real[n] + (w_r * e_r[n] - w_i * e_i[n])
+                    imag[n] = imag[n] + (w_r * e_i[n] + w_i * e_r[n])
+            parts = [tuple(v * m for v, m in zip(value, masks)) for value in (real, imag)]
+        for r in range(2):
+            result = jnp.where(left, turn(parts[r][0]), turn(parts[r][1]))
+            out_ref[LAT * r : LAT * r + LAT, 128 * tile : 128 * tile + 128] = result
+    second = lane_slot(8) % 2 == 1
+    value = extend(own_ref[0:LAT, 256:], turn(below_ref[2 * LAT :]), turn(above_ref[2 * LAT :]))
+    for which in range(2):
+        total = list(value)
+        swapped = [jnp.where(second, pltpu.roll(v, 8, 1), pltpu.roll(v, 120, 1)) for v in value]
+        for a in range(-2, 3):
+            w_r, w_i = weights(which, a + 2, 2)
+            w_i = jnp.where(second, w_i, -w_i)
+            e, f = shifted(value, a), shifted(swapped, a)
+            for n in range(2):
+                total[n] = total[n] + (w_r * e[n] + w_i * f[n])
+        value = tuple(v * m for v, m in zip(total, masks))
+    out_ref[0:LAT, 256:] = jnp.where(left, turn(value[0]), turn(value[1]))
+    out_ref[LAT:, 256:] = jnp.zeros((LAT, 128), f32)
+
+
+def taps_kernel(rows_ref, phase_ref, plain_ref, lanes_ref, taps_ref, spread_ref):
+    spread_ref[...] = jnp.dot(plain_ref[...], lanes_ref[...], precision=lax.Precision.HIGHEST)
+    for tile in range(6):
+        phase = phase_ref[:, 4 * tile : 4 * tile + 1]
+        for n in range(1, 4):
+            column = phase_ref[:, 4 * tile + n : 4 * tile + n + 1]
+            phase = jnp.where(lane_slot(LAT) >= n, column, phase)
+        total = rows_ref[:, 0:1] * phase[0:1]
+        for b in range(1, 5):
+            total = total + rows_ref[:, b : b + 1] * phase[b : b + 1]
+        taps_ref[:, 128 * tile : 128 * tile + 128] = total
 
 
 def legendre_kernel(owner_ref, angle_ref, seed_ref, high_ref, low_ref, left_ref, right_ref):
@@ -203,7 +309,6 @@
             high, low = split(source[pl.ds(k, MODES, stride=8), :])
             high_ref[k, :, 128 * part : 128 * part + 128] = high
             low_ref[k, :, 128 * part : 128 * part + 128] = low
-
 
 def spectral_kernel(in_ref, high_ref, low_ref, taps_ref, gain_ref, angle_ref, out_ref, u_ref, v_ref, f_ref):
     lane = lax.broadcasted_iota(jnp.int32, (1, 128), 1) % LAT
@@ -247,13 +352,13 @@
         return jnp.concatenate(pieces, axis=0).T
 
     for group in range(2):
-        count = min(4, KEPT - 4 * group)
+        count = min(4, OWN - 4 * group)
         for tile in range(2):
             for part in range(2):
-                block = rows_of(14 * tile + KEPT * part + 4 * group, count)
+                block = rows_of(OWN * (2 * tile + part) + 4 * group, count)
                 for e in range(ROWS):
                     u_ref[part, group, 2 + e, 16 * tile : 16 * tile + 16] = block[16 * e : 16 * e + 16]
-        block = rows_of(28 + 4 * group, count)
+        block = rows_of(4 * OWN + 4 * group, count)
         for e in range(ROWS):
             for part in range(2):
                 start = 16 * e + 8 * part
@@ -308,27 +413,29 @@
             out_ref[pl.ds(start + n, LAT, stride=LAT_CHUNK), :] = block[LAT * n : LAT * n + LAT]
 
     for group in range(2):
-        count = min(4, KEPT - 4 * group)
+        count = min(4, OWN - 4 * group)
         for tile in range(2):
             for part in range(2):
                 give(
-                    14 * tile + KEPT * part + 4 * group,
+                    OWN * (2 * tile + part) + 4 * group,
                     count,
                     [u_ref[part, group, 2 + e, 16 * tile : 16 * tile + 16] for e in range(ROWS)],
                 )
         give(
-            28 + 4 * group,
+            4 * OWN + 4 * group,
             count,
             [u_ref[part, group, 2 + e, 32:40] for e in range(ROWS) for part in range(2)],
         )
 
 
-def inverse_kernel(in_ref, high_ref, low_ref, out_ref):
+def inverse_kernel(in_ref, local_ref, high_ref, low_ref, out_ref):
     totals = []
     for part in range(2):
         columns = []
-        for start in (KEPT * part, 14 + KEPT * part, 28):
-            pieces = [in_ref[pl.ds(start + k, LAT, stride=LAT_CHUNK), :] for k in range(KEPT)]
+        for tile, start in enumerate((OWN * part, OWN * (2 + part), 4 * OWN)):
+            pieces = [in_ref[pl.ds(start + k, LAT, stride=LAT_CHUNK), :] for k in range(OWN)]
+            row = LAT * part if tile < 2 else 0
+            pieces.append(local_ref[row : row + LAT, 128 * tile : 128 * tile + 128])
             columns.append(jnp.concatenate(pieces + [jnp.zeros((LAT, 128), f32)], axis=0))
         x = split(jnp.concatenate(columns, axis=1))
         totals.append(dot3((high_ref[part], low_ref[part]), x))
@@ -404,7 +511,7 @@
     )(*operands)
 
 
-def legendre(owner, angles, seeds):
+def legendre(*operands):
     table = jax.ShapeDtypeStruct((OWN, MODES, NLAT), bf16)
     return pl.pallas_call(
         legendre_kernel,
@@ -414,12 +521,35 @@
         scratch_shapes=[pltpu.VMEM((8 * MODES, 128), f32)] * 2,
         compiler_params=pltpu.CompilerParams(vmem_limit_bytes=16 << 20),
         cost_estimate=pl.CostEstimate(flops=10**7, bytes_accessed=10**7, transcendentals=0),
-    )(owner, angles, seeds)
+    )(*operands)
+
+
+def factors(*operands):
+    return pl.pallas_call(
+        taps_kernel,
+        out_shape=tuple(jax.ShapeDtypeStruct(shape, f32) for shape in ((10 * SLICE, 768), (50, 384))),
+        in_specs=vmem(4),
+        out_specs=vmem(2),
+        compiler_params=pltpu.CompilerParams(vmem_limit_bytes=16 << 20),
+        cost_estimate=pl.CostEstimate(flops=10**7, bytes_accessed=10**7, transcendentals=0),
+    )(*operands)
 
 
 def own_channels(array, axis, start, odd):
     part = lax.dynamic_slice_in_dim(array, start, SLICE, axis)
     return jnp.where(odd, jnp.roll(part, -8, axis), part)
+
+
+def wave_np():
+    angle = 2.0 * np.pi * (MODES + np.arange(LAT)) / NLON
+    waves = [np.cos(angle), np.cos(2.0 * angle), np.sin(angle), np.sin(2.0 * angle)]
+    return np.repeat(np.stack(waves, axis=1), 128, axis=1).astype(np.float32)
+
+
+def lanes_np():
+    lane = np.arange(128)
+    channel = np.concatenate([lane % 16, 16 + lane % 16, 32 + lane % 8])
+    return (np.arange(SLICE)[:, None] == channel[None, :]).astype(np.float32)
 
 
 def exchange(array, axis, count):
@@ -441,25 +571,57 @@
         pack_kernel,
         (LON * LON_CHUNK, 128),
         latent.transpose(1, 0, 2),
-        scratch=[pltpu.VMEM((COLS, ROWS, CHANNELS), f32), pltpu.SemaphoreType.DMA((5,))],
+        scratch=[
+            pltpu.VMEM((COLS, ROWS, CHANNELS), f32),
+            pltpu.VMEM((LON * LON_CHUNK, 128), f32),
+            pltpu.SemaphoreType.DMA((5,)),
+            pltpu.SemaphoreType.DMA((8,)),
+        ],
         far=1,
         grant=60,
+        out=pltpu.HBM,
     )
     circles = exchange(packed, "lon", LON)
 
     seeds = lax.dynamic_index_in_dim(jnp.asarray(seed_np()), band, 0, False)
-    high, low = legendre(band.astype(jnp.int32).reshape(1), angles, seeds)
-    phases = lax.dynamic_index_in_dim(jnp.asarray(phase_np()), band, 0, False)
-    spread_np = np.kron(np.eye(24, dtype=np.float32), np.ones((1, LAT), np.float32))
-    taps = jnp.stack([conv_first, conv_second]).reshape(2, 5, 5, CHANNELS)
-    taps = own_channels(taps, 3, sector * SLICE, odd).transpose(0, 1, 3, 2).reshape(10 * SLICE, 5)
-    taps = jnp.dot(taps, phases, precision=lax.Precision.HIGHEST)
-    taps = jnp.dot(taps, jnp.asarray(spread_np), precision=lax.Precision.HIGHEST)
+    owner = band.astype(jnp.int32).reshape(1)
+    high, low = legendre(owner, angles, seeds)
     gains = own_channels(filter_gains, 1, 0, odd).T
     gains = jnp.concatenate([gains, gains, gains, jnp.where(band == 0, 0.0, gains)], axis=0)
 
-    coeffs = run(forward_kernel, (LAT * LAT_CHUNK, 128), circles, *map(jnp.asarray, forward))
+    circles, high, low = lax.optimization_barrier((circles, high, low))
+
+    shapes = ((LAT * LAT_CHUNK, 128), (2 * LAT, 384), (3 * LAT, 128), (3 * LAT, 128))
+    coeffs, local, up, down = pl.pallas_call(
+        forward_kernel,
+        out_shape=tuple(jax.ShapeDtypeStruct(shape, f32) for shape in shapes),
+        in_specs=vmem(3),
+        out_specs=vmem(4),
+        compiler_params=pltpu.CompilerParams(vmem_limit_bytes=24 << 20),
+    )(circles, *map(jnp.asarray, forward))
     orders = exchange(coeffs, "lat", LAT)
+    local, conv_first, conv_second = lax.optimization_barrier((local, conv_first, conv_second))
+    phases = lax.dynamic_index_in_dim(jnp.asarray(phase_np()), band, 0, False)
+    own_taps = jnp.stack([conv_first, conv_second]).reshape(2, 5, 5, CHANNELS)
+    own_taps = own_channels(own_taps, 3, sector * SLICE, odd)
+    taps, lane_taps = factors(
+        own_taps.transpose(0, 1, 3, 2).reshape(10 * SLICE, 5),
+        phases,
+        own_taps.reshape(50, SLICE),
+        jnp.asarray(lanes_np()),
+    )
+    rising = [(n, n + 1) for n in range(LAT - 1)]
+    below = lax.ppermute(up, "lat", rising)
+    above = lax.ppermute(down, "lat", [(target, source) for source, target in rising])
+    stay = pl.pallas_call(
+        local_kernel,
+        out_shape=jax.ShapeDtypeStruct((2 * LAT, 384), f32),
+        in_specs=[pl.BlockSpec(memory_space=pltpu.SMEM)] + vmem(5),
+        out_specs=vmem(1)[0],
+        compiler_params=pltpu.CompilerParams(vmem_limit_bytes=16 << 20),
+        cost_estimate=pl.CostEstimate(flops=10**7, bytes_accessed=10**6, transcendentals=0),
+    )(owner, local, below, above, lane_taps, jnp.asarray(wave_np()))
+    orders, stay, taps = lax.optimization_barrier((orders, stay, taps))
     state = pltpu.VMEM((2, 2, 12, SLICE, 128), f32)
     third = run(
         spectral_kernel,
@@ -473,7 +635,7 @@
         scratch=[state, state, pltpu.VMEM((OWN, 2 * SLICE, NLAT), f32)],
     )
     returned = exchange(third, "lat", LAT)
-    restored = run(inverse_kernel, (LON * LON_CHUNK, 128), returned, *map(jnp.asarray, inverse))
+    restored = run(inverse_kernel, (LON * LON_CHUNK, 128), returned, stay, *map(jnp.asarray, inverse))
     arrived = exchange(restored, "lon", LON)
     result = run(
         mlp_kernel,

time: 117 us -> 116 us (level)
  waiting for transfers between devices: 33.4 us -> 22.3 us
  starting transfers between devices: 21.4 us -> 28.5 us
  Pallas kernels: 12.8 us -> 16.5 us
  matrix products: 2.12 us -> 0 us
    all_to_all x2, waiting for transfers between devices: 33.4 us -> 21.8 us  [exchange(): lax.all_to_all(array.reshape(shape), axis, split_axis=0, concat_axis=0, t...]
    ppermute x0 -> x2, starting transfers between devices: none -> 7.07 us  [the longest x1 5.04 us: per_device(): lax.ppermute(down, 'lat', [(target, source) for source, target in rising])]
    pallas_call x0 -> x3, Pallas kernels: none -> 5.5 us  [the longest x1 1.98 us: per_device(): pl.pallas_call(local_kernel, out_shape=jax.ShapeDtypeStruct((2 * LAT, 384...]
    dot_general x2 -> x0, matrix products: 2.12 us -> none  [the longest x1 1.19 us: per_device(): jnp.dot(taps, jnp.asarray(spread_np), precision=lax.Precision.HIGHEST)]
    pallas_call x5 -> x4, Pallas kernels: 11.9 us -> 10.2 us  [run(): pl.pallas_call(kernel, out_shape=jax.ShapeDtypeStruct(shape, f32), in_spe...]
  transfers between devices with their start and end apart: 2 -> 4, of which waited for: 2 -> 3; matrix products, arithmetic and copies ran while one was open for 3% -> 2% of each run, Pallas kernels for 1% -> 4%
where the time goes in v3:
time: 116 us; the launch traced here: 115 us
  blocking collectives  46 us (40%)
  starting transfers between devices  28.5 us (25%)
  waiting for transfers between devices  22.3 us (19%)
  Pallas kernels  16.5 us (14%)
  local copies, waits for them, and re-layouts  1.77 us (2%)
    all_to_all x2, blocking collectives, exchange(): lax.all_to_all(array.reshape(shape), axis, split_axis=0, concat_axis=0, t...  46 us
    all_to_all x2, waiting for transfers between devices, exchange(): lax.all_to_all(array.reshape(shape), axis, split_axis=0, concat_axis=0, t...  21.8 us
    all_to_all x2, starting transfers between devices, exchange(): lax.all_to_all(array.reshape(shape), axis, split_axis=0, concat_axis=0, t...  21.4 us
    pallas_call x4, Pallas kernels, run(): pl.pallas_call(kernel, out_shape=jax.ShapeDtypeStruct(shape, f32), in_spe...  10.2 us
    ppermute x1, starting transfers between devices, per_device(): lax.ppermute(down, 'lat', [(target, source) for source, target in rising])  5.04 us
  transfers between devices with their start and end apart: 4, of which 3 were waited for; matrix products, arithmetic and copies ran while one was open for 2% of the time, Pallas kernels for 4%

profile of v3, /device:TPU:4, one launch (start us, length us, event | category | flops | bytes accessed | tf_op | source)
XLA Modules:
  0.0 115.5 jit_solution(11658334634679899706)
XLA Ops:
  0.0 3.3 %shard_map.154 = f32[1152,128]{1,0:T(8,128)} custom-call(f32[28,8,640]{2,1,0:T(8,128)} %bitcast.29), custom_call_target="tpu_custom_call" | custom-call | tf_op jit(solution)/shard_map/pallas_call | solution.py:503
  3.3 7.9 %all-to-all-start = ((f32[16,72,128]{2,1,0:T(8,128)}), f32[16,72,128]{2,1,0:T(8,128)S(1)}, u32[]{:S(2)}, u32[]{:S(2)}) async-start(f32[16,72,128]{2,1,0:T(8,128)} %bitcast.28), calls=%async_computation | async-start | bytes 1179648 | tf_op jit(solution)/shard_map/all_to_all | solution.py:558
  11.2 0.0 copy-start.12
  11.2 0.8 dynamic-slice_bitcast_fusion.1.seed_ref
  12.0 0.9 shard_map.155
  12.9 17.2 %all-to-all-done = f32[16,72,128]{2,1,0:T(8,128)S(1)} async-done(((f32[16,72,128]{2,1,0:T(8,128)}), f32[16,72,128]{2,1,0:T(8,128)S(1)}, u32[]{:S(2)}, u32[]{:S(2)}) %all-to-all-start) | async-done | bytes 589856 | tf_op jit(solution)/shard_map/all_to_all | solution.py:558
  30.1 1.7 %shard_map.156 = (f32[960,128]{1,0:T(8,128)}, f32[64,384]{1,0:T(8,128)S(1)}, f32[96,128]{1,0:T(8,128)}, f32[96,128]{1,0:T(8,128)}) custom-call(f32[1152,128]{1,0:T(8,128)S(1)} %bitcast.22, bf16[448,512]{1,0:T(8,128)(2,1)S(1)} %copy-done.5, bf16[448,512]{1,0:T(8,128)(2,1)S(1)} %copy-done.4), custom_call_target="tpu_custom_call" | custom-call | tf_op jit(solution)/shard_map/pallas_call | solution.py:595
  31.8 13.6 %all-to-all-start.1 = ((f32[32,1,3840]{2,1,0:T(1,128)}), f32[32,1,3840]{2,1,0:T(1,128)S(1)}, u32[]{:S(2)}, u32[]{:S(2)}) async-start(f32[32,1,3840]{2,1,0:T(1,128)} %bitcast.5), calls=%async_computation.1 | async-start | bytes 983040 | tf_op jit(solution)/shard_map/all_to_all | solution.py:558
  45.4 0.7 dynamic-slice_bitcast_fusion.phase_ref
  46.2 2.0 %collective-permute-start = (f32[96,128]{1,0:T(8,128)}, f32[96,128]{1,0:T(8,128)}, u32[]{:S(2)}, u32[]{:S(2)}) collective-permute-start(f32[96,128]{1,0:T(8,128)} %get-tuple-element.28), channel_id=1, source_target_pairs={{0,16},{16,32},{32,48},{48,64},{64,80},{80,96},{96,112},{112,128},... | collective-permute-start | bytes 147464 | tf_op jit(solution)/shard_map/ppermute | solution.py:614
  48.2 5.0 %collective-permute-start.1 = (f32[96,128]{1,0:T(8,128)}, f32[96,128]{1,0:T(8,128)}, u32[]{:S(2)}, u32[]{:S(2)}) collective-permute-start(f32[96,128]{1,0:T(8,128)} %get-tuple-element.29), channel_id=1, source_target_pairs={{16,0},{32,16},{48,32},{64,48},{80,64},{96,80},{112,96},{128,112},... | collective-permute-start | bytes 147464 | tf_op jit(solution)/shard_map/ppermute | solution.py:615
  53.3 0.1 fusion
  53.4 0.1 slice.20
  53.5 0.1 maximum_select_fusion
  53.6 0.1 copy.20
  53.7 1.8 %shard_map.157 = (f32[400,768]{1,0:T(8,128)S(1)}, f32[50,384]{1,0:T(8,128)S(1)}) custom-call(f32[400,5]{1,0:T(8,128)S(1)} %bitcast.27, f32[8,24]{1,0:T(8,128)S(1)} %dynamic-slice_bitcast_fusion.phase_ref, f32[50,40]{1,0:T(8,128)S(1)} %reshape.44.plain_ref, f32[40,384]{1,0:T(8,128)S(1)} %copy-done.7), custom_call_target="tpu_custom_call" | custom-call | flops 10000000 | bytes 10000000 | tf_op jit(solution)/shard_map/pallas_call | solution.py:528
  55.6 0.5 collective-permute-done.1.above_ref
  56.1 2.0 %shard_map.158.local_ref = f32[64,384]{1,0:T(8,128)S(1)} custom-call(s32[1]{0:T(128)} %bitcast.3.owner_ref.band_ref, f32[64,384]{1,0:T(8,128)S(1)} %get-tuple-element.27.own_ref, f32[96,128]{1,0:T(8,128)} %collective-permute-done.below_ref, f32[96,128]{1,0:T(8,128)} %collective-permute-done.1.above_ref, f32[50,384]{1,0:T(8,128)S(1)} %get-tuple-element.32.taps_ref, ...), custom_call_target="tpu_custom_call" | custom-call | flops 10000000 | bytes 1000000 | tf_op jit(solution)/shard_map/pallas_call | solution.py:616
  58.0 4.6 %all-to-all-done.1 = f32[32,1,3840]{2,1,0:T(1,128)S(1)} async-done(((f32[32,1,3840]{2,1,0:T(1,128)}), f32[32,1,3840]{2,1,0:T(1,128)S(1)}, u32[]{:S(2)}, u32[]{:S(2)}) %all-to-all-start.1) | async-done | bytes 491552 | tf_op jit(solution)/shard_map/all_to_all | solution.py:558
  62.6 3.1 %shard_map.159 = f32[960,128]{1,0:T(8,128)S(1)} custom-call(f32[960,128]{1,0:T(8,128)S(1)} %bitcast.24, bf16[6,192,256]{2,1,0:T(8,128)(2,1)S(1)} %get-tuple-element.35.high_ref, bf16[6,192,256]{2,1,0:T(8,128)(2,1)S(1)} %get-tuple-element.36.low_ref, f32[400,768]{1,0:T(8,128)S(1)} %get-tuple-element.37.taps_ref, f32[160,192]{1,0:T(8,128)S(1)} %pad_maximum_fusion.gain_ref, ...), custom_call_target="tpu_custom_call" | custom-call | tf_op jit(solution)/shard_map/pallas_call | solution.py:503
  65.7 24.1 %all_to_all.20 = f32[32,1,3840]{2,1,0:T(1,128)S(1)} all-to-all(f32[32,1,3840]{2,1,0:T(1,128)S(1)} %bitcast.25), channel_id=1, replica_groups=mesh['lat'=32,'lon'=16] {'lat'}, dimensions={0} | all-to-all | bytes 983040 | tf_op jit(solution)/shard_map/all_to_all | solution.py:558
  89.9 1.0 shard_map.160
  90.9 21.9 %all_to_all.21 = f32[16,72,128]{2,1,0:T(8,128)S(1)} all-to-all(f32[16,72,128]{2,1,0:T(8,128)S(1)} %bitcast.23), channel_id=1, replica_groups=mesh['lat'=32,'lon'=16] {'lon'}, dimensions={0} | all-to-all | bytes 1179648 | tf_op jit(solution)/shard_map/all_to_all | solution.py:558
  112.8 2.7 %shard_map.161 = f32[28,8,640]{2,1,0:T(8,128)} custom-call(f32[1152,128]{1,0:T(8,128)S(1)} %bitcast.21, f32[640]{0:T(1024)S(1)} %copy-done.9, bf16[640,1280]{1,0:T(8,128)(2,1)S(1)} %copy-done, bf16[1280,640]{1,0:T(8,128)(2,1)S(1)} %copy-done.1), custom_call_target="tpu_custom_call" | custom-call | tf_op jit(solution)/shard_map/pallas_call | solution.py:503
  (35 shorter events, 0.1 us)
Async XLA Ops:
  0.0 12.0 %copy-start.8 = (f32[8,256]{1,0:T(8,128)S(1)}, f32[8,256]{1,0:T(8,128)}, u32[]{:S(2)}) copy-start(f32[8,256]{1,0:T(8,128)} %constant.57.clone.angle_ref) | copy-start | bytes 24580
  0.0 30.1 %copy-start.4 = (bf16[448,512]{1,0:T(8,128)(2,1)S(1)}, bf16[448,512]{1,0:T(8,128)(2,1)}, u32[]{:S(2)}) copy-start(bf16[448,512]{1,0:T(8,128)(2,1)} %constant.60.clone.low_ref) | copy-start | bytes 1376260
  0.0 30.1 %copy-start.5 = (bf16[448,512]{1,0:T(8,128)(2,1)S(1)}, bf16[448,512]{1,0:T(8,128)(2,1)}, u32[]{:S(2)}) copy-start(bf16[448,512]{1,0:T(8,128)(2,1)} %constant.59.clone.high_ref) | copy-start | bytes 1376260
  3.3 26.8 %all-to-all-start = ((f32[16,72,128]{2,1,0:T(8,128)}), f32[16,72,128]{2,1,0:T(8,128)S(1)}, u32[]{:S(2)}, u32[]{:S(2)}) async-start(f32[16,72,128]{2,1,0:T(8,128)} %bitcast.28), calls=%async_computation | async-start | bytes 1179648 | tf_op jit(solution)/shard_map/all_to_all | solution.py:558
  11.2 34.9 %copy-start.10 = (f32[192,40]{0,1:T(8,128)S(1)}, f32[192,40]{0,1:T(8,128)}, u32[]{:S(2)}) copy-start(f32[192,40]{0,1:T(8,128)} %param.19) | copy-start | bytes 92164
  11.2 34.9 %slice-start = ((f32[192,40]{0,1:T(8,128)}), f32[192,8]{0,1:T(8,128)S(1)}, s32[]{:S(2)}) async-start(f32[192,40]{0,1:T(8,128)} %param.19), calls=%async_computation.4 | async-start | bytes 16384 | tf_op jit(solution)/shard_map/jit(_roll_static)/slice | solution.py:540
  11.2 34.9 %slice-start.1 = ((f32[192,40]{0,1:T(8,128)}), f32[192,32]{0,1:T(8,128)S(1)}, s32[]{:S(2)}) async-start(f32[192,40]{0,1:T(8,128)} %param.19), calls=%async_computation.5 | async-start | bytes 65536 | tf_op jit(solution)/shard_map/jit(_roll_static)/slice | solution.py:540
  11.2 42.0 %copy-start.11 = (f32[25,640]{1,0:T(8,128)S(1)}, f32[25,640]{1,0:T(8,128)}, u32[]{:S(2)}) copy-start(f32[25,640]{1,0:T(8,128)} %param.17) | copy-start | bytes 192004
  11.2 42.0 %copy-start.12 = (f32[25,640]{1,0:T(8,128)S(1)}, f32[25,640]{1,0:T(8,128)}, u32[]{:S(2)}) copy-start(f32[25,640]{1,0:T(8,128)} %param.18) | copy-start | bytes 192004
  31.8 21.9 %copy-start.7 = (f32[40,384]{1,0:T(8,128)S(1)}, f32[40,384]{1,0:T(8,128)}, u32[]{:S(2)}) copy-start(f32[40,384]{1,0:T(8,128)} %constant.62.clone.lanes_ref) | copy-start | bytes 184324
  31.8 24.2 %copy-start.6 = (f32[32,512]{1,0:T(8,128)S(1)}, f32[32,512]{1,0:T(8,128)}, u32[]{:S(2)}) copy-start(f32[32,512]{1,0:T(8,128)} %constant.63.clone.wave_ref) | copy-start | bytes 196612
  31.8 30.8 %all-to-all-start.1 = ((f32[32,1,3840]{2,1,0:T(1,128)}), f32[32,1,3840]{2,1,0:T(1,128)S(1)}, u32[]{:S(2)}, u32[]{:S(2)}) async-start(f32[32,1,3840]{2,1,0:T(1,128)} %bitcast.5), calls=%async_computation.1 | async-start | bytes 983040 | tf_op jit(solution)/shard_map/all_to_all | solution.py:558
  46.2 9.4 %collective-permute-start = (f32[96,128]{1,0:T(8,128)}, f32[96,128]{1,0:T(8,128)}, u32[]{:S(2)}, u32[]{:S(2)}) collective-permute-start(f32[96,128]{1,0:T(8,128)} %get-tuple-element.28), channel_id=1, source_target_pairs={{0,16},{16,32},{32,48},{48,64},{64,80},{80,96},{96,112},{112,128},... | collective-permute-start | bytes 147464 | tf_op jit(solution)/shard_map/ppermute | solution.py:614
  48.2 7.9 %collective-permute-start.1 = (f32[96,128]{1,0:T(8,128)}, f32[96,128]{1,0:T(8,128)}, u32[]{:S(2)}, u32[]{:S(2)}) collective-permute-start(f32[96,128]{1,0:T(8,128)} %get-tuple-element.29), channel_id=1, source_target_pairs={{16,0},{32,16},{48,32},{64,48},{80,64},{96,80},{112,96},{128,112},... | collective-permute-start | bytes 147464 | tf_op jit(solution)/shard_map/ppermute | solution.py:615
  62.6 27.3 %copy-start.2 = (bf16[2,512,256]{2,1,0:T(8,128)(2,1)S(1)}, bf16[2,512,256]{2,1,0:T(8,128)(2,1)}, u32[]{:S(2)}) copy-start(bf16[2,512,256]{2,1,0:T(8,128)(2,1)} %constant.65.clone.low_ref) | copy-start | bytes 1572868
  62.6 27.3 %copy-start.3 = (bf16[2,512,256]{2,1,0:T(8,128)(2,1)S(1)}, bf16[2,512,256]{2,1,0:T(8,128)(2,1)}, u32[]{:S(2)}) copy-start(bf16[2,512,256]{2,1,0:T(8,128)(2,1)} %constant.64.clone.high_ref) | copy-start | bytes 1572868
  89.9 22.9 %copy-start = (bf16[640,1280]{1,0:T(8,128)(2,1)S(1)}, bf16[640,1280]{1,0:T(8,128)(2,1)}, u32[]{:S(2)}) copy-start(bf16[640,1280]{1,0:T(8,128)(2,1)} %up_ref.1) | copy-start | bytes 4915204
  89.9 22.9 %copy-start.1 = (bf16[1280,640]{1,0:T(8,128)(2,1)S(1)}, bf16[1280,640]{1,0:T(8,128)(2,1)}, u32[]{:S(2)}) copy-start(bf16[1280,640]{1,0:T(8,128)(2,1)} %down_ref.1) | copy-start | bytes 4915204
  89.9 22.9 %copy-start.9 = (f32[640]{0:T(1024)S(1)}, f32[640]{0:T(1024)}, u32[]{:S(2)}) copy-start(f32[640]{0:T(1024)} %gain_ref.1) | copy-start | bytes 7684

commit v4 on v3

--- a/solution.py
+++ b/solution.py
@@ -13,7 +13,7 @@
 NLAT, NLON, MODES = 256, 448, 192
 OWN = MODES // LAT
 KEPT = OWN + 1
-LON_CHUNK = 72
+LON_CHUNK = 70
 LAT_CHUNK = 30
 f32, bf16 = jnp.float32, jnp.bfloat16
 
@@ -49,18 +49,22 @@
     return forward.reshape(2 * KEPT * LAT, 512), inverse.reshape(2, 512, 8 * LAT)
 
 
+FACTOR_TILES = ((0, 1, 2), (3, 3, 4))
+
+
 def phase_np():
-    table = np.zeros((LAT, 8, 2, 3, 4))
+    table = np.zeros((LAT, 8, 5, 4))
     for owner in range(LAT):
-        for slot in range(KEPT):
+        for slot in range(OWN):
             order = order_of(owner, slot)
+            real, second, imag = FACTOR_TILES[slot // 4]
             for b in range(-2, 3):
                 angle = 2.0 * np.pi * ((order * b) % NLON) / NLON
-                where = (owner, b + 2, slot // 4)
-                table[where + (0, slot % 4)] = np.cos(angle)
-                table[where + (1, slot % 4)] = np.cos(np.pi * b) if order == 0 else np.cos(angle)
-                table[where + (2, slot % 4)] = np.sin(angle)
-    return table.reshape(LAT, 8, 24).astype(np.float32)
+                table[owner, b + 2, real, slot % 4] = np.cos(angle)
+                if second != real:
+                    table[owner, b + 2, second, slot % 4] = np.cos(np.pi * b) if order == 0 else np.cos(angle)
+                table[owner, b + 2, imag, slot % 4] = np.sin(angle)
+    return table.reshape(LAT, 8, 20).astype(np.float32)
 
 
 def latitude_np():
@@ -135,15 +139,13 @@
                 top, bottom = block[:14], block[14:]
                 out_ref[even + 56 : even + 70] = jnp.where(first, top, pltpu.roll(bottom, 8, 1))
                 out_ref[odd + 56 : odd + 70] = jnp.where(first, pltpu.roll(top, 120, 1), bottom)
-                out_ref[even + 70 : even + 72] = jnp.zeros((2, 128), f32)
-                out_ref[odd + 70 : odd + 72] = jnp.zeros((2, 128), f32)
             else:
                 base = (even, even + 28, None, odd, odd + 28)[place]
                 out_ref[base : base + 28] = block
-            if place == 4:
-                rows = pl.ds(even, 2 * LON_CHUNK)
-                stores.append(pltpu.make_async_copy(out_ref.at[rows], out_hbm.at[rows], sent.at[pair]))
-                stores[pair].start()
+            if place == 4 and pair % 2:
+                rows = pl.ds(even - 2 * LON_CHUNK, 4 * LON_CHUNK)
+                stores.append(pltpu.make_async_copy(out_ref.at[rows], out_hbm.at[rows], sent.at[pair // 2]))
+                stores[-1].start()
     for store in stores:
         store.wait()
 
@@ -153,12 +155,10 @@
     for half in range(2):
         pieces = []
         for start in (14 * half, 28 + 14 * half, 56):
-            pieces.append(
-                jnp.concatenate(
-                    [in_ref[LON_CHUNK * q + start : LON_CHUNK * q + start + 16] for q in range(LON)],
-                    axis=0,
-                )
-            )
+            blocks = [in_ref[LON_CHUNK * q + start : LON_CHUNK * q + start + 16] for q in range(LON - 1)]
+            tail = LON_CHUNK * (LON - 1) + start
+            blocks += [in_ref[tail : tail + 14], jnp.zeros((2, 128), f32)]
+            pieces.append(jnp.concatenate(blocks, axis=0))
         x = split(jnp.concatenate(pieces, axis=1))
         lanes = slice(256 * half, 256 * half + 256)
         totals.append(dot3((high_ref[:, lanes], low_ref[:, lanes]), x))
@@ -267,7 +267,7 @@
 
 def taps_kernel(rows_ref, phase_ref, plain_ref, lanes_ref, taps_ref, spread_ref):
     spread_ref[...] = jnp.dot(plain_ref[...], lanes_ref[...], precision=lax.Precision.HIGHEST)
-    for tile in range(6):
+    for tile in range(5):
         phase = phase_ref[:, 4 * tile : 4 * tile + 1]
         for n in range(1, 4):
             column = phase_ref[:, 4 * tile + n : 4 * tile + n + 1]
@@ -331,8 +331,8 @@
                     base = (which * 5 + a) * SLICE + 8 * tile
                     taps.append(
                         [
-                            taps_ref[base : base + 8, (group * 3 + kind) * 128 : (group * 3 + kind) * 128 + 128]
-                            for kind in range(3)
+                            taps_ref[base : base + 8, 128 * column : 128 * column + 128]
+                            for column in FACTOR_TILES[group]
                         ]
                     )
                 real = [ref[0, group, e, rows] for e in range(12)]
@@ -454,7 +454,7 @@
                 row = 256 * half + 16 * q
                 start = base + 28 * tile + 14 * half
                 out_ref[start : start + 14] = both[row : row + 14, 128 * tile : 128 * tile + 128]
-        out_ref[base + 56 : base + 72] = last[16 * q : 16 * q + 16]
+        out_ref[base + 56 : base + 70] = last[16 * q : 16 * q + 14]
 
 
 def mlp_kernel(in_ref, gain_ref, up_ref, down_ref, out_hbm, x_ref, y_ref, sent):
@@ -527,7 +527,7 @@
 def factors(*operands):
     return pl.pallas_call(
         taps_kernel,
-        out_shape=tuple(jax.ShapeDtypeStruct(shape, f32) for shape in ((10 * SLICE, 768), (50, 384))),
+        out_shape=tuple(jax.ShapeDtypeStruct(shape, f32) for shape in ((10 * SLICE, 640), (50, 384))),
         in_specs=vmem(4),
         out_specs=vmem(2),
         compiler_params=pltpu.CompilerParams(vmem_limit_bytes=16 << 20),
@@ -575,7 +575,7 @@
             pltpu.VMEM((COLS, ROWS, CHANNELS), f32),
             pltpu.VMEM((LON * LON_CHUNK, 128), f32),
             pltpu.SemaphoreType.DMA((5,)),
-            pltpu.SemaphoreType.DMA((8,)),
+            pltpu.SemaphoreType.DMA((4,)),
         ],
         far=1,
         grant=60,
@@ -621,7 +621,7 @@
         compiler_params=pltpu.CompilerParams(vmem_limit_bytes=16 << 20),
         cost_estimate=pl.CostEstimate(flops=10**7, bytes_accessed=10**6, transcendentals=0),
     )(owner, local, below, above, lane_taps, jnp.asarray(wave_np()))
-    orders, stay, taps = lax.optimization_barrier((orders, stay, taps))
+    orders, taps = lax.optimization_barrier((orders, taps))
     state = pltpu.VMEM((2, 2, 12, SLICE, 128), f32)
     third = run(
         spectral_kernel,

time: 116 us -> 114 us (0.983)
  blocking collectives: 46 us -> 21.3 us
  waiting for transfers between devices: 22.3 us -> 40 us
  starting transfers between devices: 28.5 us -> 33.7 us
    all_to_all x2 -> x1, blocking collectives: 46 us -> 21.3 us  [exchange(): lax.all_to_all(array.reshape(shape), axis, split_axis=0, concat_axis=0, t...]
    all_to_all x2 -> x3, waiting for transfers between devices: 21.8 us -> 38.3 us  [exchange(): lax.all_to_all(array.reshape(shape), axis, split_axis=0, concat_axis=0, t...]
    all_to_all x2 -> x3, starting transfers between devices: 21.4 us -> 26.7 us  [exchange(): lax.all_to_all(array.reshape(shape), axis, split_axis=0, concat_axis=0, t...]
    ppermute x1, waiting for transfers between devices: 0.48 us -> 1.72 us  [per_device(): lax.ppermute(down, 'lat', [(target, source) for source, target in rising])]
  transfers between devices with their start and end apart: 4 -> 5, of which waited for: 3 -> 4; matrix products, arithmetic and copies ran while one was open for 2% -> 2% of each run, Pallas kernels for 4% -> 3%
where the time goes in v4:
time: 114 us; the launch traced here: 113 us
  waiting for transfers between devices  40 us (35%)
  starting transfers between devices  33.7 us (30%)
  blocking collectives  21.3 us (19%)
  Pallas kernels  16.1 us (14%)
  local copies, waits for them, and re-layouts  1.75 us (2%)
    all_to_all x3, waiting for transfers between devices, exchange(): lax.all_to_all(array.reshape(shape), axis, split_axis=0, concat_axis=0, t...  38.3 us
    all_to_all x3, starting transfers between devices, exchange(): lax.all_to_all(array.reshape(shape), axis, split_axis=0, concat_axis=0, t...  26.7 us
    all_to_all x1, blocking collectives, exchange(): lax.all_to_all(array.reshape(shape), axis, split_axis=0, concat_axis=0, t...  21.3 us
    pallas_call x4, Pallas kernels, run(): pl.pallas_call(kernel, out_shape=jax.ShapeDtypeStruct(shape, f32), in_spe...  10.9 us
    ppermute x1, starting transfers between devices, per_device(): lax.ppermute(down, 'lat', [(target, source) for source, target in rising])  5.04 us
  transfers between devices with their start and end apart: 5, of which 4 were waited for; matrix products, arithmetic and copies ran while one was open for 2% of the time, Pallas kernels for 3%

profile of v4, /device:TPU:4, one launch (start us, length us, event | category | flops | bytes accessed | tf_op | source)
XLA Modules:
  0.0 113.4 jit_solution(5058986588944579036)
XLA Ops:
  0.0 3.3 %shard_map.154 = f32[1120,128]{1,0:T(8,128)} custom-call(f32[28,8,640]{2,1,0:T(8,128)} %bitcast.28), custom_call_target="tpu_custom_call" | custom-call | tf_op jit(solution)/shard_map/pallas_call | solution.py:503
  3.3 8.0 %all-to-all-start = ((f32[16,1,8960]{2,1,0:T(1,128)}), f32[16,1,8960]{2,1,0:T(1,128)S(1)}, u32[]{:S(2)}, u32[]{:S(2)}) async-start(f32[16,1,8960]{2,1,0:T(1,128)} %bitcast.27), calls=%async_computation | async-start | bytes 1146880 | tf_op jit(solution)/shard_map/all_to_all | solution.py:558
  11.3 0.7 dynamic-slice_bitcast_fusion.1.seed_ref
  12.1 0.9 shard_map.155
  13.0 16.9 %all-to-all-done = f32[16,1,8960]{2,1,0:T(1,128)S(1)} async-done(((f32[16,1,8960]{2,1,0:T(1,128)}), f32[16,1,8960]{2,1,0:T(1,128)S(1)}, u32[]{:S(2)}, u32[]{:S(2)}) %all-to-all-start) | async-done | bytes 573472 | tf_op jit(solution)/shard_map/all_to_all | solution.py:558
  29.8 1.7 %shard_map.156 = (f32[960,128]{1,0:T(8,128)}, f32[64,384]{1,0:T(8,128)S(1)}, f32[96,128]{1,0:T(8,128)S(1)}, f32[96,128]{1,0:T(8,128)S(1)}) custom-call(f32[1120,128]{1,0:T(8,128)S(1)} %bitcast.23, bf16[448,512]{1,0:T(8,128)(2,1)S(1)} %copy-done.5, bf16[448,512]{1,0:T(8,128)(2,1)S(1)} %copy-done.4), custom_call_target="tpu_custom_call" | custom-call | tf_op jit(solution)/shard_map/pallas_call | solution.py:595
  31.5 13.6 %all-to-all-start.1 = ((f32[32,1,3840]{2,1,0:T(1,128)}), f32[32,1,3840]{2,1,0:T(1,128)S(1)}, u32[]{:S(2)}, u32[]{:S(2)}) async-start(f32[32,1,3840]{2,1,0:T(1,128)} %bitcast.5), calls=%async_computation.1 | async-start | bytes 983040 | tf_op jit(solution)/shard_map/all_to_all | solution.py:558
  45.1 0.7 dynamic-slice_bitcast_fusion.phase_ref
  45.9 0.1 fusion
  46.0 0.1 slice.20
  46.1 0.1 maximum_select_fusion
  46.2 0.1 copy.21
  46.4 1.5 %shard_map.157 = (f32[400,640]{1,0:T(8,128)S(1)}, f32[50,384]{1,0:T(8,128)S(1)}) custom-call(f32[400,5]{1,0:T(8,128)S(1)} %bitcast.26, f32[8,20]{1,0:T(8,128)S(1)} %dynamic-slice_bitcast_fusion.phase_ref, f32[50,40]{1,0:T(8,128)S(1)} %reshape.44.plain_ref, f32[40,384]{1,0:T(8,128)S(1)} %copy-done.7), custom_call_target="tpu_custom_call" | custom-call | flops 10000000 | bytes 10000000 | tf_op jit(solution)/shard_map/pallas_call | solution.py:528
  47.9 14.2 %all-to-all-done.1 = f32[32,1,3840]{2,1,0:T(1,128)S(1)} async-done(((f32[32,1,3840]{2,1,0:T(1,128)}), f32[32,1,3840]{2,1,0:T(1,128)S(1)}, u32[]{:S(2)}, u32[]{:S(2)}) %all-to-all-start.1) | async-done | bytes 491552 | tf_op jit(solution)/shard_map/all_to_all | solution.py:558
  62.1 3.9 %shard_map.158 = f32[960,128]{1,0:T(8,128)} custom-call(f32[960,128]{1,0:T(8,128)S(1)} %bitcast.24, bf16[6,192,256]{2,1,0:T(8,128)(2,1)S(1)} %get-tuple-element.30.high_ref, bf16[6,192,256]{2,1,0:T(8,128)(2,1)S(1)} %get-tuple-element.31.low_ref, f32[400,640]{1,0:T(8,128)S(1)} %get-tuple-element.32.taps_ref, f32[160,192]{1,0:T(8,128)S(1)} %pad_maximum_fusion.gain_ref, ...), custom_call_target="tpu_custom_call" | custom-call | tf_op jit(solution)/shard_map/pallas_call | solution.py:503
  66.0 5.1 %all-to-all-start.2 = ((f32[32,1,3840]{2,1,0:T(1,128)}), f32[32,1,3840]{2,1,0:T(1,128)S(1)}, u32[]{:S(2)}, u32[]{:S(2)}) async-start(f32[32,1,3840]{2,1,0:T(1,128)} %bitcast.11), calls=%async_computation.2 | async-start | bytes 983040 | tf_op jit(solution)/shard_map/all_to_all | solution.py:558
  71.1 2.0 %collective-permute-start = (f32[96,128]{1,0:T(8,128)S(1)}, f32[96,128]{1,0:T(8,128)S(1)}, u32[]{:S(2)}, u32[]{:S(2)}) collective-permute-start(f32[96,128]{1,0:T(8,128)S(1)} %get-tuple-element.34), channel_id=1, source_target_pairs={{0,16},{16,32},{32,48},{48,64},{64,80},{80,96},{96,112},{112,128},... | collective-permute-start | bytes 147464 | tf_op jit(solution)/shard_map/ppermute | solution.py:614
  73.1 5.0 %collective-permute-start.1 = (f32[96,128]{1,0:T(8,128)S(1)}, f32[96,128]{1,0:T(8,128)S(1)}, u32[]{:S(2)}, u32[]{:S(2)}) collective-permute-start(f32[96,128]{1,0:T(8,128)S(1)} %get-tuple-element.35), channel_id=1, source_target_pairs={{16,0},{32,16},{48,32},{64,48},{80,64},{96,80},{112,96},{128,112},... | collective-permute-start | bytes 147464 | tf_op jit(solution)/shard_map/ppermute | solution.py:615
  78.2 1.7 %collective-permute-done.1.above_ref = f32[96,128]{1,0:T(8,128)S(1)} collective-permute-done((f32[96,128]{1,0:T(8,128)S(1)}, f32[96,128]{1,0:T(8,128)S(1)}, u32[]{:S(2)}, u32[]{:S(2)}) %collective-permute-start.1) | collective-permute-done | bytes 49184 | tf_op jit(solution)/shard_map/ppermute | solution.py:615
  79.9 1.2 %shard_map.159.local_ref = f32[64,384]{1,0:T(8,128)S(1)} custom-call(s32[1]{0:T(128)} %bitcast.3.owner_ref.band_ref, f32[64,384]{1,0:T(8,128)S(1)} %get-tuple-element.33.own_ref, f32[96,128]{1,0:T(8,128)S(1)} %collective-permute-done.below_ref, f32[96,128]{1,0:T(8,128)S(1)} %collective-permute-done.1.above_ref, f32[50,384]{1,0:T(8,128)S(1)} %get-tuple-element.36.taps_ref, ...), custom_call_target="tpu_custom_call" | custom-call | flops 10000000 | bytes 1000000 | tf_op jit(solution)/shard_map/pallas_call | solution.py:616
  81.1 7.2 %all-to-all-done.2 = f32[32,1,3840]{2,1,0:T(1,128)S(1)} async-done(((f32[32,1,3840]{2,1,0:T(1,128)}), f32[32,1,3840]{2,1,0:T(1,128)S(1)}, u32[]{:S(2)}, u32[]{:S(2)}) %all-to-all-start.2) | async-done | bytes 491552 | tf_op jit(solution)/shard_map/all_to_all | solution.py:558
  88.3 1.0 shard_map.160
  89.3 21.3 %all_to_all.20 = f32[16,1,8960]{2,1,0:T(1,128)S(1)} all-to-all(f32[16,1,8960]{2,1,0:T(1,128)S(1)} %bitcast.22), channel_id=1, replica_groups=mesh['lat'=32,'lon'=16] {'lon'}, dimensions={0} | all-to-all | bytes 1146880 | tf_op jit(solution)/shard_map/all_to_all | solution.py:558
  110.6 2.7 %shard_map.161 = f32[28,8,640]{2,1,0:T(8,128)} custom-call(f32[1120,128]{1,0:T(8,128)S(1)} %bitcast.21, f32[640]{0:T(1024)S(1)} %copy-done.9, bf16[640,1280]{1,0:T(8,128)(2,1)S(1)} %copy-done, bf16[1280,640]{1,0:T(8,128)(2,1)S(1)} %copy-done.1), custom_call_target="tpu_custom_call" | custom-call | tf_op jit(solution)/shard_map/pallas_call | solution.py:503
  (36 shorter events, 0.1 us)
Async XLA Ops:
  0.0 12.1 %copy-start.8 = (f32[8,256]{1,0:T(8,128)S(1)}, f32[8,256]{1,0:T(8,128)}, u32[]{:S(2)}) copy-start(f32[8,256]{1,0:T(8,128)} %constant.57.clone.angle_ref) | copy-start | bytes 24580
  0.0 29.8 %copy-start.4 = (bf16[448,512]{1,0:T(8,128)(2,1)S(1)}, bf16[448,512]{1,0:T(8,128)(2,1)}, u32[]{:S(2)}) copy-start(bf16[448,512]{1,0:T(8,128)(2,1)} %constant.60.clone.low_ref) | copy-start | bytes 1376260
  0.0 29.8 %copy-start.5 = (bf16[448,512]{1,0:T(8,128)(2,1)S(1)}, bf16[448,512]{1,0:T(8,128)(2,1)}, u32[]{:S(2)}) copy-start(bf16[448,512]{1,0:T(8,128)(2,1)} %constant.59.clone.high_ref) | copy-start | bytes 1376260
  3.3 42.5 %copy-start.10 = (f32[192,40]{0,1:T(8,128)S(1)}, f32[192,40]{0,1:T(8,128)}, u32[]{:S(2)}) copy-start(f32[192,40]{0,1:T(8,128)} %param.19) | copy-start | bytes 92164
  3.3 42.5 %slice-start = ((f32[192,40]{0,1:T(8,128)}), f32[192,8]{0,1:T(8,128)S(1)}, s32[]{:S(2)}) async-start(f32[192,40]{0,1:T(8,128)} %param.19), calls=%async_computation.4 | async-start | bytes 16384 | tf_op jit(solution)/shard_map/jit(_roll_static)/slice | solution.py:540
  3.3 42.5 %slice-start.1 = ((f32[192,40]{0,1:T(8,128)}), f32[192,32]{0,1:T(8,128)S(1)}, s32[]{:S(2)}) async-start(f32[192,40]{0,1:T(8,128)} %param.19), calls=%async_computation.5 | async-start | bytes 65536 | tf_op jit(solution)/shard_map/jit(_roll_static)/slice | solution.py:540
  3.3 26.5 %all-to-all-start = ((f32[16,1,8960]{2,1,0:T(1,128)}), f32[16,1,8960]{2,1,0:T(1,128)S(1)}, u32[]{:S(2)}, u32[]{:S(2)}) async-start(f32[16,1,8960]{2,1,0:T(1,128)} %bitcast.27), calls=%async_computation | async-start | bytes 1146880 | tf_op jit(solution)/shard_map/all_to_all | solution.py:558
  11.3 34.6 %copy-start.11 = (f32[25,640]{1,0:T(8,128)S(1)}, f32[25,640]{1,0:T(8,128)}, u32[]{:S(2)}) copy-start(f32[25,640]{1,0:T(8,128)} %param.17) | copy-start | bytes 192004
  11.3 34.6 %copy-start.12 = (f32[25,640]{1,0:T(8,128)S(1)}, f32[25,640]{1,0:T(8,128)}, u32[]{:S(2)}) copy-start(f32[25,640]{1,0:T(8,128)} %param.18) | copy-start | bytes 192004
  31.5 14.8 %copy-start.7 = (f32[40,384]{1,0:T(8,128)S(1)}, f32[40,384]{1,0:T(8,128)}, u32[]{:S(2)}) copy-start(f32[40,384]{1,0:T(8,128)} %constant.62.clone.lanes_ref) | copy-start | bytes 184324
  31.5 30.5 %all-to-all-start.1 = ((f32[32,1,3840]{2,1,0:T(1,128)}), f32[32,1,3840]{2,1,0:T(1,128)S(1)}, u32[]{:S(2)}, u32[]{:S(2)}) async-start(f32[32,1,3840]{2,1,0:T(1,128)} %bitcast.5), calls=%async_computation.1 | async-start | bytes 983040 | tf_op jit(solution)/shard_map/all_to_all | solution.py:558
  62.1 17.8 %copy-start.6 = (f32[32,512]{1,0:T(8,128)S(1)}, f32[32,512]{1,0:T(8,128)}, u32[]{:S(2)}) copy-start(f32[32,512]{1,0:T(8,128)} %constant.63.clone.wave_ref) | copy-start | bytes 196612
  65.9 22.4 %copy-start.2 = (bf16[2,512,256]{2,1,0:T(8,128)(2,1)S(1)}, bf16[2,512,256]{2,1,0:T(8,128)(2,1)}, u32[]{:S(2)}) copy-start(bf16[2,512,256]{2,1,0:T(8,128)(2,1)} %constant.65.clone.low_ref) | copy-start | bytes 1572868
  65.9 22.4 %copy-start.3 = (bf16[2,512,256]{2,1,0:T(8,128)(2,1)S(1)}, bf16[2,512,256]{2,1,0:T(8,128)(2,1)}, u32[]{:S(2)}) copy-start(bf16[2,512,256]{2,1,0:T(8,128)(2,1)} %constant.64.clone.high_ref) | copy-start | bytes 1572868
  66.0 22.3 %all-to-all-start.2 = ((f32[32,1,3840]{2,1,0:T(1,128)}), f32[32,1,3840]{2,1,0:T(1,128)S(1)}, u32[]{:S(2)}, u32[]{:S(2)}) async-start(f32[32,1,3840]{2,1,0:T(1,128)} %bitcast.11), calls=%async_computation.2 | async-start | bytes 983040 | tf_op jit(solution)/shard_map/all_to_all | solution.py:558
  71.1 7.1 %collective-permute-start = (f32[96,128]{1,0:T(8,128)S(1)}, f32[96,128]{1,0:T(8,128)S(1)}, u32[]{:S(2)}, u32[]{:S(2)}) collective-permute-start(f32[96,128]{1,0:T(8,128)S(1)} %get-tuple-element.34), channel_id=1, source_target_pairs={{0,16},{16,32},{32,48},{48,64},{64,80},{80,96},{96,112},{112,128},... | collective-permute-start | bytes 147464 | tf_op jit(solution)/shard_map/ppermute | solution.py:614
  73.1 6.8 %collective-permute-start.1 = (f32[96,128]{1,0:T(8,128)S(1)}, f32[96,128]{1,0:T(8,128)S(1)}, u32[]{:S(2)}, u32[]{:S(2)}) collective-permute-start(f32[96,128]{1,0:T(8,128)S(1)} %get-tuple-element.35), channel_id=1, source_target_pairs={{16,0},{32,16},{48,32},{64,48},{80,64},{96,80},{112,96},{128,112},... | collective-permute-start | bytes 147464 | tf_op jit(solution)/shard_map/ppermute | solution.py:615
  88.3 22.3 %copy-start = (bf16[640,1280]{1,0:T(8,128)(2,1)S(1)}, bf16[640,1280]{1,0:T(8,128)(2,1)}, u32[]{:S(2)}) copy-start(bf16[640,1280]{1,0:T(8,128)(2,1)} %up_ref.1) | copy-start | bytes 4915204
  88.3 22.3 %copy-start.1 = (bf16[1280,640]{1,0:T(8,128)(2,1)S(1)}, bf16[1280,640]{1,0:T(8,128)(2,1)}, u32[]{:S(2)}) copy-start(bf16[1280,640]{1,0:T(8,128)(2,1)} %down_ref.1) | copy-start | bytes 4915204
  88.3 22.3 %copy-start.9 = (f32[640]{0:T(1024)S(1)}, f32[640]{0:T(1024)}, u32[]{:S(2)}) copy-start(f32[640]{0:T(1024)} %gain_ref.1) | copy-start | bytes 7684

commit v5 on v4

--- a/solution.py
+++ b/solution.py
@@ -117,17 +117,18 @@
 
 
 def dot3(a, b, dims=((1,), (0,))):
-    return dot(a[0], b[0], dims) + (dot(a[1], b[0], dims) + dot(a[0], b[1], dims))
-
-
-def pack_kernel(x_hbm, out_hbm, x_ref, out_ref, arrivals, sent):
+    rows = a[0].shape[0]
+    both = dot(jnp.concatenate(a, axis=0), b[0], dims)
+    return both[:rows] + (both[rows:] + dot(a[0], b[1], dims))
+
+
+def pack_kernel(x_hbm, out_ref, x_ref, arrivals):
     first = lane_slot(8) % 2 == 0
     fetches = []
     for j in range(5):
         lanes = pl.ds(128 * j, 128)
         fetches.append(pltpu.make_async_copy(x_hbm.at[:, :, lanes], x_ref.at[:, :, lanes], arrivals.at[j]))
         fetches[j].start()
-    stores = []
     for j in range(5):
         fetches[j].wait()
         blocks = swap_blocks([x_ref[:, i, 128 * j : 128 * j + 128] for i in range(ROWS)], 16)
@@ -142,15 +143,9 @@
             else:
                 base = (even, even + 28, None, odd, odd + 28)[place]
                 out_ref[base : base + 28] = block
-            if place == 4 and pair % 2:
-                rows = pl.ds(even - 2 * LON_CHUNK, 4 * LON_CHUNK)
-                stores.append(pltpu.make_async_copy(out_ref.at[rows], out_hbm.at[rows], sent.at[pair // 2]))
-                stores[-1].start()
-    for store in stores:
-        store.wait()
-
-
-def forward_kernel(in_ref, high_ref, low_ref, out_ref, local_ref, up_ref, down_ref):
+
+
+def forward_kernel(in_ref, high_ref, low_ref, out_ref, local_ref):
     totals = []
     for half in range(2):
         pieces = []
@@ -179,27 +174,25 @@
             out_ref[pl.ds(2 * OWN + row, LAT, stride=LAT_CHUNK), :] = part[:, 128:]
     for k in range(OWN):
         out_ref[pl.ds(4 * OWN + k, LAT, stride=LAT_CHUNK), :] = last[LAT * k : LAT * k + LAT]
-    left = lane_slot(64) == 0
     for r in range(2):
-        part = both[LAT * (KEPT * r + OWN) : LAT * (KEPT * r + OWN) + LAT]
-        a, b = part[:, :128], part[:, 128:]
         rows = slice(LAT * r, LAT * r + LAT)
-        local_ref[rows, :128] = a
-        local_ref[rows, 128:256] = b
-        up_ref[rows] = jnp.where(left, pltpu.roll(a, 64, 1), b)
-        down_ref[rows] = jnp.where(left, a, pltpu.roll(b, 64, 1))
-    part = last[LAT * OWN : LAT * OWN + LAT]
-    local_ref[0:LAT, 256:] = part
+        local_ref[rows, :256] = both[LAT * (KEPT * r + OWN) : LAT * (KEPT * r + OWN) + LAT]
+    local_ref[0:LAT, 256:] = last[LAT * OWN : LAT * OWN + LAT]
     local_ref[LAT:, 256:] = jnp.zeros((LAT, 128), f32)
-    up_ref[2 * LAT :] = part
-    down_ref[2 * LAT :] = part
-
-
-def local_kernel(band_ref, own_ref, below_ref, above_ref, taps_ref, wave_ref, out_ref):
+
+
+def local_kernel(place_ref, own_ref, below_ref, above_ref, first_ref, second_ref, wave_ref, out_ref, taps_ref):
+    shape = (CHANNELS, 384)
+    at = lax.broadcasted_iota(jnp.int32, shape, 1)
+    tail = at % 8 + 32
+    at = jnp.where(at >= 256, tail, at // 128 * 16 + at % 16)
+    chosen = (lax.broadcasted_iota(jnp.int32, shape, 0) == channel_at(place_ref, at)).astype(f32)
+    taps_ref[0:25] = pick(first_ref[...], chosen, ((1,), (0,)))
+    taps_ref[32:57] = pick(second_ref[...], chosen, ((1,), (0,)))
     lane = lax.broadcasted_iota(jnp.int32, (1, 128), 1)
     left = lane < 64
-    south = jnp.where(band_ref[0] == 0, 0.0, 1.0)
-    north = jnp.where(band_ref[0] == LAT - 1, 0.0, 1.0)
+    south = jnp.where(place_ref[0] == 0, 0.0, 1.0)
+    north = jnp.where(place_ref[0] == LAT - 1, 0.0, 1.0)
     masks = (jnp.where(left, south, 1.0), jnp.where(left, 1.0, north))
 
     def extend(own, below, above):
@@ -221,7 +214,7 @@
         return jnp.where(keep, first, second), jnp.where(keep, second, first)
 
     def weights(which, a, tile):
-        rows = [taps_ref[(which * 5 + a) * 5 + b : (which * 5 + a) * 5 + b + 1, 128 * tile : 128 * tile + 128] for b in range(5)]
+        rows = [taps_ref[32 * which + 5 * a + b : 32 * which + 5 * a + b + 1, 128 * tile : 128 * tile + 128] for b in range(5)]
         cos1, cos2, sin1, sin2 = (wave_ref[:, 128 * n : 128 * n + 128] for n in range(4))
         real = rows[2] + (rows[3] + rows[1]) * cos1 + (rows[4] + rows[0]) * cos2
         imag = (rows[3] - rows[1]) * sin1 + (rows[4] - rows[0]) * sin2
@@ -265,17 +258,38 @@
     out_ref[LAT:, 256:] = jnp.zeros((LAT, 128), f32)
 
 
-def taps_kernel(rows_ref, phase_ref, plain_ref, lanes_ref, taps_ref, spread_ref):
-    spread_ref[...] = jnp.dot(plain_ref[...], lanes_ref[...], precision=lax.Precision.HIGHEST)
+def channel_at(place_ref, local):
+    turned = jnp.where(local >= 32, local - 32, local + 8)
+    return place_ref[2] * SLICE + jnp.where(place_ref[1] == 1, turned, local)
+
+
+def pick(a, b, dims):
+    return lax.dot_general(a, b, (dims, ((), ())), precision=lax.Precision.HIGHEST, preferred_element_type=f32)
+
+
+def taps_kernel(place_ref, first_ref, second_ref, phase_ref, local_ref, taps_ref, up_ref, down_ref):
+    left = lane_slot(64) == 0
+    a, b = local_ref[:, :128], local_ref[:, 128:256]
+    up_ref[: 2 * LAT] = jnp.where(left, pltpu.roll(a, 64, 1), b)
+    down_ref[: 2 * LAT] = jnp.where(left, a, pltpu.roll(b, 64, 1))
+    up_ref[2 * LAT :] = local_ref[:LAT, 256:]
+    down_ref[2 * LAT :] = local_ref[:LAT, 256:]
+    shape = (SLICE, CHANNELS)
+    wanted = channel_at(place_ref, lax.broadcasted_iota(jnp.int32, shape, 0))
+    chosen = (lax.broadcasted_iota(jnp.int32, shape, 1) == wanted).astype(f32)
+    rows = [pick(chosen, ref[...], ((1,), (1,))) for ref in (first_ref, second_ref)]
     for tile in range(5):
         phase = phase_ref[:, 4 * tile : 4 * tile + 1]
         for n in range(1, 4):
             column = phase_ref[:, 4 * tile + n : 4 * tile + n + 1]
             phase = jnp.where(lane_slot(LAT) >= n, column, phase)
-        total = rows_ref[:, 0:1] * phase[0:1]
-        for b in range(1, 5):
-            total = total + rows_ref[:, b : b + 1] * phase[b : b + 1]
-        taps_ref[:, 128 * tile : 128 * tile + 128] = total
+        for which in range(2):
+            for a in range(5):
+                total = rows[which][:, 5 * a : 5 * a + 1] * phase[0:1]
+                for b in range(1, 5):
+                    total = total + rows[which][:, 5 * a + b : 5 * a + b + 1] * phase[b : b + 1]
+                base = (5 * which + a) * SLICE
+                taps_ref[base : base + SLICE, 128 * tile : 128 * tile + 128] = total
 
 
 def legendre_kernel(owner_ref, angle_ref, seed_ref, high_ref, low_ref, left_ref, right_ref):
@@ -310,7 +324,7 @@
             high_ref[k, :, 128 * part : 128 * part + 128] = high
             low_ref[k, :, 128 * part : 128 * part + 128] = low
 
-def spectral_kernel(in_ref, high_ref, low_ref, taps_ref, gain_ref, angle_ref, out_ref, u_ref, v_ref, f_ref):
+def spectral_kernel(place_ref, in_ref, high_ref, low_ref, taps_ref, gain_ref, angle_ref, out_ref, u_ref, v_ref, f_ref):
     lane = lax.broadcasted_iota(jnp.int32, (1, 128), 1) % LAT
 
     def fill_edges(ref):
@@ -382,11 +396,13 @@
                     f_ref[4 * group + n, SLICE * part : SLICE * part + SLICE] = (
                         jnp.concatenate([halves[0][n], halves[1][n]], axis=1) * weight
                     )
+    gain = gain_ref[...]
+    gain = jnp.where(place_ref[1] == 1, jnp.concatenate([gain[8:], gain[:8]], axis=0), gain)
     for k in range(OWN):
         table = (high_ref[k], low_ref[k])
         spectrum = dot3(split(f_ref[k]), table, ((1,), (1,)))
-        gain = gain_ref[80:160] if k == 0 else gain_ref[0:80]
-        f_ref[k] = dot3(split(spectrum * gain), table)
+        second = jnp.where(place_ref[0] == 0, 0.0, gain) if k == 0 else gain
+        f_ref[k] = dot3(split(spectrum * jnp.concatenate([gain, second], axis=0)), table)
     for part in range(2):
         for group in range(2):
             rows = slice(SLICE * part, SLICE * part + SLICE)
@@ -524,32 +540,10 @@
     )(*operands)
 
 
-def factors(*operands):
-    return pl.pallas_call(
-        taps_kernel,
-        out_shape=tuple(jax.ShapeDtypeStruct(shape, f32) for shape in ((10 * SLICE, 640), (50, 384))),
-        in_specs=vmem(4),
-        out_specs=vmem(2),
-        compiler_params=pltpu.CompilerParams(vmem_limit_bytes=16 << 20),
-        cost_estimate=pl.CostEstimate(flops=10**7, bytes_accessed=10**7, transcendentals=0),
-    )(*operands)
-
-
-def own_channels(array, axis, start, odd):
-    part = lax.dynamic_slice_in_dim(array, start, SLICE, axis)
-    return jnp.where(odd, jnp.roll(part, -8, axis), part)
-
-
 def wave_np():
     angle = 2.0 * np.pi * (MODES + np.arange(LAT)) / NLON
     waves = [np.cos(angle), np.cos(2.0 * angle), np.sin(angle), np.sin(2.0 * angle)]
     return np.repeat(np.stack(waves, axis=1), 128, axis=1).astype(np.float32)
-
-
-def lanes_np():
-    lane = np.arange(128)
-    channel = np.concatenate([lane % 16, 16 + lane % 16, 32 + lane % 8])
-    return (np.arange(SLICE)[:, None] == channel[None, :]).astype(np.float32)
 
 
 def exchange(array, axis, count):
@@ -573,67 +567,61 @@
         latent.transpose(1, 0, 2),
         scratch=[
             pltpu.VMEM((COLS, ROWS, CHANNELS), f32),
-            pltpu.VMEM((LON * LON_CHUNK, 128), f32),
             pltpu.SemaphoreType.DMA((5,)),
-            pltpu.SemaphoreType.DMA((4,)),
         ],
         far=1,
-        grant=60,
-        out=pltpu.HBM,
+        grant=53,
     )
     circles = exchange(packed, "lon", LON)
 
+    shapes = ((LAT * LAT_CHUNK, 128), (2 * LAT, 384))
+    coeffs, local = pl.pallas_call(
+        forward_kernel,
+        out_shape=tuple(jax.ShapeDtypeStruct(shape, f32) for shape in shapes),
+        in_specs=vmem(3),
+        out_specs=vmem(2),
+        compiler_params=pltpu.CompilerParams(vmem_limit_bytes=24 << 20),
+    )(circles, *map(jnp.asarray, forward))
+    orders = exchange(coeffs, "lat", LAT)
+    local, conv_first, conv_second, band = lax.optimization_barrier(
+        (local, conv_first, conv_second, band)
+    )
     seeds = lax.dynamic_index_in_dim(jnp.asarray(seed_np()), band, 0, False)
     owner = band.astype(jnp.int32).reshape(1)
     high, low = legendre(owner, angles, seeds)
-    gains = own_channels(filter_gains, 1, 0, odd).T
-    gains = jnp.concatenate([gains, gains, gains, jnp.where(band == 0, 0.0, gains)], axis=0)
-
-    circles, high, low = lax.optimization_barrier((circles, high, low))
-
-    shapes = ((LAT * LAT_CHUNK, 128), (2 * LAT, 384), (3 * LAT, 128), (3 * LAT, 128))
-    coeffs, local, up, down = pl.pallas_call(
-        forward_kernel,
+    phases = lax.dynamic_index_in_dim(jnp.asarray(phase_np()), band, 0, False)
+    place = jnp.stack([band, odd, sector]).astype(jnp.int32)
+    shapes = ((10 * SLICE, 640), (3 * LAT, 128), (3 * LAT, 128))
+    taps, up, down = pl.pallas_call(
+        taps_kernel,
         out_shape=tuple(jax.ShapeDtypeStruct(shape, f32) for shape in shapes),
-        in_specs=vmem(3),
-        out_specs=vmem(4),
-        compiler_params=pltpu.CompilerParams(vmem_limit_bytes=24 << 20),
-    )(circles, *map(jnp.asarray, forward))
-    orders = exchange(coeffs, "lat", LAT)
-    local, conv_first, conv_second = lax.optimization_barrier((local, conv_first, conv_second))
-    phases = lax.dynamic_index_in_dim(jnp.asarray(phase_np()), band, 0, False)
-    own_taps = jnp.stack([conv_first, conv_second]).reshape(2, 5, 5, CHANNELS)
-    own_taps = own_channels(own_taps, 3, sector * SLICE, odd)
-    taps, lane_taps = factors(
-        own_taps.transpose(0, 1, 3, 2).reshape(10 * SLICE, 5),
-        phases,
-        own_taps.reshape(50, SLICE),
-        jnp.asarray(lanes_np()),
-    )
+        in_specs=[pl.BlockSpec(memory_space=pltpu.SMEM)] + vmem(4),
+        out_specs=vmem(3),
+        compiler_params=pltpu.CompilerParams(vmem_limit_bytes=16 << 20),
+        cost_estimate=pl.CostEstimate(flops=10**7, bytes_accessed=10**7, transcendentals=0),
+    )(place, conv_first, conv_second, phases, local)
     rising = [(n, n + 1) for n in range(LAT - 1)]
     below = lax.ppermute(up, "lat", rising)
     above = lax.ppermute(down, "lat", [(target, source) for source, target in rising])
     stay = pl.pallas_call(
         local_kernel,
         out_shape=jax.ShapeDtypeStruct((2 * LAT, 384), f32),
-        in_specs=[pl.BlockSpec(memory_space=pltpu.SMEM)] + vmem(5),
+        in_specs=[pl.BlockSpec(memory_space=pltpu.SMEM)] + vmem(6),
         out_specs=vmem(1)[0],
+        scratch_shapes=[pltpu.VMEM((64, 384), f32)],
         compiler_params=pltpu.CompilerParams(vmem_limit_bytes=16 << 20),
         cost_estimate=pl.CostEstimate(flops=10**7, bytes_accessed=10**6, transcendentals=0),
-    )(owner, local, below, above, lane_taps, jnp.asarray(wave_np()))
-    orders, taps = lax.optimization_barrier((orders, taps))
+    )(place, local, below, above, conv_first, conv_second, jnp.asarray(wave_np()))
+    orders, taps, high, low = lax.optimization_barrier((orders, taps, high, low))
     state = pltpu.VMEM((2, 2, 12, SLICE, 128), f32)
-    third = run(
+    third = pl.pallas_call(
         spectral_kernel,
-        (LAT * LAT_CHUNK, 128),
-        orders,
-        high,
-        low,
-        taps,
-        gains,
-        angles,
-        scratch=[state, state, pltpu.VMEM((OWN, 2 * SLICE, NLAT), f32)],
-    )
+        out_shape=jax.ShapeDtypeStruct((LAT * LAT_CHUNK, 128), f32),
+        in_specs=[pl.BlockSpec(memory_space=pltpu.SMEM)] + vmem(6),
+        out_specs=vmem(1)[0],
+        scratch_shapes=[state, state, pltpu.VMEM((OWN, 2 * SLICE, NLAT), f32)],
+        compiler_params=pltpu.CompilerParams(vmem_limit_bytes=24 << 20),
+    )(place, orders, high, low, taps, filter_gains.T, angles)
     returned = exchange(third, "lat", LAT)
     restored = run(inverse_kernel, (LON * LON_CHUNK, 128), returned, stay, *map(jnp.asarray, inverse))
     arrived = exchange(restored, "lon", LON)

time: 114 us -> 115 us (level)
  blocking collectives: 21.3 us -> 48.6 us
  waiting for transfers between devices: 40 us -> 19.2 us
  starting transfers between devices: 33.7 us -> 25.6 us
  local copies, waits for them, and re-layouts: 1.75 us -> 4.81 us
    all_to_all x1 -> x2, blocking collectives: 21.3 us -> 48.6 us  [exchange(): lax.all_to_all(array.reshape(shape), axis, split_axis=0, concat_axis=0, t...]
    all_to_all x3 -> x2, waiting for transfers between devices: 38.3 us -> 17.1 us  [exchange(): lax.all_to_all(array.reshape(shape), axis, split_axis=0, concat_axis=0, t...]
    all_to_all x3 -> x2, starting transfers between devices: 26.7 us -> 18.6 us  [exchange(): lax.all_to_all(array.reshape(shape), axis, split_axis=0, concat_axis=0, t...]
    pallas_call x4 -> x3, Pallas kernels: 10.9 us -> 6.27 us  [run(): pl.pallas_call(kernel, out_shape=jax.ShapeDtypeStruct(shape, f32), in_spe...]
    pallas_call x1 -> x2, Pallas kernels: 1.51 us -> 5.55 us  [the longest x1 3.96 us: per_device(): pl.pallas_call(spectral_kernel, out_shape=jax.ShapeDtypeStruct((LAT * LAT...]
    unnamed x26 -> x34, local copies, waits for them, and re-layouts: 0.06 us -> 3.42 us
  transfers between devices with their start and end apart: 5 -> 4, of which waited for: 4 -> 4; matrix products, arithmetic and copies ran while one was open for 2% -> 1% of each run, Pallas kernels for 3% -> 4%
where the time goes in v5:
time: 115 us
  blocking collectives  48.6 us (42%)
  starting transfers between devices  25.6 us (22%)
  waiting for transfers between devices  19.2 us (17%)
  Pallas kernels  16.4 us (14%)
  local copies, waits for them, and re-layouts  4.81 us (4%)
    all_to_all x2, blocking collectives, exchange(): lax.all_to_all(array.reshape(shape), axis, split_axis=0, concat_axis=0, t...  48.6 us
    all_to_all x2, starting transfers between devices, exchange(): lax.all_to_all(array.reshape(shape), axis, split_axis=0, concat_axis=0, t...  18.6 us
    all_to_all x2, waiting for transfers between devices, exchange(): lax.all_to_all(array.reshape(shape), axis, split_axis=0, concat_axis=0, t...  17.1 us
    pallas_call x3, Pallas kernels, run(): pl.pallas_call(kernel, out_shape=jax.ShapeDtypeStruct(shape, f32), in_spe...  6.27 us
    ppermute x1, starting transfers between devices, per_device(): lax.ppermute(down, 'lat', [(target, source) for source, target in rising])  5.04 us
    pallas_call x1, Pallas kernels, per_device(): pl.pallas_call(spectral_kernel, out_shape=jax.ShapeDtypeStruct((LAT * LAT...  3.96 us
    unnamed x34, local copies, waits for them, and re-layouts  3.42 us
  transfers between devices with their start and end apart: 4, of which 4 were waited for; matrix products, arithmetic and copies ran while one was open for 1% of the time, Pallas kernels for 4%

profile of v5, /device:TPU:4, one launch (start us, length us, event | category | flops | bytes accessed | tf_op | source)
XLA Modules:
  0.0 114.8 jit_solution(8609150928899435801)
XLA Ops:
  0.0 2.5 %shard_map.145 = f32[1120,128]{1,0:T(8,128)S(1)} custom-call(f32[28,8,640]{2,1,0:T(8,128)} %bitcast.25), custom_call_target="tpu_custom_call" | custom-call | tf_op jit(solution)/shard_map/pallas_call | solution.py:519
  2.6 27.0 %all_to_all.20 = f32[16,1,8960]{2,1,0:T(1,128)S(1)} all-to-all(f32[16,1,8960]{2,1,0:T(1,128)S(1)} %bitcast.21), channel_id=1, replica_groups=mesh['lat'=32,'lon'=16] {'lon'}, dimensions={0} | all-to-all | bytes 1146880 | tf_op jit(solution)/shard_map/all_to_all | solution.py:552
  29.6 1.7 %shard_map.146 = (f32[960,128]{1,0:T(8,128)}, f32[64,384]{1,0:T(8,128)S(1)}) custom-call(f32[1120,128]{1,0:T(8,128)S(1)} %bitcast.20, bf16[448,512]{1,0:T(8,128)(2,1)S(1)} %copy-done.5, bf16[448,512]{1,0:T(8,128)(2,1)S(1)} %copy-done.4), custom_call_target="tpu_custom_call" | custom-call | tf_op jit(solution)/shard_map/pallas_call | solution.py:578
  31.3 13.4 %all-to-all-start.1 = ((f32[32,1,3840]{2,1,0:T(1,128)}), f32[32,1,3840]{2,1,0:T(1,128)S(1)}, u32[]{:S(2)}, u32[]{:S(2)}) async-start(f32[32,1,3840]{2,1,0:T(1,128)} %bitcast.6), calls=%async_computation.1 | async-start | bytes 983040 | tf_op jit(solution)/shard_map/all_to_all | solution.py:552
  44.7 0.7 dynamic-slice_bitcast_fusion.seed_ref
  45.4 0.9 shard_map.148
  46.4 0.7 dynamic-slice_bitcast_fusion.1.phase_ref
  47.1 1.6 %shard_map.147 = (f32[400,640]{1,0:T(8,128)S(1)}, f32[96,128]{1,0:T(8,128)S(1)}, f32[96,128]{1,0:T(8,128)S(1)}) custom-call(s32[3]{0:T(128)S(1)} %pad_add_fusion.place_ref, f32[25,640]{1,0:T(8,128)S(1)} %copy-done.6, f32[25,640]{1,0:T(8,128)S(1)} %copy-done.7, f32[8,20]{1,0:T(8,128)S(1)} %dynamic-slice_bitcast_fusion.1.phase_ref, ...), custom_call_target="tpu_custom_call" | custom-call | flops 10000000 | bytes 10000000 | tf_op jit(solution)/shard_map/pallas_call | solution.py:595
  48.7 0.6 copy-done.15
  49.3 0.6 copy-done.16
  50.0 11.7 %all-to-all-done.1 = f32[32,1,3840]{2,1,0:T(1,128)S(1)} async-done(((f32[32,1,3840]{2,1,0:T(1,128)}), f32[32,1,3840]{2,1,0:T(1,128)S(1)}, u32[]{:S(2)}, u32[]{:S(2)}) %all-to-all-start.1) | async-done | bytes 491552 | tf_op jit(solution)/shard_map/all_to_all | solution.py:552
  61.7 0.8 copy-done.9
  62.5 0.7 copy-done.12
  63.2 4.0 %shard_map.149 = f32[960,128]{1,0:T(8,128)} custom-call(s32[3]{0:T(128)S(1)} %copy-done.12, f32[960,128]{1,0:T(8,128)S(1)} %bitcast.22, bf16[6,192,256]{2,1,0:T(8,128)(2,1)S(1)} %get-tuple-element.30.high_ref, bf16[6,192,256]{2,1,0:T(8,128)(2,1)S(1)} %get-tuple-element.31.low_ref, f32[400,640]{1,0:T(8,128)S(1)} %get-tuple-element.32.taps_ref, ...), custom_call_target="tpu_custom_call" | custom-call | tf_op jit(solution)/shard_map/pallas_call | solution.py:617
  67.1 5.1 %all-to-all-start.2 = ((f32[32,1,3840]{2,1,0:T(1,128)}), f32[32,1,3840]{2,1,0:T(1,128)S(1)}, u32[]{:S(2)}, u32[]{:S(2)}) async-start(f32[32,1,3840]{2,1,0:T(1,128)} %bitcast.11), calls=%async_computation.2 | async-start | bytes 983040 | tf_op jit(solution)/shard_map/all_to_all | solution.py:552
  72.3 2.0 %collective-permute-start = (f32[96,128]{1,0:T(8,128)}, f32[96,128]{1,0:T(8,128)S(1)}, u32[]{:S(2)}, u32[]{:S(2)}) collective-permute-start(f32[96,128]{1,0:T(8,128)} %copy-done.16), channel_id=1, source_target_pairs={{0,16},{16,32},{32,48},{48,64},{64,80},{80,96},{96,112},{112,128},... | collective-permute-start | bytes 147464 | tf_op jit(solution)/shard_map/ppermute | solution.py:604
  74.3 5.0 %collective-permute-start.1 = (f32[96,128]{1,0:T(8,128)}, f32[96,128]{1,0:T(8,128)S(1)}, u32[]{:S(2)}, u32[]{:S(2)}) collective-permute-start(f32[96,128]{1,0:T(8,128)} %copy-done.15), channel_id=1, source_target_pairs={{16,0},{32,16},{48,32},{64,48},{80,64},{96,80},{112,96},{128,112},... | collective-permute-start | bytes 147464 | tf_op jit(solution)/shard_map/ppermute | solution.py:605
  79.5 1.9 %collective-permute-done.1.above_ref = f32[96,128]{1,0:T(8,128)S(1)} collective-permute-done((f32[96,128]{1,0:T(8,128)}, f32[96,128]{1,0:T(8,128)S(1)}, u32[]{:S(2)}, u32[]{:S(2)}) %collective-permute-start.1) | collective-permute-done | bytes 49184 | tf_op jit(solution)/shard_map/ppermute | solution.py:605
  81.4 0.7 copy-done.13
  82.1 2.0 %shard_map.150.local_ref = f32[64,384]{1,0:T(8,128)S(1)} custom-call(s32[3]{0:T(128)S(1)} %copy-done.13, f32[64,384]{1,0:T(8,128)S(1)} %get-tuple-element.25.local_ref.own_ref, f32[96,128]{1,0:T(8,128)S(1)} %collective-permute-done.below_ref, f32[96,128]{1,0:T(8,128)S(1)} %collective-permute-done.1.above_ref, f32[25,640]{1,0:T(8,128)S(1)} %copy-done.6, ...), custom_call_target="tpu_custom_call" | custom-call | flops 10000000 | bytes 1000000 | tf_op jit(solution)/shard_map/pallas_call | solution.py:606
  84.1 5.4 %all-to-all-done.2 = f32[32,1,3840]{2,1,0:T(1,128)S(1)} async-done(((f32[32,1,3840]{2,1,0:T(1,128)}), f32[32,1,3840]{2,1,0:T(1,128)S(1)}, u32[]{:S(2)}, u32[]{:S(2)}) %all-to-all-start.2) | async-done | bytes 491552 | tf_op jit(solution)/shard_map/all_to_all | solution.py:552
  89.5 1.0 shard_map.151
  90.5 21.6 %all_to_all.21 = f32[16,1,8960]{2,1,0:T(1,128)S(1)} all-to-all(f32[16,1,8960]{2,1,0:T(1,128)S(1)} %bitcast.19), channel_id=1, replica_groups=mesh['lat'=32,'lon'=16] {'lon'}, dimensions={0} | all-to-all | bytes 1146880 | tf_op jit(solution)/shard_map/all_to_all | solution.py:552
  112.1 2.7 %shard_map.152 = f32[28,8,640]{2,1,0:T(8,128)} custom-call(f32[1120,128]{1,0:T(8,128)S(1)} %bitcast.18, f32[640]{0:T(1024)S(1)} %copy-done.14, bf16[640,1280]{1,0:T(8,128)(2,1)S(1)} %copy-done, bf16[1280,640]{1,0:T(8,128)(2,1)S(1)} %copy-done.1), custom_call_target="tpu_custom_call" | custom-call | tf_op jit(solution)/shard_map/pallas_call | solution.py:519
  (31 shorter events, 0.3 us)
Async XLA Ops:
  0.0 29.6 %copy-start.4 = (bf16[448,512]{1,0:T(8,128)(2,1)S(1)}, bf16[448,512]{1,0:T(8,128)(2,1)}, u32[]{:S(2)}) copy-start(bf16[448,512]{1,0:T(8,128)(2,1)} %constant.50.clone.low_ref) | copy-start | bytes 1376260
  0.0 29.6 %copy-start.5 = (bf16[448,512]{1,0:T(8,128)(2,1)S(1)}, bf16[448,512]{1,0:T(8,128)(2,1)}, u32[]{:S(2)}) copy-start(bf16[448,512]{1,0:T(8,128)(2,1)} %constant.49.clone.high_ref) | copy-start | bytes 1376260
  2.6 42.9 %copy-start.10 = (f32[8,256]{1,0:T(8,128)S(1)}, f32[8,256]{1,0:T(8,128)}, u32[]{:S(2)}) copy-start(f32[8,256]{1,0:T(8,128)} %constant.48.clone.angle_ref) | copy-start | bytes 24580
  2.6 44.6 %copy-start.6 = (f32[25,640]{1,0:T(8,128)S(1)}, f32[25,640]{1,0:T(8,128)}, u32[]{:S(2)}) copy-start(f32[25,640]{1,0:T(8,128)} %first_ref.1) | copy-start | bytes 192004
  2.6 44.5 %copy-start.7 = (f32[25,640]{1,0:T(8,128)S(1)}, f32[25,640]{1,0:T(8,128)}, u32[]{:S(2)}) copy-start(f32[25,640]{1,0:T(8,128)} %second_ref.1) | copy-start | bytes 192004
  31.3 30.4 %all-to-all-start.1 = ((f32[32,1,3840]{2,1,0:T(1,128)}), f32[32,1,3840]{2,1,0:T(1,128)S(1)}, u32[]{:S(2)}, u32[]{:S(2)}) async-start(f32[32,1,3840]{2,1,0:T(1,128)} %bitcast.6), calls=%async_computation.1 | async-start | bytes 983040 | tf_op jit(solution)/shard_map/all_to_all | solution.py:552
  46.4 15.3 %copy-start.11 = (s32[3]{0:T(128)}, s32[3]{0:T(128)S(1)}, u32[]{:S(2)}) copy-start(s32[3]{0:T(128)S(1)} %pad_add_fusion.place_ref) | copy-start | bytes 40
  48.7 0.6 copy-start.15
  49.3 0.6 copy-start.16
  61.7 0.8 copy-start.9
  62.5 0.7 copy-start.12
  63.2 18.2 %copy-start.8 = (f32[32,512]{1,0:T(8,128)S(1)}, f32[32,512]{1,0:T(8,128)}, u32[]{:S(2)}) copy-start(f32[32,512]{1,0:T(8,128)} %constant.53.clone.wave_ref) | copy-start | bytes 196612
  63.2 26.3 %copy-start.2 = (bf16[2,512,256]{2,1,0:T(8,128)(2,1)S(1)}, bf16[2,512,256]{2,1,0:T(8,128)(2,1)}, u32[]{:S(2)}) copy-start(bf16[2,512,256]{2,1,0:T(8,128)(2,1)} %constant.55.clone.low_ref) | copy-start | bytes 1572868
  67.1 22.4 %copy-start.3 = (bf16[2,512,256]{2,1,0:T(8,128)(2,1)S(1)}, bf16[2,512,256]{2,1,0:T(8,128)(2,1)}, u32[]{:S(2)}) copy-start(bf16[2,512,256]{2,1,0:T(8,128)(2,1)} %constant.54.clone.high_ref) | copy-start | bytes 1572868
  67.1 22.3 %all-to-all-start.2 = ((f32[32,1,3840]{2,1,0:T(1,128)}), f32[32,1,3840]{2,1,0:T(1,128)S(1)}, u32[]{:S(2)}, u32[]{:S(2)}) async-start(f32[32,1,3840]{2,1,0:T(1,128)} %bitcast.11), calls=%async_computation.2 | async-start | bytes 983040 | tf_op jit(solution)/shard_map/all_to_all | solution.py:552
  72.3 7.2 %collective-permute-start = (f32[96,128]{1,0:T(8,128)}, f32[96,128]{1,0:T(8,128)S(1)}, u32[]{:S(2)}, u32[]{:S(2)}) collective-permute-start(f32[96,128]{1,0:T(8,128)} %copy-done.16), channel_id=1, source_target_pairs={{0,16},{16,32},{32,48},{48,64},{64,80},{80,96},{96,112},{112,128},... | collective-permute-start | bytes 147464 | tf_op jit(solution)/shard_map/ppermute | solution.py:604
  74.3 7.1 %collective-permute-start.1 = (f32[96,128]{1,0:T(8,128)}, f32[96,128]{1,0:T(8,128)S(1)}, u32[]{:S(2)}, u32[]{:S(2)}) collective-permute-start(f32[96,128]{1,0:T(8,128)} %copy-done.15), channel_id=1, source_target_pairs={{16,0},{32,16},{48,32},{64,48},{80,64},{96,80},{112,96},{128,112},... | collective-permute-start | bytes 147464 | tf_op jit(solution)/shard_map/ppermute | solution.py:605
  81.4 0.7 copy-start.13
  89.5 22.6 %copy-start = (bf16[640,1280]{1,0:T(8,128)(2,1)S(1)}, bf16[640,1280]{1,0:T(8,128)(2,1)}, u32[]{:S(2)}) copy-start(bf16[640,1280]{1,0:T(8,128)(2,1)} %up_ref.1) | copy-start | bytes 4915204
  89.5 22.6 %copy-start.1 = (bf16[1280,640]{1,0:T(8,128)(2,1)S(1)}, bf16[1280,640]{1,0:T(8,128)(2,1)}, u32[]{:S(2)}) copy-start(bf16[1280,640]{1,0:T(8,128)(2,1)} %down_ref.1) | copy-start | bytes 4915204
  89.5 22.6 %copy-start.14 = (f32[640]{0:T(1024)S(1)}, f32[640]{0:T(1024)}, u32[]{:S(2)}) copy-start(f32[640]{0:T(1024)} %gain_ref.1) | copy-start | bytes 7684

commit v6 on v5

--- a/solution.py
+++ b/solution.py
@@ -181,14 +181,7 @@
     local_ref[LAT:, 256:] = jnp.zeros((LAT, 128), f32)
 
 
-def local_kernel(place_ref, own_ref, below_ref, above_ref, first_ref, second_ref, wave_ref, out_ref, taps_ref):
-    shape = (CHANNELS, 384)
-    at = lax.broadcasted_iota(jnp.int32, shape, 1)
-    tail = at % 8 + 32
-    at = jnp.where(at >= 256, tail, at // 128 * 16 + at % 16)
-    chosen = (lax.broadcasted_iota(jnp.int32, shape, 0) == channel_at(place_ref, at)).astype(f32)
-    taps_ref[0:25] = pick(first_ref[...], chosen, ((1,), (0,)))
-    taps_ref[32:57] = pick(second_ref[...], chosen, ((1,), (0,)))
+def local_kernel(place_ref, own_ref, below_ref, above_ref, taps_ref, out_ref):
     lane = lax.broadcasted_iota(jnp.int32, (1, 128), 1)
     left = lane < 64
     south = jnp.where(place_ref[0] == 0, 0.0, 1.0)
@@ -214,8 +207,9 @@
         return jnp.where(keep, first, second), jnp.where(keep, second, first)
 
     def weights(which, a, tile):
-        rows = [taps_ref[32 * which + 5 * a + b : 32 * which + 5 * a + b + 1, 128 * tile : 128 * tile + 128] for b in range(5)]
-        cos1, cos2, sin1, sin2 = (wave_ref[:, 128 * n : 128 * n + 128] for n in range(4))
+        start = 480 + 32 * which + 5 * a
+        rows = [taps_ref[start + b : start + b + 1, 128 * tile : 128 * tile + 128] for b in range(5)]
+        cos1, cos2, sin1, sin2 = (taps_ref[544:576, 128 * n : 128 * n + 128] for n in range(4))
         real = rows[2] + (rows[3] + rows[1]) * cos1 + (rows[4] + rows[0]) * cos2
         imag = (rows[3] - rows[1]) * sin1 + (rows[4] - rows[0]) * sin2
         return real, imag
@@ -267,13 +261,26 @@
     return lax.dot_general(a, b, (dims, ((), ())), precision=lax.Precision.HIGHEST, preferred_element_type=f32)
 
 
-def taps_kernel(place_ref, first_ref, second_ref, phase_ref, local_ref, taps_ref, up_ref, down_ref):
+def taps_kernel(place_ref, first_ref, second_ref, phase_ref, local_ref, gain_ref, wave_ref, taps_ref, up_ref, down_ref):
+    gain = gain_ref[...]
+    gain = jnp.where(place_ref[1] == 1, jnp.concatenate([gain[8:], gain[:8]], axis=0), gain)
+    base = 10 * SLICE
+    taps_ref[base : base + SLICE, :MODES] = gain
+    taps_ref[base + SLICE : base + 2 * SLICE, :MODES] = jnp.where(place_ref[0] == 0, 0.0, gain)
     left = lane_slot(64) == 0
     a, b = local_ref[:, :128], local_ref[:, 128:256]
     up_ref[: 2 * LAT] = jnp.where(left, pltpu.roll(a, 64, 1), b)
     down_ref[: 2 * LAT] = jnp.where(left, a, pltpu.roll(b, 64, 1))
     up_ref[2 * LAT :] = local_ref[:LAT, 256:]
     down_ref[2 * LAT :] = local_ref[:LAT, 256:]
+    taps_ref[544:576, :512] = wave_ref[...]
+    shape = (CHANNELS, 384)
+    at = lax.broadcasted_iota(jnp.int32, shape, 1)
+    tail = at % 8 + 32
+    at = jnp.where(at >= 256, tail, at // 128 * 16 + at % 16)
+    chosen = (lax.broadcasted_iota(jnp.int32, shape, 0) == channel_at(place_ref, at)).astype(f32)
+    taps_ref[480:505, :384] = pick(first_ref[...], chosen, ((1,), (0,)))
+    taps_ref[512:537, :384] = pick(second_ref[...], chosen, ((1,), (0,)))
     shape = (SLICE, CHANNELS)
     wanted = channel_at(place_ref, lax.broadcasted_iota(jnp.int32, shape, 0))
     chosen = (lax.broadcasted_iota(jnp.int32, shape, 1) == wanted).astype(f32)
@@ -324,7 +331,7 @@
             high_ref[k, :, 128 * part : 128 * part + 128] = high
             low_ref[k, :, 128 * part : 128 * part + 128] = low
 
-def spectral_kernel(place_ref, in_ref, high_ref, low_ref, taps_ref, gain_ref, angle_ref, out_ref, u_ref, v_ref, f_ref):
+def spectral_kernel(in_ref, high_ref, low_ref, taps_ref, angle_ref, out_ref, u_ref, v_ref, f_ref):
     lane = lax.broadcasted_iota(jnp.int32, (1, 128), 1) % LAT
 
     def fill_edges(ref):
@@ -396,12 +403,11 @@
                     f_ref[4 * group + n, SLICE * part : SLICE * part + SLICE] = (
                         jnp.concatenate([halves[0][n], halves[1][n]], axis=1) * weight
                     )
-    gain = gain_ref[...]
-    gain = jnp.where(place_ref[1] == 1, jnp.concatenate([gain[8:], gain[:8]], axis=0), gain)
+    gain, masked = (taps_ref[SLICE * n : SLICE * n + SLICE, :MODES] for n in (10, 11))
     for k in range(OWN):
         table = (high_ref[k], low_ref[k])
         spectrum = dot3(split(f_ref[k]), table, ((1,), (1,)))
-        second = jnp.where(place_ref[0] == 0, 0.0, gain) if k == 0 else gain
+        second = masked if k == 0 else gain
         f_ref[k] = dot3(split(spectrum * jnp.concatenate([gain, second], axis=0)), table)
     for part in range(2):
         for group in range(2):
@@ -591,37 +597,38 @@
     high, low = legendre(owner, angles, seeds)
     phases = lax.dynamic_index_in_dim(jnp.asarray(phase_np()), band, 0, False)
     place = jnp.stack([band, odd, sector]).astype(jnp.int32)
-    shapes = ((10 * SLICE, 640), (3 * LAT, 128), (3 * LAT, 128))
+    shapes = ((576, 640), (3 * LAT, 128), (3 * LAT, 128))
     taps, up, down = pl.pallas_call(
         taps_kernel,
         out_shape=tuple(jax.ShapeDtypeStruct(shape, f32) for shape in shapes),
-        in_specs=[pl.BlockSpec(memory_space=pltpu.SMEM)] + vmem(4),
+        in_specs=[pl.BlockSpec(memory_space=pltpu.SMEM)] + vmem(6),
         out_specs=vmem(3),
         compiler_params=pltpu.CompilerParams(vmem_limit_bytes=16 << 20),
         cost_estimate=pl.CostEstimate(flops=10**7, bytes_accessed=10**7, transcendentals=0),
-    )(place, conv_first, conv_second, phases, local)
+    )(place, conv_first, conv_second, phases, local, filter_gains.T, jnp.asarray(wave_np()))
     rising = [(n, n + 1) for n in range(LAT - 1)]
     below = lax.ppermute(up, "lat", rising)
     above = lax.ppermute(down, "lat", [(target, source) for source, target in rising])
     stay = pl.pallas_call(
         local_kernel,
         out_shape=jax.ShapeDtypeStruct((2 * LAT, 384), f32),
-        in_specs=[pl.BlockSpec(memory_space=pltpu.SMEM)] + vmem(6),
+        in_specs=[pl.BlockSpec(memory_space=pltpu.SMEM)] + vmem(4),
         out_specs=vmem(1)[0],
-        scratch_shapes=[pltpu.VMEM((64, 384), f32)],
         compiler_params=pltpu.CompilerParams(vmem_limit_bytes=16 << 20),
         cost_estimate=pl.CostEstimate(flops=10**7, bytes_accessed=10**6, transcendentals=0),
-    )(place, local, below, above, conv_first, conv_second, jnp.asarray(wave_np()))
+    )(place, local, below, above, taps)
     orders, taps, high, low = lax.optimization_barrier((orders, taps, high, low))
     state = pltpu.VMEM((2, 2, 12, SLICE, 128), f32)
-    third = pl.pallas_call(
+    third = run(
         spectral_kernel,
-        out_shape=jax.ShapeDtypeStruct((LAT * LAT_CHUNK, 128), f32),
-        in_specs=[pl.BlockSpec(memory_space=pltpu.SMEM)] + vmem(6),
-        out_specs=vmem(1)[0],
-        scratch_shapes=[state, state, pltpu.VMEM((OWN, 2 * SLICE, NLAT), f32)],
-        compiler_params=pltpu.CompilerParams(vmem_limit_bytes=24 << 20),
-    )(place, orders, high, low, taps, filter_gains.T, angles)
+        (LAT * LAT_CHUNK, 128),
+        orders,
+        high,
+        low,
+        taps,
+        angles,
+        scratch=[state, state, pltpu.VMEM((OWN, 2 * SLICE, NLAT), f32)],
+    )
     returned = exchange(third, "lat", LAT)
     restored = run(inverse_kernel, (LON * LON_CHUNK, 128), returned, stay, *map(jnp.asarray, inverse))
     arrived = exchange(restored, "lon", LON)

time: 115 us -> 113 us (0.983)
  local copies, waits for them, and re-layouts: 4.81 us -> 2.68 us
    pallas_call x1 -> x0, Pallas kernels: 3.96 us -> none  [per_device(): pl.pallas_call(spectral_kernel, out_shape=jax.ShapeDtypeStruct((LAT * LAT...]
    pallas_call x3 -> x4, Pallas kernels: 6.27 us -> 9.51 us  [run(): pl.pallas_call(kernel, out_shape=jax.ShapeDtypeStruct(shape, f32), in_spe...]
    unnamed x34 -> x32, local copies, waits for them, and re-layouts: 3.42 us -> 1.29 us
  transfers between devices with their start and end apart: 4 -> 4, of which waited for: 4 -> 3; matrix products, arithmetic and copies ran while one was open for 1% -> 1% of each run, Pallas kernels for 4% -> 4%
where the time goes in v6:
time: 113 us; the launch traced here: 112 us
  blocking collectives  48.3 us (43%)
  starting transfers between devices  25.6 us (23%)
  waiting for transfers between devices  19.5 us (17%)
  Pallas kernels  16 us (14%)
  local copies, waits for them, and re-layouts  2.68 us (2%)
    all_to_all x2, blocking collectives, exchange(): lax.all_to_all(array.reshape(shape), axis, split_axis=0, concat_axis=0, t...  48.3 us
    all_to_all x2, starting transfers between devices, exchange(): lax.all_to_all(array.reshape(shape), axis, split_axis=0, concat_axis=0, t...  18.6 us
    all_to_all x2, waiting for transfers between devices, exchange(): lax.all_to_all(array.reshape(shape), axis, split_axis=0, concat_axis=0, t...  17.7 us
    pallas_call x4, Pallas kernels, run(): pl.pallas_call(kernel, out_shape=jax.ShapeDtypeStruct(shape, f32), in_spe...  9.51 us
    ppermute x1, starting transfers between devices, per_device(): lax.ppermute(down, 'lat', [(target, source) for source, target in rising])  5.04 us
    pallas_call x1, Pallas kernels, per_device(): pl.pallas_call(taps_kernel, out_shape=tuple((jax.ShapeDtypeStruct(shape,...  2.28 us
  transfers between devices with their start and end apart: 4, of which 3 were waited for; matrix products, arithmetic and copies ran while one was open for 1% of the time, Pallas kernels for 4%

profile of v6, /device:TPU:4, one launch (start us, length us, event | category | flops | bytes accessed | tf_op | source)
XLA Modules:
  0.0 112.4 jit_solution(4163458836168252365)
XLA Ops:
  0.0 2.5 %shard_map.145 = f32[1120,128]{1,0:T(8,128)S(1)} custom-call(f32[28,8,640]{2,1,0:T(8,128)} %bitcast.25), custom_call_target="tpu_custom_call" | custom-call | tf_op jit(solution)/shard_map/pallas_call | solution.py:525
  2.6 0.0 copy-start.10
  2.6 0.0 copy-start.8
  2.6 27.0 %all_to_all.20 = f32[16,1,8960]{2,1,0:T(1,128)S(1)} all-to-all(f32[16,1,8960]{2,1,0:T(1,128)S(1)} %bitcast.21), channel_id=1, replica_groups=mesh['lat'=32,'lon'=16] {'lon'}, dimensions={0} | all-to-all | bytes 1146880 | tf_op jit(solution)/shard_map/all_to_all | solution.py:558
  29.6 1.7 %shard_map.146 = (f32[960,128]{1,0:T(8,128)}, f32[64,384]{1,0:T(8,128)S(1)}) custom-call(f32[1120,128]{1,0:T(8,128)S(1)} %bitcast.20, bf16[448,512]{1,0:T(8,128)(2,1)S(1)} %copy-done.4, bf16[448,512]{1,0:T(8,128)(2,1)S(1)} %copy-done.5), custom_call_target="tpu_custom_call" | custom-call | tf_op jit(solution)/shard_map/pallas_call | solution.py:584
  31.3 13.4 %all-to-all-start.1 = ((f32[32,1,3840]{2,1,0:T(1,128)}), f32[32,1,3840]{2,1,0:T(1,128)S(1)}, u32[]{:S(2)}, u32[]{:S(2)}) async-start(f32[32,1,3840]{2,1,0:T(1,128)} %bitcast.3), calls=%async_computation.1 | async-start | bytes 983040 | tf_op jit(solution)/shard_map/all_to_all | solution.py:558
  44.8 0.7 dynamic-slice_bitcast_fusion.seed_ref
  45.5 0.9 shard_map.148
  46.4 0.1 pad_add_fusion.place_ref
  46.5 0.7 dynamic-slice_bitcast_fusion.1.phase_ref
  47.2 2.3 %shard_map.147 = (f32[576,640]{1,0:T(8,128)S(1)}, f32[96,128]{1,0:T(8,128)S(1)}, f32[96,128]{1,0:T(8,128)S(1)}) custom-call(s32[3]{0:T(128)S(1)} %pad_add_fusion.place_ref, f32[25,640]{1,0:T(8,128)S(1)} %copy-done.6, f32[25,640]{1,0:T(8,128)S(1)} %copy-done.7, f32[8,20]{1,0:T(8,128)S(1)} %dynamic-slice_bitcast_fusion.1.phase_ref, ...), custom_call_target="tpu_custom_call" | custom-call | flops 10000000 | bytes 10000000 | tf_op jit(solution)/shard_map/pallas_call | solution.py:601
  49.5 0.6 copy-done.12
  50.1 0.6 copy-done.14
  50.7 11.0 %all-to-all-done.1 = f32[32,1,3840]{2,1,0:T(1,128)S(1)} async-done(((f32[32,1,3840]{2,1,0:T(1,128)}), f32[32,1,3840]{2,1,0:T(1,128)S(1)}, u32[]{:S(2)}, u32[]{:S(2)}) %all-to-all-start.1) | async-done | bytes 491552 | tf_op jit(solution)/shard_map/all_to_all | solution.py:558
  61.7 3.3 %shard_map.149 = f32[960,128]{1,0:T(8,128)} custom-call(f32[960,128]{1,0:T(8,128)S(1)} %bitcast.22, bf16[6,192,256]{2,1,0:T(8,128)(2,1)S(1)} %get-tuple-element.30.high_ref, bf16[6,192,256]{2,1,0:T(8,128)(2,1)S(1)} %get-tuple-element.31.low_ref, f32[576,640]{1,0:T(8,128)S(1)} %get-tuple-element.32.taps_ref, f32[8,256]{1,0:T(8,128)S(1)} %copy-done.10), custom_call_target="tpu_custom_call" | custom-call | tf_op jit(solution)/shard_map/pallas_call | solution.py:525
  65.0 5.1 %all-to-all-start.2 = ((f32[32,1,3840]{2,1,0:T(1,128)}), f32[32,1,3840]{2,1,0:T(1,128)S(1)}, u32[]{:S(2)}, u32[]{:S(2)}) async-start(f32[32,1,3840]{2,1,0:T(1,128)} %bitcast.11), calls=%async_computation.2 | async-start | bytes 983040 | tf_op jit(solution)/shard_map/all_to_all | solution.py:558
  70.2 2.0 %collective-permute-start = (f32[96,128]{1,0:T(8,128)S(1)}, f32[96,128]{1,0:T(8,128)S(1)}, u32[]{:S(2)}, u32[]{:S(2)}) collective-permute-start(f32[96,128]{1,0:T(8,128)S(1)} %copy-done.15), channel_id=1, source_target_pairs={{0,16},{16,32},{32,48},{48,64},{64,80},{80,96},{96,112},{112,128},... | collective-permute-start | bytes 147464 | tf_op jit(solution)/shard_map/ppermute | solution.py:610
  72.2 5.0 %collective-permute-start.1 = (f32[96,128]{1,0:T(8,128)S(1)}, f32[96,128]{1,0:T(8,128)S(1)}, u32[]{:S(2)}, u32[]{:S(2)}) collective-permute-start(f32[96,128]{1,0:T(8,128)S(1)} %copy-done.13), channel_id=1, source_target_pairs={{16,0},{32,16},{48,32},{64,48},{80,64},{96,80},{112,96},{128,112},... | collective-permute-start | bytes 147464 | tf_op jit(solution)/shard_map/ppermute | solution.py:611
  77.3 1.7 %collective-permute-done.1.above_ref = f32[96,128]{1,0:T(8,128)S(1)} collective-permute-done((f32[96,128]{1,0:T(8,128)S(1)}, f32[96,128]{1,0:T(8,128)S(1)}, u32[]{:S(2)}, u32[]{:S(2)}) %collective-permute-start.1) | collective-permute-done | bytes 49184 | tf_op jit(solution)/shard_map/ppermute | solution.py:611
  79.0 1.7 %shard_map.150.local_ref = f32[64,384]{1,0:T(8,128)S(1)} custom-call(s32[3]{0:T(128)S(1)} %pad_add_fusion.place_ref, f32[64,384]{1,0:T(8,128)S(1)} %get-tuple-element.25.local_ref.own_ref, f32[96,128]{1,0:T(8,128)S(1)} %collective-permute-done.below_ref, f32[96,128]{1,0:T(8,128)S(1)} %collective-permute-done.1.above_ref, ...), custom_call_target="tpu_custom_call" | custom-call | flops 10000000 | bytes 1000000 | tf_op jit(solution)/shard_map/pallas_call | solution.py:612
  80.7 6.7 %all-to-all-done.2 = f32[32,1,3840]{2,1,0:T(1,128)S(1)} async-done(((f32[32,1,3840]{2,1,0:T(1,128)}), f32[32,1,3840]{2,1,0:T(1,128)S(1)}, u32[]{:S(2)}, u32[]{:S(2)}) %all-to-all-start.2) | async-done | bytes 491552 | tf_op jit(solution)/shard_map/all_to_all | solution.py:558
  87.4 1.0 shard_map.151
  88.4 21.3 %all_to_all.21 = f32[16,1,8960]{2,1,0:T(1,128)S(1)} all-to-all(f32[16,1,8960]{2,1,0:T(1,128)S(1)} %bitcast.19), channel_id=1, replica_groups=mesh['lat'=32,'lon'=16] {'lon'}, dimensions={0} | all-to-all | bytes 1146880 | tf_op jit(solution)/shard_map/all_to_all | solution.py:558
  109.7 2.7 %shard_map.152 = f32[28,8,640]{2,1,0:T(8,128)} custom-call(f32[1120,128]{1,0:T(8,128)S(1)} %bitcast.18, f32[640]{0:T(1024)S(1)} %copy-done.11, bf16[640,1280]{1,0:T(8,128)(2,1)S(1)} %copy-done, bf16[1280,640]{1,0:T(8,128)(2,1)S(1)} %copy-done.1), custom_call_target="tpu_custom_call" | custom-call | tf_op jit(solution)/shard_map/pallas_call | solution.py:525
  (29 shorter events, 0.1 us)
Async XLA Ops:
  0.0 29.6 %copy-start.4 = (bf16[448,512]{1,0:T(8,128)(2,1)S(1)}, bf16[448,512]{1,0:T(8,128)(2,1)}, u32[]{:S(2)}) copy-start(bf16[448,512]{1,0:T(8,128)(2,1)} %constant.49.clone.high_ref) | copy-start | bytes 1376260
  0.0 29.6 %copy-start.5 = (bf16[448,512]{1,0:T(8,128)(2,1)S(1)}, bf16[448,512]{1,0:T(8,128)(2,1)}, u32[]{:S(2)}) copy-start(bf16[448,512]{1,0:T(8,128)(2,1)} %constant.50.clone.low_ref) | copy-start | bytes 1376260
  2.6 42.9 %copy-start.10 = (f32[8,256]{1,0:T(8,128)S(1)}, f32[8,256]{1,0:T(8,128)}, u32[]{:S(2)}) copy-start(f32[8,256]{1,0:T(8,128)} %constant.48.clone.angle_ref) | copy-start | bytes 24580
  2.6 44.6 %copy-start.6 = (f32[25,640]{1,0:T(8,128)S(1)}, f32[25,640]{1,0:T(8,128)}, u32[]{:S(2)}) copy-start(f32[25,640]{1,0:T(8,128)} %first_ref) | copy-start | bytes 192004
  2.6 44.6 %copy-start.7 = (f32[25,640]{1,0:T(8,128)S(1)}, f32[25,640]{1,0:T(8,128)}, u32[]{:S(2)}) copy-start(f32[25,640]{1,0:T(8,128)} %second_ref) | copy-start | bytes 192004
  2.6 44.6 %copy-start.8 = (f32[32,512]{1,0:T(8,128)S(1)}, f32[32,512]{1,0:T(8,128)}, u32[]{:S(2)}) copy-start(f32[32,512]{1,0:T(8,128)} %constant.53.clone.wave_ref) | copy-start | bytes 196612
  2.6 44.5 %copy-start.9 = (f32[192,40]{0,1:T(8,128)S(1)}, f32[192,40]{0,1:T(8,128)}, u32[]{:S(2)}) copy-start(f32[192,40]{0,1:T(8,128)} %param.18) | copy-start | bytes 92164
  31.3 30.4 %all-to-all-start.1 = ((f32[32,1,3840]{2,1,0:T(1,128)}), f32[32,1,3840]{2,1,0:T(1,128)S(1)}, u32[]{:S(2)}, u32[]{:S(2)}) async-start(f32[32,1,3840]{2,1,0:T(1,128)} %bitcast.3), calls=%async_computation.1 | async-start | bytes 983040 | tf_op jit(solution)/shard_map/all_to_all | solution.py:558
  49.5 0.6 copy-start.12
  50.1 0.6 copy-start.14
  61.7 8.4 %copy-start.15 = (f32[96,128]{1,0:T(8,128)S(1)}, f32[96,128]{1,0:T(8,128)}, u32[]{:S(2)}) copy-start(f32[96,128]{1,0:T(8,128)} %copy-done.14) | copy-start | bytes 147460
  61.7 10.5 %copy-start.13 = (f32[96,128]{1,0:T(8,128)S(1)}, f32[96,128]{1,0:T(8,128)}, u32[]{:S(2)}) copy-start(f32[96,128]{1,0:T(8,128)} %copy-done.12) | copy-start | bytes 147460
  65.0 22.4 %copy-start.2 = (bf16[2,512,256]{2,1,0:T(8,128)(2,1)S(1)}, bf16[2,512,256]{2,1,0:T(8,128)(2,1)}, u32[]{:S(2)}) copy-start(bf16[2,512,256]{2,1,0:T(8,128)(2,1)} %constant.54.clone.high_ref) | copy-start | bytes 1572868
  65.0 22.4 %copy-start.3 = (bf16[2,512,256]{2,1,0:T(8,128)(2,1)S(1)}, bf16[2,512,256]{2,1,0:T(8,128)(2,1)}, u32[]{:S(2)}) copy-start(bf16[2,512,256]{2,1,0:T(8,128)(2,1)} %constant.55.clone.low_ref) | copy-start | bytes 1572868
  65.0 22.3 %all-to-all-start.2 = ((f32[32,1,3840]{2,1,0:T(1,128)}), f32[32,1,3840]{2,1,0:T(1,128)S(1)}, u32[]{:S(2)}, u32[]{:S(2)}) async-start(f32[32,1,3840]{2,1,0:T(1,128)} %bitcast.11), calls=%async_computation.2 | async-start | bytes 983040 | tf_op jit(solution)/shard_map/all_to_all | solution.py:558
  70.2 7.1 %collective-permute-start = (f32[96,128]{1,0:T(8,128)S(1)}, f32[96,128]{1,0:T(8,128)S(1)}, u32[]{:S(2)}, u32[]{:S(2)}) collective-permute-start(f32[96,128]{1,0:T(8,128)S(1)} %copy-done.15), channel_id=1, source_target_pairs={{0,16},{16,32},{32,48},{48,64},{64,80},{80,96},{96,112},{112,128},... | collective-permute-start | bytes 147464 | tf_op jit(solution)/shard_map/ppermute | solution.py:610
  72.2 6.8 %collective-permute-start.1 = (f32[96,128]{1,0:T(8,128)S(1)}, f32[96,128]{1,0:T(8,128)S(1)}, u32[]{:S(2)}, u32[]{:S(2)}) collective-permute-start(f32[96,128]{1,0:T(8,128)S(1)} %copy-done.13), channel_id=1, source_target_pairs={{16,0},{32,16},{48,32},{64,48},{80,64},{96,80},{112,96},{128,112},... | collective-permute-start | bytes 147464 | tf_op jit(solution)/shard_map/ppermute | solution.py:611
  87.4 22.3 %copy-start = (bf16[640,1280]{1,0:T(8,128)(2,1)S(1)}, bf16[640,1280]{1,0:T(8,128)(2,1)}, u32[]{:S(2)}) copy-start(bf16[640,1280]{1,0:T(8,128)(2,1)} %up_ref.1) | copy-start | bytes 4915204
  87.4 22.3 %copy-start.1 = (bf16[1280,640]{1,0:T(8,128)(2,1)S(1)}, bf16[1280,640]{1,0:T(8,128)(2,1)}, u32[]{:S(2)}) copy-start(bf16[1280,640]{1,0:T(8,128)(2,1)} %down_ref.1) | copy-start | bytes 4915204
  87.4 22.3 %copy-start.11 = (f32[640]{0:T(1024)S(1)}, f32[640]{0:T(1024)}, u32[]{:S(2)}) copy-start(f32[640]{0:T(1024)} %gain_ref.1) | copy-start | bytes 7684

commit v7 on v6

--- a/solution.py
+++ b/solution.py
@@ -181,12 +181,10 @@
     local_ref[LAT:, 256:] = jnp.zeros((LAT, 128), f32)
 
 
-def local_kernel(place_ref, own_ref, below_ref, above_ref, taps_ref, out_ref):
+def local_kernel(own_ref, below_ref, above_ref, taps_ref, out_ref):
     lane = lax.broadcasted_iota(jnp.int32, (1, 128), 1)
     left = lane < 64
-    south = jnp.where(place_ref[0] == 0, 0.0, 1.0)
-    north = jnp.where(place_ref[0] == LAT - 1, 0.0, 1.0)
-    masks = (jnp.where(left, south, 1.0), jnp.where(left, 1.0, north))
+    masks = (taps_ref[576:577, :128], taps_ref[577:578, :128])
 
     def extend(own, below, above):
         turned = pltpu.roll(own, 64, 1)
@@ -274,6 +272,11 @@
     up_ref[2 * LAT :] = local_ref[:LAT, 256:]
     down_ref[2 * LAT :] = local_ref[:LAT, 256:]
     taps_ref[544:576, :512] = wave_ref[...]
+    south = jnp.where(place_ref[0] == 0, 0.0, 1.0)
+    north = jnp.where(place_ref[0] == LAT - 1, 0.0, 1.0)
+    row = lax.broadcasted_iota(jnp.int32, (8, 128), 0)
+    edges = jnp.where(row == 0, jnp.where(left, south, 1.0), jnp.where(left, 1.0, north))
+    taps_ref[576:584, :128] = edges
     shape = (CHANNELS, 384)
     at = lax.broadcasted_iota(jnp.int32, shape, 1)
     tail = at % 8 + 32
@@ -597,7 +600,7 @@
     high, low = legendre(owner, angles, seeds)
     phases = lax.dynamic_index_in_dim(jnp.asarray(phase_np()), band, 0, False)
     place = jnp.stack([band, odd, sector]).astype(jnp.int32)
-    shapes = ((576, 640), (3 * LAT, 128), (3 * LAT, 128))
+    shapes = ((584, 640), (3 * LAT, 128), (3 * LAT, 128))
     taps, up, down = pl.pallas_call(
         taps_kernel,
         out_shape=tuple(jax.ShapeDtypeStruct(shape, f32) for shape in shapes),
@@ -612,11 +615,11 @@
     stay = pl.pallas_call(
         local_kernel,
         out_shape=jax.ShapeDtypeStruct((2 * LAT, 384), f32),
-        in_specs=[pl.BlockSpec(memory_space=pltpu.SMEM)] + vmem(4),
+        in_specs=vmem(4),
         out_specs=vmem(1)[0],
         compiler_params=pltpu.CompilerParams(vmem_limit_bytes=16 << 20),
         cost_estimate=pl.CostEstimate(flops=10**7, bytes_accessed=10**6, transcendentals=0),
-    )(place, local, below, above, taps)
+    )(local, below, above, taps)
     orders, taps, high, low = lax.optimization_barrier((orders, taps, high, low))
     state = pltpu.VMEM((2, 2, 12, SLICE, 128), f32)
     third = run(

time: 113 us -> 113 us (level)
  no operation moved by 1% of the time
where the time goes in v7:
time: 113 us; the launch traced here: 112 us
  blocking collectives  48.3 us (43%)
  starting transfers between devices  25.6 us (23%)
  waiting for transfers between devices  20 us (18%)
  Pallas kernels  15.5 us (14%)
  local copies, waits for them, and re-layouts  2.68 us (2%)
    all_to_all x2, blocking collectives, exchange(): lax.all_to_all(array.reshape(shape), axis, split_axis=0, concat_axis=0, t...  48.3 us
    all_to_all x2, starting transfers between devices, exchange(): lax.all_to_all(array.reshape(shape), axis, split_axis=0, concat_axis=0, t...  18.6 us
    all_to_all x2, waiting for transfers between devices, exchange(): lax.all_to_all(array.reshape(shape), axis, split_axis=0, concat_axis=0, t...  18.3 us
    pallas_call x4, Pallas kernels, run(): pl.pallas_call(kernel, out_shape=jax.ShapeDtypeStruct(shape, f32), in_spe...  9.55 us
    ppermute x1, starting transfers between devices, per_device(): lax.ppermute(down, 'lat', [(target, source) for source, target in rising])  5.04 us
    pallas_call x1, Pallas kernels, per_device(): pl.pallas_call(taps_kernel, out_shape=tuple((jax.ShapeDtypeStruct(shape,...  2.28 us
  transfers between devices with their start and end apart: 4, of which 3 were waited for; matrix products, arithmetic and copies ran while one was open for 1% of the time, Pallas kernels for 4%

profile of v7, /device:TPU:4, one launch (start us, length us, event | category | flops | bytes accessed | tf_op | source)
XLA Modules:
  0.0 112.4 jit_solution(2865991420850161964)
XLA Ops:
  0.0 2.5 %shard_map.145 = f32[1120,128]{1,0:T(8,128)S(1)} custom-call(f32[28,8,640]{2,1,0:T(8,128)} %bitcast.25), custom_call_target="tpu_custom_call" | custom-call | tf_op jit(solution)/shard_map/pallas_call | solution.py:528
  2.6 0.0 copy-start.10
  2.6 0.0 copy-start.8
  2.6 27.0 %all_to_all.20 = f32[16,1,8960]{2,1,0:T(1,128)S(1)} all-to-all(f32[16,1,8960]{2,1,0:T(1,128)S(1)} %bitcast.21), channel_id=1, replica_groups=mesh['lat'=32,'lon'=16] {'lon'}, dimensions={0} | all-to-all | bytes 1146880 | tf_op jit(solution)/shard_map/all_to_all | solution.py:561
  29.6 1.7 %shard_map.146 = (f32[960,128]{1,0:T(8,128)}, f32[64,384]{1,0:T(8,128)S(1)}) custom-call(f32[1120,128]{1,0:T(8,128)S(1)} %bitcast.20, bf16[448,512]{1,0:T(8,128)(2,1)S(1)} %copy-done.4, bf16[448,512]{1,0:T(8,128)(2,1)S(1)} %copy-done.5), custom_call_target="tpu_custom_call" | custom-call | tf_op jit(solution)/shard_map/pallas_call | solution.py:587
  31.3 13.4 %all-to-all-start.1 = ((f32[32,1,3840]{2,1,0:T(1,128)}), f32[32,1,3840]{2,1,0:T(1,128)S(1)}, u32[]{:S(2)}, u32[]{:S(2)}) async-start(f32[32,1,3840]{2,1,0:T(1,128)} %bitcast.3), calls=%async_computation.1 | async-start | bytes 983040 | tf_op jit(solution)/shard_map/all_to_all | solution.py:561
  44.8 0.7 dynamic-slice_bitcast_fusion.seed_ref
  45.5 0.9 shard_map.148
  46.4 0.1 pad_add_fusion.place_ref
  46.5 0.7 dynamic-slice_bitcast_fusion.1.phase_ref
  47.2 2.3 %shard_map.147 = (f32[584,640]{1,0:T(8,128)S(1)}, f32[96,128]{1,0:T(8,128)S(1)}, f32[96,128]{1,0:T(8,128)S(1)}) custom-call(s32[3]{0:T(128)S(1)} %pad_add_fusion.place_ref, f32[25,640]{1,0:T(8,128)S(1)} %copy-done.6, f32[25,640]{1,0:T(8,128)S(1)} %copy-done.7, f32[8,20]{1,0:T(8,128)S(1)} %dynamic-slice_bitcast_fusion.1.phase_ref, ...), custom_call_target="tpu_custom_call" | custom-call | flops 10000000 | bytes 10000000 | tf_op jit(solution)/shard_map/pallas_call | solution.py:604
  49.5 0.6 copy-done.12
  50.1 0.6 copy-done.14
  50.7 11.0 %all-to-all-done.1 = f32[32,1,3840]{2,1,0:T(1,128)S(1)} async-done(((f32[32,1,3840]{2,1,0:T(1,128)}), f32[32,1,3840]{2,1,0:T(1,128)S(1)}, u32[]{:S(2)}, u32[]{:S(2)}) %all-to-all-start.1) | async-done | bytes 491552 | tf_op jit(solution)/shard_map/all_to_all | solution.py:561
  61.7 3.3 %shard_map.149 = f32[960,128]{1,0:T(8,128)} custom-call(f32[960,128]{1,0:T(8,128)S(1)} %bitcast.22, bf16[6,192,256]{2,1,0:T(8,128)(2,1)S(1)} %get-tuple-element.30.high_ref, bf16[6,192,256]{2,1,0:T(8,128)(2,1)S(1)} %get-tuple-element.31.low_ref, f32[584,640]{1,0:T(8,128)S(1)} %get-tuple-element.32.taps_ref, f32[8,256]{1,0:T(8,128)S(1)} %copy-done.10), custom_call_target="tpu_custom_call" | custom-call | tf_op jit(solution)/shard_map/pallas_call | solution.py:528
  65.1 5.1 %all-to-all-start.2 = ((f32[32,1,3840]{2,1,0:T(1,128)}), f32[32,1,3840]{2,1,0:T(1,128)S(1)}, u32[]{:S(2)}, u32[]{:S(2)}) async-start(f32[32,1,3840]{2,1,0:T(1,128)} %bitcast.11), calls=%async_computation.2 | async-start | bytes 983040 | tf_op jit(solution)/shard_map/all_to_all | solution.py:561
  70.2 2.0 %collective-permute-start = (f32[96,128]{1,0:T(8,128)S(1)}, f32[96,128]{1,0:T(8,128)S(1)}, u32[]{:S(2)}, u32[]{:S(2)}) collective-permute-start(f32[96,128]{1,0:T(8,128)S(1)} %copy-done.15), channel_id=1, source_target_pairs={{0,16},{16,32},{32,48},{48,64},{64,80},{80,96},{96,112},{112,128},... | collective-permute-start | bytes 147464 | tf_op jit(solution)/shard_map/ppermute | solution.py:613
  72.2 5.0 %collective-permute-start.1 = (f32[96,128]{1,0:T(8,128)S(1)}, f32[96,128]{1,0:T(8,128)S(1)}, u32[]{:S(2)}, u32[]{:S(2)}) collective-permute-start(f32[96,128]{1,0:T(8,128)S(1)} %copy-done.13), channel_id=1, source_target_pairs={{16,0},{32,16},{48,32},{64,48},{80,64},{96,80},{112,96},{128,112},... | collective-permute-start | bytes 147464 | tf_op jit(solution)/shard_map/ppermute | solution.py:614
  77.3 1.7 %collective-permute-done.1.above_ref = f32[96,128]{1,0:T(8,128)S(1)} collective-permute-done((f32[96,128]{1,0:T(8,128)S(1)}, f32[96,128]{1,0:T(8,128)S(1)}, u32[]{:S(2)}, u32[]{:S(2)}) %collective-permute-start.1) | collective-permute-done | bytes 49184 | tf_op jit(solution)/shard_map/ppermute | solution.py:614
  79.0 1.1 %shard_map.150.local_ref = f32[64,384]{1,0:T(8,128)S(1)} custom-call(f32[64,384]{1,0:T(8,128)S(1)} %get-tuple-element.25.local_ref.own_ref, f32[96,128]{1,0:T(8,128)S(1)} %collective-permute-done.below_ref, f32[96,128]{1,0:T(8,128)S(1)} %collective-permute-done.1.above_ref, f32[584,640]{1,0:T(8,128)S(1)} %get-tuple-element.32.taps_ref), custom_call_target="tpu_custom_call" | custom-call | flops 10000000 | bytes 1000000 | tf_op jit(solution)/shard_map/pallas_call | solution.py:615
  80.2 7.2 %all-to-all-done.2 = f32[32,1,3840]{2,1,0:T(1,128)S(1)} async-done(((f32[32,1,3840]{2,1,0:T(1,128)}), f32[32,1,3840]{2,1,0:T(1,128)S(1)}, u32[]{:S(2)}, u32[]{:S(2)}) %all-to-all-start.2) | async-done | bytes 491552 | tf_op jit(solution)/shard_map/all_to_all | solution.py:561
  87.4 1.0 shard_map.151
  88.4 21.3 %all_to_all.21 = f32[16,1,8960]{2,1,0:T(1,128)S(1)} all-to-all(f32[16,1,8960]{2,1,0:T(1,128)S(1)} %bitcast.19), channel_id=1, replica_groups=mesh['lat'=32,'lon'=16] {'lon'}, dimensions={0} | all-to-all | bytes 1146880 | tf_op jit(solution)/shard_map/all_to_all | solution.py:561
  109.7 2.7 %shard_map.152 = f32[28,8,640]{2,1,0:T(8,128)} custom-call(f32[1120,128]{1,0:T(8,128)S(1)} %bitcast.18, f32[640]{0:T(1024)S(1)} %copy-done.11, bf16[640,1280]{1,0:T(8,128)(2,1)S(1)} %copy-done, bf16[1280,640]{1,0:T(8,128)(2,1)S(1)} %copy-done.1), custom_call_target="tpu_custom_call" | custom-call | tf_op jit(solution)/shard_map/pallas_call | solution.py:528
  (29 shorter events, 0.1 us)
Async XLA Ops:
  0.0 29.6 %copy-start.4 = (bf16[448,512]{1,0:T(8,128)(2,1)S(1)}, bf16[448,512]{1,0:T(8,128)(2,1)}, u32[]{:S(2)}) copy-start(bf16[448,512]{1,0:T(8,128)(2,1)} %constant.49.clone.high_ref) | copy-start | bytes 1376260
  0.0 29.6 %copy-start.5 = (bf16[448,512]{1,0:T(8,128)(2,1)S(1)}, bf16[448,512]{1,0:T(8,128)(2,1)}, u32[]{:S(2)}) copy-start(bf16[448,512]{1,0:T(8,128)(2,1)} %constant.50.clone.low_ref) | copy-start | bytes 1376260
  2.6 42.9 %copy-start.10 = (f32[8,256]{1,0:T(8,128)S(1)}, f32[8,256]{1,0:T(8,128)}, u32[]{:S(2)}) copy-start(f32[8,256]{1,0:T(8,128)} %constant.48.clone.angle_ref) | copy-start | bytes 24580
  2.6 44.6 %copy-start.6 = (f32[25,640]{1,0:T(8,128)S(1)}, f32[25,640]{1,0:T(8,128)}, u32[]{:S(2)}) copy-start(f32[25,640]{1,0:T(8,128)} %first_ref) | copy-start | bytes 192004
  2.6 44.6 %copy-start.7 = (f32[25,640]{1,0:T(8,128)S(1)}, f32[25,640]{1,0:T(8,128)}, u32[]{:S(2)}) copy-start(f32[25,640]{1,0:T(8,128)} %second_ref) | copy-start | bytes 192004
  2.6 44.6 %copy-start.8 = (f32[32,512]{1,0:T(8,128)S(1)}, f32[32,512]{1,0:T(8,128)}, u32[]{:S(2)}) copy-start(f32[32,512]{1,0:T(8,128)} %constant.53.clone.wave_ref) | copy-start | bytes 196612
  2.6 44.5 %copy-start.9 = (f32[192,40]{0,1:T(8,128)S(1)}, f32[192,40]{0,1:T(8,128)}, u32[]{:S(2)}) copy-start(f32[192,40]{0,1:T(8,128)} %param.18) | copy-start | bytes 92164
  31.3 30.4 %all-to-all-start.1 = ((f32[32,1,3840]{2,1,0:T(1,128)}), f32[32,1,3840]{2,1,0:T(1,128)S(1)}, u32[]{:S(2)}, u32[]{:S(2)}) async-start(f32[32,1,3840]{2,1,0:T(1,128)} %bitcast.3), calls=%async_computation.1 | async-start | bytes 983040 | tf_op jit(solution)/shard_map/all_to_all | solution.py:561
  49.5 0.6 copy-start.12
  50.1 0.6 copy-start.14
  61.7 8.5 %copy-start.15 = (f32[96,128]{1,0:T(8,128)S(1)}, f32[96,128]{1,0:T(8,128)}, u32[]{:S(2)}) copy-start(f32[96,128]{1,0:T(8,128)} %copy-done.14) | copy-start | bytes 147460
  61.7 10.5 %copy-start.13 = (f32[96,128]{1,0:T(8,128)S(1)}, f32[96,128]{1,0:T(8,128)}, u32[]{:S(2)}) copy-start(f32[96,128]{1,0:T(8,128)} %copy-done.12) | copy-start | bytes 147460
  65.0 22.4 %copy-start.2 = (bf16[2,512,256]{2,1,0:T(8,128)(2,1)S(1)}, bf16[2,512,256]{2,1,0:T(8,128)(2,1)}, u32[]{:S(2)}) copy-start(bf16[2,512,256]{2,1,0:T(8,128)(2,1)} %constant.54.clone.high_ref) | copy-start | bytes 1572868
  65.1 22.4 %copy-start.3 = (bf16[2,512,256]{2,1,0:T(8,128)(2,1)S(1)}, bf16[2,512,256]{2,1,0:T(8,128)(2,1)}, u32[]{:S(2)}) copy-start(bf16[2,512,256]{2,1,0:T(8,128)(2,1)} %constant.55.clone.low_ref) | copy-start | bytes 1572868
  65.1 22.3 %all-to-all-start.2 = ((f32[32,1,3840]{2,1,0:T(1,128)}), f32[32,1,3840]{2,1,0:T(1,128)S(1)}, u32[]{:S(2)}, u32[]{:S(2)}) async-start(f32[32,1,3840]{2,1,0:T(1,128)} %bitcast.11), calls=%async_computation.2 | async-start | bytes 983040 | tf_op jit(solution)/shard_map/all_to_all | solution.py:561
  70.2 7.1 %collective-permute-start = (f32[96,128]{1,0:T(8,128)S(1)}, f32[96,128]{1,0:T(8,128)S(1)}, u32[]{:S(2)}, u32[]{:S(2)}) collective-permute-start(f32[96,128]{1,0:T(8,128)S(1)} %copy-done.15), channel_id=1, source_target_pairs={{0,16},{16,32},{32,48},{48,64},{64,80},{80,96},{96,112},{112,128},... | collective-permute-start | bytes 147464 | tf_op jit(solution)/shard_map/ppermute | solution.py:613
  72.2 6.8 %collective-permute-start.1 = (f32[96,128]{1,0:T(8,128)S(1)}, f32[96,128]{1,0:T(8,128)S(1)}, u32[]{:S(2)}, u32[]{:S(2)}) collective-permute-start(f32[96,128]{1,0:T(8,128)S(1)} %copy-done.13), channel_id=1, source_target_pairs={{16,0},{32,16},{48,32},{64,48},{80,64},{96,80},{112,96},{128,112},... | collective-permute-start | bytes 147464 | tf_op jit(solution)/shard_map/ppermute | solution.py:614
  87.4 22.3 %copy-start = (bf16[640,1280]{1,0:T(8,128)(2,1)S(1)}, bf16[640,1280]{1,0:T(8,128)(2,1)}, u32[]{:S(2)}) copy-start(bf16[640,1280]{1,0:T(8,128)(2,1)} %up_ref.1) | copy-start | bytes 4915204
  87.4 22.3 %copy-start.1 = (bf16[1280,640]{1,0:T(8,128)(2,1)S(1)}, bf16[1280,640]{1,0:T(8,128)(2,1)}, u32[]{:S(2)}) copy-start(bf16[1280,640]{1,0:T(8,128)(2,1)} %down_ref.1) | copy-start | bytes 4915204
  87.4 22.3 %copy-start.11 = (f32[640]{0:T(1024)S(1)}, f32[640]{0:T(1024)}, u32[]{:S(2)}) copy-start(f32[640]{0:T(1024)} %gain_ref.1) | copy-start | bytes 7684

commit v8 on v7

--- a/solution.py
+++ b/solution.py
@@ -127,10 +127,13 @@
     fetches = []
     for j in range(5):
         lanes = pl.ds(128 * j, 128)
-        fetches.append(pltpu.make_async_copy(x_hbm.at[:, :, lanes], x_ref.at[:, :, lanes], arrivals.at[j]))
-        fetches[j].start()
+        for part in range(4):
+            place = (pl.ds(7 * part, 7), slice(None), lanes)
+            fetches.append(pltpu.make_async_copy(x_hbm.at[place], x_ref.at[place], arrivals.at[4 * j + part]))
+            fetches[-1].start()
     for j in range(5):
-        fetches[j].wait()
+        for fetch in fetches[4 * j : 4 * j + 4]:
+            fetch.wait()
         blocks = swap_blocks([x_ref[:, i, 128 * j : 128 * j + 128] for i in range(ROWS)], 16)
         for b in range(8):
             pair, place = divmod(8 * j + b, 5)
@@ -576,7 +579,7 @@
         latent.transpose(1, 0, 2),
         scratch=[
             pltpu.VMEM((COLS, ROWS, CHANNELS), f32),
-            pltpu.SemaphoreType.DMA((5,)),
+            pltpu.SemaphoreType.DMA((20,)),
         ],
         far=1,
         grant=53,

time: 113 us -> 113 us (level)
  no operation moved by 1% of the time
where the time goes in v8:
time: 113 us; the launch traced here: 112 us
  blocking collectives  48.3 us (43%)
  starting transfers between devices  25.6 us (23%)
  waiting for transfers between devices  20 us (18%)
  Pallas kernels  15.6 us (14%)
  local copies, waits for them, and re-layouts  2.68 us (2%)
    all_to_all x2, blocking collectives, exchange(): lax.all_to_all(array.reshape(shape), axis, split_axis=0, concat_axis=0, t...  48.3 us
    all_to_all x2, starting transfers between devices, exchange(): lax.all_to_all(array.reshape(shape), axis, split_axis=0, concat_axis=0, t...  18.6 us
    all_to_all x2, waiting for transfers between devices, exchange(): lax.all_to_all(array.reshape(shape), axis, split_axis=0, concat_axis=0, t...  18.3 us
    pallas_call x4, Pallas kernels, run(): pl.pallas_call(kernel, out_shape=jax.ShapeDtypeStruct(shape, f32), in_spe...  9.6 us
    ppermute x1, starting transfers between devices, per_device(): lax.ppermute(down, 'lat', [(target, source) for source, target in rising])  5.04 us
    pallas_call x1, Pallas kernels, per_device(): pl.pallas_call(taps_kernel, out_shape=tuple((jax.ShapeDtypeStruct(shape,...  2.28 us
  transfers between devices with their start and end apart: 4, of which 3 were waited for; matrix products, arithmetic and copies ran while one was open for 1% of the time, Pallas kernels for 4%

profile of v8, /device:TPU:4, one launch (start us, length us, event | category | flops | bytes accessed | tf_op | source)
XLA Modules:
  0.0 112.5 jit_solution(12140600317108288488)
XLA Ops:
  0.0 2.6 %shard_map.145 = f32[1120,128]{1,0:T(8,128)S(1)} custom-call(f32[28,8,640]{2,1,0:T(8,128)} %bitcast.25), custom_call_target="tpu_custom_call" | custom-call | tf_op jit(solution)/shard_map/pallas_call | solution.py:531
  2.6 0.0 copy-start.10
  2.6 0.0 copy-start.8
  2.7 27.0 %all_to_all.20 = f32[16,1,8960]{2,1,0:T(1,128)S(1)} all-to-all(f32[16,1,8960]{2,1,0:T(1,128)S(1)} %bitcast.21), channel_id=1, replica_groups=mesh['lat'=32,'lon'=16] {'lon'}, dimensions={0} | all-to-all | bytes 1146880 | tf_op jit(solution)/shard_map/all_to_all | solution.py:564
  29.7 1.7 %shard_map.146 = (f32[960,128]{1,0:T(8,128)}, f32[64,384]{1,0:T(8,128)S(1)}) custom-call(f32[1120,128]{1,0:T(8,128)S(1)} %bitcast.20, bf16[448,512]{1,0:T(8,128)(2,1)S(1)} %copy-done.4, bf16[448,512]{1,0:T(8,128)(2,1)S(1)} %copy-done.5), custom_call_target="tpu_custom_call" | custom-call | tf_op jit(solution)/shard_map/pallas_call | solution.py:590
  31.4 13.4 %all-to-all-start.1 = ((f32[32,1,3840]{2,1,0:T(1,128)}), f32[32,1,3840]{2,1,0:T(1,128)S(1)}, u32[]{:S(2)}, u32[]{:S(2)}) async-start(f32[32,1,3840]{2,1,0:T(1,128)} %bitcast.3), calls=%async_computation.1 | async-start | bytes 983040 | tf_op jit(solution)/shard_map/all_to_all | solution.py:564
  44.8 0.7 dynamic-slice_bitcast_fusion.seed_ref
  45.5 0.9 shard_map.148
  46.4 0.1 pad_add_fusion.place_ref
  46.5 0.7 dynamic-slice_bitcast_fusion.1.phase_ref
  47.2 2.3 %shard_map.147 = (f32[584,640]{1,0:T(8,128)S(1)}, f32[96,128]{1,0:T(8,128)S(1)}, f32[96,128]{1,0:T(8,128)S(1)}) custom-call(s32[3]{0:T(128)S(1)} %pad_add_fusion.place_ref, f32[25,640]{1,0:T(8,128)S(1)} %copy-done.6, f32[25,640]{1,0:T(8,128)S(1)} %copy-done.7, f32[8,20]{1,0:T(8,128)S(1)} %dynamic-slice_bitcast_fusion.1.phase_ref, ...), custom_call_target="tpu_custom_call" | custom-call | flops 10000000 | bytes 10000000 | tf_op jit(solution)/shard_map/pallas_call | solution.py:607
  49.5 0.6 copy-done.12
  50.1 0.6 copy-done.14
  50.7 11.0 %all-to-all-done.1 = f32[32,1,3840]{2,1,0:T(1,128)S(1)} async-done(((f32[32,1,3840]{2,1,0:T(1,128)}), f32[32,1,3840]{2,1,0:T(1,128)S(1)}, u32[]{:S(2)}, u32[]{:S(2)}) %all-to-all-start.1) | async-done | bytes 491552 | tf_op jit(solution)/shard_map/all_to_all | solution.py:564
  61.8 3.3 %shard_map.149 = f32[960,128]{1,0:T(8,128)} custom-call(f32[960,128]{1,0:T(8,128)S(1)} %bitcast.22, bf16[6,192,256]{2,1,0:T(8,128)(2,1)S(1)} %get-tuple-element.30.high_ref, bf16[6,192,256]{2,1,0:T(8,128)(2,1)S(1)} %get-tuple-element.31.low_ref, f32[584,640]{1,0:T(8,128)S(1)} %get-tuple-element.32.taps_ref, f32[8,256]{1,0:T(8,128)S(1)} %copy-done.10), custom_call_target="tpu_custom_call" | custom-call | tf_op jit(solution)/shard_map/pallas_call | solution.py:531
  65.1 5.1 %all-to-all-start.2 = ((f32[32,1,3840]{2,1,0:T(1,128)}), f32[32,1,3840]{2,1,0:T(1,128)S(1)}, u32[]{:S(2)}, u32[]{:S(2)}) async-start(f32[32,1,3840]{2,1,0:T(1,128)} %bitcast.11), calls=%async_computation.2 | async-start | bytes 983040 | tf_op jit(solution)/shard_map/all_to_all | solution.py:564
  70.2 2.0 %collective-permute-start = (f32[96,128]{1,0:T(8,128)S(1)}, f32[96,128]{1,0:T(8,128)S(1)}, u32[]{:S(2)}, u32[]{:S(2)}) collective-permute-start(f32[96,128]{1,0:T(8,128)S(1)} %copy-done.15), channel_id=1, source_target_pairs={{0,16},{16,32},{32,48},{48,64},{64,80},{80,96},{96,112},{112,128},... | collective-permute-start | bytes 147464 | tf_op jit(solution)/shard_map/ppermute | solution.py:616
  72.3 5.0 %collective-permute-start.1 = (f32[96,128]{1,0:T(8,128)S(1)}, f32[96,128]{1,0:T(8,128)S(1)}, u32[]{:S(2)}, u32[]{:S(2)}) collective-permute-start(f32[96,128]{1,0:T(8,128)S(1)} %copy-done.13), channel_id=1, source_target_pairs={{16,0},{32,16},{48,32},{64,48},{80,64},{96,80},{112,96},{128,112},... | collective-permute-start | bytes 147464 | tf_op jit(solution)/shard_map/ppermute | solution.py:617
  77.3 1.7 %collective-permute-done.1.above_ref = f32[96,128]{1,0:T(8,128)S(1)} collective-permute-done((f32[96,128]{1,0:T(8,128)S(1)}, f32[96,128]{1,0:T(8,128)S(1)}, u32[]{:S(2)}, u32[]{:S(2)}) %collective-permute-start.1) | collective-permute-done | bytes 49184 | tf_op jit(solution)/shard_map/ppermute | solution.py:617
  79.1 1.1 %shard_map.150.local_ref = f32[64,384]{1,0:T(8,128)S(1)} custom-call(f32[64,384]{1,0:T(8,128)S(1)} %get-tuple-element.25.local_ref.own_ref, f32[96,128]{1,0:T(8,128)S(1)} %collective-permute-done.below_ref, f32[96,128]{1,0:T(8,128)S(1)} %collective-permute-done.1.above_ref, f32[584,640]{1,0:T(8,128)S(1)} %get-tuple-element.32.taps_ref), custom_call_target="tpu_custom_call" | custom-call | flops 10000000 | bytes 1000000 | tf_op jit(solution)/shard_map/pallas_call | solution.py:618
  80.2 7.2 %all-to-all-done.2 = f32[32,1,3840]{2,1,0:T(1,128)S(1)} async-done(((f32[32,1,3840]{2,1,0:T(1,128)}), f32[32,1,3840]{2,1,0:T(1,128)S(1)}, u32[]{:S(2)}, u32[]{:S(2)}) %all-to-all-start.2) | async-done | bytes 491552 | tf_op jit(solution)/shard_map/all_to_all | solution.py:564
  87.5 1.0 shard_map.151
  88.5 21.3 %all_to_all.21 = f32[16,1,8960]{2,1,0:T(1,128)S(1)} all-to-all(f32[16,1,8960]{2,1,0:T(1,128)S(1)} %bitcast.19), channel_id=1, replica_groups=mesh['lat'=32,'lon'=16] {'lon'}, dimensions={0} | all-to-all | bytes 1146880 | tf_op jit(solution)/shard_map/all_to_all | solution.py:564
  109.8 2.7 %shard_map.152 = f32[28,8,640]{2,1,0:T(8,128)} custom-call(f32[1120,128]{1,0:T(8,128)S(1)} %bitcast.18, f32[640]{0:T(1024)S(1)} %copy-done.11, bf16[640,1280]{1,0:T(8,128)(2,1)S(1)} %copy-done, bf16[1280,640]{1,0:T(8,128)(2,1)S(1)} %copy-done.1), custom_call_target="tpu_custom_call" | custom-call | tf_op jit(solution)/shard_map/pallas_call | solution.py:531
  (29 shorter events, 0.1 us)
Async XLA Ops:
  0.0 29.7 %copy-start.4 = (bf16[448,512]{1,0:T(8,128)(2,1)S(1)}, bf16[448,512]{1,0:T(8,128)(2,1)}, u32[]{:S(2)}) copy-start(bf16[448,512]{1,0:T(8,128)(2,1)} %constant.49.clone.high_ref) | copy-start | bytes 1376260
  0.0 29.7 %copy-start.5 = (bf16[448,512]{1,0:T(8,128)(2,1)S(1)}, bf16[448,512]{1,0:T(8,128)(2,1)}, u32[]{:S(2)}) copy-start(bf16[448,512]{1,0:T(8,128)(2,1)} %constant.50.clone.low_ref) | copy-start | bytes 1376260
  2.6 42.9 %copy-start.10 = (f32[8,256]{1,0:T(8,128)S(1)}, f32[8,256]{1,0:T(8,128)}, u32[]{:S(2)}) copy-start(f32[8,256]{1,0:T(8,128)} %constant.48.clone.angle_ref) | copy-start | bytes 24580
  2.6 44.6 %copy-start.6 = (f32[25,640]{1,0:T(8,128)S(1)}, f32[25,640]{1,0:T(8,128)}, u32[]{:S(2)}) copy-start(f32[25,640]{1,0:T(8,128)} %first_ref) | copy-start | bytes 192004
  2.6 44.6 %copy-start.7 = (f32[25,640]{1,0:T(8,128)S(1)}, f32[25,640]{1,0:T(8,128)}, u32[]{:S(2)}) copy-start(f32[25,640]{1,0:T(8,128)} %second_ref) | copy-start | bytes 192004
  2.6 44.6 %copy-start.8 = (f32[32,512]{1,0:T(8,128)S(1)}, f32[32,512]{1,0:T(8,128)}, u32[]{:S(2)}) copy-start(f32[32,512]{1,0:T(8,128)} %constant.53.clone.wave_ref) | copy-start | bytes 196612
  2.7 44.5 %copy-start.9 = (f32[192,40]{0,1:T(8,128)S(1)}, f32[192,40]{0,1:T(8,128)}, u32[]{:S(2)}) copy-start(f32[192,40]{0,1:T(8,128)} %param.18) | copy-start | bytes 92164
  31.4 30.4 %all-to-all-start.1 = ((f32[32,1,3840]{2,1,0:T(1,128)}), f32[32,1,3840]{2,1,0:T(1,128)S(1)}, u32[]{:S(2)}, u32[]{:S(2)}) async-start(f32[32,1,3840]{2,1,0:T(1,128)} %bitcast.3), calls=%async_computation.1 | async-start | bytes 983040 | tf_op jit(solution)/shard_map/all_to_all | solution.py:564
  49.5 0.6 copy-start.12
  50.1 0.6 copy-start.14
  61.8 8.5 %copy-start.15 = (f32[96,128]{1,0:T(8,128)S(1)}, f32[96,128]{1,0:T(8,128)}, u32[]{:S(2)}) copy-start(f32[96,128]{1,0:T(8,128)} %copy-done.14) | copy-start | bytes 147460
  61.8 10.5 %copy-start.13 = (f32[96,128]{1,0:T(8,128)S(1)}, f32[96,128]{1,0:T(8,128)}, u32[]{:S(2)}) copy-start(f32[96,128]{1,0:T(8,128)} %copy-done.12) | copy-start | bytes 147460
  65.1 22.4 %copy-start.2 = (bf16[2,512,256]{2,1,0:T(8,128)(2,1)S(1)}, bf16[2,512,256]{2,1,0:T(8,128)(2,1)}, u32[]{:S(2)}) copy-start(bf16[2,512,256]{2,1,0:T(8,128)(2,1)} %constant.54.clone.high_ref) | copy-start | bytes 1572868
  65.1 22.4 %copy-start.3 = (bf16[2,512,256]{2,1,0:T(8,128)(2,1)S(1)}, bf16[2,512,256]{2,1,0:T(8,128)(2,1)}, u32[]{:S(2)}) copy-start(bf16[2,512,256]{2,1,0:T(8,128)(2,1)} %constant.55.clone.low_ref) | copy-start | bytes 1572868
  65.1 22.3 %all-to-all-start.2 = ((f32[32,1,3840]{2,1,0:T(1,128)}), f32[32,1,3840]{2,1,0:T(1,128)S(1)}, u32[]{:S(2)}, u32[]{:S(2)}) async-start(f32[32,1,3840]{2,1,0:T(1,128)} %bitcast.11), calls=%async_computation.2 | async-start | bytes 983040 | tf_op jit(solution)/shard_map/all_to_all | solution.py:564
  70.2 7.1 %collective-permute-start = (f32[96,128]{1,0:T(8,128)S(1)}, f32[96,128]{1,0:T(8,128)S(1)}, u32[]{:S(2)}, u32[]{:S(2)}) collective-permute-start(f32[96,128]{1,0:T(8,128)S(1)} %copy-done.15), channel_id=1, source_target_pairs={{0,16},{16,32},{32,48},{48,64},{64,80},{80,96},{96,112},{112,128},... | collective-permute-start | bytes 147464 | tf_op jit(solution)/shard_map/ppermute | solution.py:616
  72.3 6.8 %collective-permute-start.1 = (f32[96,128]{1,0:T(8,128)S(1)}, f32[96,128]{1,0:T(8,128)S(1)}, u32[]{:S(2)}, u32[]{:S(2)}) collective-permute-start(f32[96,128]{1,0:T(8,128)S(1)} %copy-done.13), channel_id=1, source_target_pairs={{16,0},{32,16},{48,32},{64,48},{80,64},{96,80},{112,96},{128,112},... | collective-permute-start | bytes 147464 | tf_op jit(solution)/shard_map/ppermute | solution.py:617
  87.5 22.3 %copy-start = (bf16[640,1280]{1,0:T(8,128)(2,1)S(1)}, bf16[640,1280]{1,0:T(8,128)(2,1)}, u32[]{:S(2)}) copy-start(bf16[640,1280]{1,0:T(8,128)(2,1)} %up_ref.1) | copy-start | bytes 4915204
  87.5 22.3 %copy-start.1 = (bf16[1280,640]{1,0:T(8,128)(2,1)S(1)}, bf16[1280,640]{1,0:T(8,128)(2,1)}, u32[]{:S(2)}) copy-start(bf16[1280,640]{1,0:T(8,128)(2,1)} %down_ref.1) | copy-start | bytes 4915204
  87.5 22.3 %copy-start.11 = (f32[640]{0:T(1024)S(1)}, f32[640]{0:T(1024)}, u32[]{:S(2)}) copy-start(f32[640]{0:T(1024)} %gain_ref.1) | copy-start | bytes 7684
